TPU v7x, 32 devices: a whole 2x2x4 slice. The times are simulated.
32 devices in a mesh: groups: 2 (over x), ctx: 16 (over z, y, core).
Axes of the slice: x: 2, y: 2, z: 4, core: 2. Of those that a mesh axis runs over, the one named last changes fastest.
Arguments:
- queries: bfloat16 [8192, 2560], P(('groups', 'ctx')), parts along dimension 0, may hold values from -22 to 22
- answer_keys: bfloat16 [8192, 512], P(('groups', 'ctx')), parts along dimension 0, may hold values from -15 to 15
- answer_values: bfloat16 [8192, 512], P(('groups', 'ctx')), parts along dimension 0, may hold values from -6 to 6
- prompt_keys: bfloat16 [128, 512], P(('groups', 'ctx')), parts along dimension 0, may hold values from -15 to 15
- prompt_values: bfloat16 [128, 512], P(('groups', 'ctx')), parts along dimension 0, may hold values from -6 to 6
- positions: int32 [8192], P(('groups', 'ctx')), parts along dimension 0, may hold values from 64 to 1087, as said below
- ancestry: int32 [32, 16], P(('groups', 'ctx')), parts along dimension 0, may hold values from 0 to 1, as said below
- out_grad: bfloat16 [8192, 2560], P(('groups', 'ctx')), parts along dimension 0, may hold values from -6 to 6
Outputs:
- attended: bfloat16 [8192, 2560], P(('groups', 'ctx')), parts along dimension 0
- grad_queries: bfloat16 [8192, 2560], P(('groups', 'ctx')), parts along dimension 0
- grad_keys: bfloat16 [8192, 512], P(('groups', 'ctx')), parts along dimension 0
- grad_values: bfloat16 [8192, 512], P(('groups', 'ctx')), parts along dimension 0
- grad_prompt_keys: bfloat16 [128, 512], P(('groups', 'ctx')), parts along dimension 0
- grad_prompt_values: bfloat16 [128, 512], P(('groups', 'ctx')), parts along dimension 0
There are 2 independent parts, one for each index of `groups`. A program takes and returns all parts, laid end to end along the dimension named above; each array names one. Nothing has to cross between parts.
Inputs may be any that keep to these rules, and one draw needn't show every extreme that they name: Tree tokens are packed in blocks of 256, parents before children, one branch a block. ancestry[b, c] is 1 exactly when block c is block b or an ancestor of it. Every ancestor of a block lies among the 3 blocks before it; in every draw block 3 descends from block 0 through every block between. `positions`: A token's position is 64 plus the number of its ancestor tokens in the tree.
All inputs are finite; a program needn't handle non-finite values.
Results may differ from a plain program's by a relative error of at most 0.0085.
The roundings to bfloat16 on the way count: a program that leaves them out, or rounds other values in their place, can miss the bound.
Values may be sent and summed in bfloat16 or wider, within the bound.
No kernel may reach another device: no remote copies, remote signals or barrier semaphores. Data moves between devices by JAX's collectives and lax.ppermute only.
A program may use at most 64 MiB of HBM per device.

v0:
```python
import jax
import jax.numpy as jnp
from jax import lax
from jax.sharding import PartitionSpec as P

QH = 20
KVH = 4
HD = 128
SPAN = 4


rope_base = 1000000.0


def passed_along(value, axis, steps):
    count = lax.axis_size(axis)
    initial, last = (max(0, -steps), min(count, count - steps))
    return lax.ppermute(value, axis, [(source, source + steps) for source in range(initial, last)])


def rotate(values, places, sign):
    rows = values.shape[0]
    split = values.astype(jnp.float32).reshape(rows, -1, HD)
    half = HD // 2
    freqs = rope_base ** (-(2.0 * jnp.arange(half, dtype=jnp.float32)) / HD)
    angles = places.astype(jnp.float32)[:, None] * freqs[None, :]
    cosine = jnp.cos(angles)[:, None, :]
    sine = sign * jnp.sin(angles)[:, None, :]
    first = split[..., :half]
    second = split[..., half:]
    joined = jnp.concatenate(
        [first * cosine - second * sine, second * cosine + first * sine], axis=-1
    )
    return joined.reshape(rows, -1)


def head_scores(head_q, head_k, visible):
    scores = jnp.einsum("tgd,kd->gtk", head_q, head_k, preferred_element_type=jnp.float32) * HD ** (
        -0.5
    )
    return jnp.where(visible[None], scores, -jnp.inf)


def head_forward(head_q, head_k, head_v, visible):
    scores = head_scores(head_q, head_k, visible)
    peak = jnp.max(scores, axis=-1, keepdims=True)
    log_total = peak + jnp.log(jnp.sum(jnp.exp(scores - peak), axis=-1, keepdims=True))
    weights = jnp.exp(scores - log_total).astype(jnp.bfloat16)
    mixed = jnp.einsum("gtk,kd->tgd", weights, head_v, preferred_element_type=jnp.float32).astype(
        jnp.bfloat16
    )
    return (mixed, log_total[..., 0])


def head_backward(head_q, head_k, head_v, visible, head_g, mixed, log_total):
    scores = head_scores(head_q, head_k, visible)
    probs = jnp.exp(scores - log_total[..., None])
    weights = probs.astype(jnp.bfloat16)
    delta = jnp.sum(head_g.astype(jnp.float32) * mixed.astype(jnp.float32), axis=-1)
    dweights = jnp.einsum("tgd,kd->gtk", head_g, head_v, preferred_element_type=jnp.float32)
    dscores = (probs * (dweights - jnp.transpose(delta)[..., None]) * HD ** (-0.5)).astype(
        jnp.bfloat16
    )
    grad_v = jnp.einsum("gtk,tgd->kd", weights, head_g, preferred_element_type=jnp.float32)
    grad_q = jnp.einsum("gtk,kd->tgd", dscores, head_k, preferred_element_type=jnp.float32)
    grad_k = jnp.einsum("gtk,tgd->kd", dscores, head_q, preferred_element_type=jnp.float32)
    return (grad_q, grad_k, grad_v)


def split_query(values):
    rows = values.shape[0]
    return values.reshape(rows, KVH, QH // KVH, HD).transpose(1, 0, 2, 3)


def split_key(values):
    rows = values.shape[0]
    return values.reshape(rows, KVH, HD).transpose(1, 0, 2)


def fetch_window(k_rot, values):

    def advance(turn, state):
        moving, store_k, store_v = state
        moving = passed_along((moving[0], moving[1]), "ctx", 1)
        store_k = lax.dynamic_update_index_in_dim(store_k, moving[0], turn, 0)
        store_v = lax.dynamic_update_index_in_dim(store_v, moving[1], turn, 0)
        return (moving, store_k, store_v)

    empty = jnp.zeros((SPAN,) + k_rot.shape, jnp.bfloat16)
    start = ((k_rot, values), empty.at[0].set(k_rot), empty.at[0].set(values))
    moved, store_k, store_v = lax.fori_loop(1, SPAN, advance, start)
    return (store_k, store_v)


def return_window(terms_k, terms_v):

    def carry_back(turn, state):
        slot = SPAN - turn
        summed = (
            state[0] + lax.dynamic_index_in_dim(terms_k, slot, 0, False),
            state[1] + lax.dynamic_index_in_dim(terms_v, slot, 0, False),
        )
        return passed_along((summed[0], summed[1]), "ctx", -1)

    zeros = jnp.zeros(terms_k.shape[1:], jnp.float32)
    total_k, total_v = lax.fori_loop(1, SPAN, carry_back, (zeros, zeros))
    return (total_k + terms_k[0], total_v + terms_v[0])


def local(
    queries, answer_keys, answer_values, prompt_keys, prompt_values, positions, ancestry, out_grad
):
    rows = queries.shape[0]
    width = answer_keys.shape[1]
    my_block = lax.axis_index("ctx")
    q_rot = rotate(queries, positions, 1.0).astype(jnp.bfloat16)
    k_rot = rotate(answer_keys, positions, 1.0).astype(jnp.bfloat16)
    prompt_rows = prompt_keys.shape[0]
    prompt_places = my_block * prompt_rows + jnp.arange(prompt_rows, dtype=jnp.int32)
    pk_rot = rotate(prompt_keys, prompt_places, 1.0).astype(jnp.bfloat16)
    prompt_k_all, prompt_v_all = (
        lax.all_gather(pk_rot, "ctx", axis=0, tiled=True),
        lax.all_gather(prompt_values, "ctx", axis=0, tiled=True),
    )
    prompt_count = prompt_k_all.shape[0]
    window_k, window_v = fetch_window(k_rot, answer_values)
    slot_ids = jnp.arange(SPAN, dtype=jnp.int32)
    blocks_in = my_block - slot_ids
    table = ancestry[0]
    match = jnp.arange(table.shape[0], dtype=jnp.int32)[None, :] == blocks_in[:, None]
    seen = jnp.sum(jnp.where(match, table[None, :], 0), axis=1) > 0
    lower = jnp.arange(rows, dtype=jnp.int32)[None, :] <= jnp.arange(rows, dtype=jnp.int32)[:, None]
    window_seen = seen[None, :, None] & ((slot_ids[None, :, None] > 0) | lower[:, None, :])
    visible = jnp.concatenate(
        [jnp.ones((rows, prompt_count), bool), window_seen.reshape(rows, SPAN * rows)], axis=1
    )
    keys = jnp.concatenate([prompt_k_all, window_k.reshape(SPAN * rows, width)], axis=0)
    vals = jnp.concatenate([prompt_v_all, window_v.reshape(SPAN * rows, width)], axis=0)
    count = keys.shape[0]
    heads_q = split_query(q_rot)
    heads_k = split_key(keys)
    heads_v = split_key(vals)
    heads_g = split_query(out_grad)
    mixed, log_total = lax.map(
        lambda group: head_forward(group[0], group[1], group[2], visible),
        (heads_q, heads_k, heads_v),
    )
    attended = mixed.transpose(1, 0, 2, 3).reshape(rows, QH * HD)
    grad_q, grad_k, grad_v = lax.map(
        lambda group: head_backward(
            group[0], group[1], group[2], visible, group[3], group[4], group[5]
        ),
        (heads_q, heads_k, heads_v, heads_g, mixed, log_total),
    )
    grad_q = grad_q.transpose(1, 0, 2, 3).reshape(rows, QH * HD)
    grad_k = grad_k.transpose(1, 0, 2).reshape(count, width)
    grad_v = grad_v.transpose(1, 0, 2).reshape(count, width)
    prompt_sum_k, prompt_sum_v = (
        lax.psum_scatter(grad_k[:prompt_count], "ctx", scatter_dimension=0, tiled=True),
        lax.psum_scatter(grad_v[:prompt_count], "ctx", scatter_dimension=0, tiled=True),
    )
    own_k, own_v = return_window(
        grad_k[prompt_count:].reshape(SPAN, rows, width),
        grad_v[prompt_count:].reshape(SPAN, rows, width),
    )
    grad_queries = rotate(grad_q, positions, -1.0).astype(jnp.bfloat16)
    grad_keys = rotate(own_k, positions, -1.0).astype(jnp.bfloat16)
    grad_values = own_v.astype(jnp.bfloat16)
    grad_prompt_keys = rotate(prompt_sum_k, prompt_places, -1.0).astype(jnp.bfloat16)
    grad_prompt_values = prompt_sum_v.astype(jnp.bfloat16)
    return (attended, grad_queries, grad_keys, grad_values, grad_prompt_keys, grad_prompt_values)


def solution(mesh):
    return jax.shard_map(
        local,
        mesh=mesh,
        in_specs=(
            P(("groups", "ctx"), None),
            P(("groups", "ctx"), None),
            P(("groups", "ctx"), None),
            P(("groups", "ctx"), None),
            P(("groups", "ctx"), None),
            P(("groups", "ctx")),
            P(("groups", "ctx"), None),
            P(("groups", "ctx"), None),
        ),
        out_specs=(
            P(("groups", "ctx"), None),
            P(("groups", "ctx"), None),
            P(("groups", "ctx"), None),
            P(("groups", "ctx"), None),
            P(("groups", "ctx"), None),
            P(("groups", "ctx"), None),
        ),
        check_vma=False,
    )
```

profile of v0, /device:TPU:1, one launch (start us, length us, event | category | flops | bytes accessed | tf_op | source)
XLA Modules:
  0.0 326.0 jit_solution(10764893775638197956)
XLA Ops:
  12.3 23.1 %all-gather.1 = bf16[16,4,512]{2,1,0:T(4,128)(2,1)S(1)} all-gather(bf16[1,4,512]{2,1,0:T(4,128)(2,1)S(1)} %reshape.386), channel_id=1, replica_groups=mesh['groups'=2,'ctx'=16] {'ctx'}, dimensions={0}, use_global_device_ids=true | all-gather | bytes 69632 | tf_op jit(solution)/shard_map/all_gather | solution.py:122
  36.1 17.9 %all-gather = bf16[16,4,512]{2,1,0:T(4,128)(2,1)S(1)} all-gather(bf16[1,4,512]{2,1,0:T(4,128)(2,1)} %bitcast.229), channel_id=1, replica_groups=mesh['groups'=2,'ctx'=16] {'ctx'}, dimensions={0}, use_global_device_ids=true | all-gather | bytes 69632 | tf_op jit(solution)/shard_map/all_gather | solution.py:123
  59.0 31.5 %while.64 = (s32[]{:T(128)}, bf16[256,512]{1,0:T(8,128)(2,1)S(1)}, bf16[256,512]{1,0:T(8,128)(2,1)}, bf16[4,256,512]{2,1,0:T(8,128)(2,1)S(1)}, bf16[4,256,512]{2...) while((s32[]{:T(128)}, bf16[256,512]{1,0:T(8,128)(2,1)S(1)}, bf16[256,512]{1,0:T(8,128)(2,1)}, ...), condition=%wide.region_1.0_spmd, body=%wide.region_0.0_spmd.sunk | while | flops 5 | bytes 4194511 | solution.py:91
  59.2 3.3 %collective-permute-start.1 = (bf16[256,512]{1,0:T(8,128)(2,1)}, bf16[256,512]{1,0:T(8,128)(2,1)S(1)}, u32[]{:S(2)}, u32[]{:S(2)}) collective-permute-start(bf16[256,512]{1,0:T(8,128)(2,1)} %get-tuple-element.721), channel_id=1, source_target_pairs={{0,1},{1,2},{2,3},{3,4},{4,5},{5,6},{6,7},{7,8},{8,9},{9,10},{10,1... | collective-permute-start | bytes 786440 | tf_op jit(solution)/shard_map/while/body/eval_jaxpr/ppermute | solution.py:18
  68.9 4.4 %collective-permute-start.1 = (bf16[256,512]{1,0:T(8,128)(2,1)}, bf16[256,512]{1,0:T(8,128)(2,1)S(1)}, u32[]{:S(2)}, u32[]{:S(2)}) collective-permute-start(bf16[256,512]{1,0:T(8,128)(2,1)} %get-tuple-element.721), channel_id=1, source_target_pairs={{0,1},{1,2},{2,3},{3,4},{4,5},{5,6},{6,7},{7,8},{8,9},{9,10},{10,1... | collective-permute-start | bytes 786440 | tf_op jit(solution)/shard_map/while/body/eval_jaxpr/ppermute | solution.py:18
  79.7 4.4 %collective-permute-start.1 = (bf16[256,512]{1,0:T(8,128)(2,1)}, bf16[256,512]{1,0:T(8,128)(2,1)S(1)}, u32[]{:S(2)}, u32[]{:S(2)}) collective-permute-start(bf16[256,512]{1,0:T(8,128)(2,1)} %get-tuple-element.721), channel_id=1, source_target_pairs={{0,1},{1,2},{2,3},{3,4},{4,5},{5,6},{6,7},{7,8},{8,9},{9,10},{10,1... | collective-permute-start | bytes 786440 | tf_op jit(solution)/shard_map/while/body/eval_jaxpr/ppermute | solution.py:18
  102.7 22.1 %while.65 = (s32[]{:T(128)}, bf16[4,256,5,128]{1,3,2,0:T(8,128)(2,1)}, f32[4,5,256]{2,1,0:T(8,128)S(1)}, bf16[4,1088,128]{2,1,0:T(8,128)(2,1)}, pred[256,1088]{0...) while((s32[]{:T(128)}, ...), condition=%wide.region_6.7_spmd, body=%wide.region_3.6_spmd.sunk | while | flops 722942720 | bytes 18258016 | solution.py:144
  105.4 2.8 fusion.71
  110.9 2.8 fusion.71
  116.5 2.8 fusion.71
  122.0 2.8 fusion.71
  124.8 52.3 %while.66 = (s32[]{:T(128)}, f32[4,256,5,128]{1,3,2,0:T(8,128)}, f32[4,1088,128]{2,1,0:T(8,128)}, f32[4,1088,128]{2,1,0:T(8,128)}, bf16[4,1088,128]{2,1,0:T(8,12...) while((s32[]{:T(128)}, f32[4,256,5,128]{1,3,2,0:T(8,128)}, ...), condition=%wide.region_9.10_spmd, body=%wide.region_7.9_spmd.sunk | while | flops 1794374400 | bytes 43058364 | solution.py:149
  153.7 2.5 fusion.82
  191.1 54.5 %all-reduce.9 = bf16[64,512]{1,0:T(8,128)(2,1)S(1)} all-reduce(f32[64,512]{1,0:T(8,128)} %copy_bitcast_fusion.2), channel_id=3, replica_groups=mesh['groups'=2,'ctx'=16] {'ctx'}, use_global_device_ids=true, to_apply=%region_13.14.clone | all-reduce | flops 32768 | bytes 196608
  245.5 2.7 copy.76
  250.3 4.3 %copy.75 = f32[1024,4,128]{2,1,0:T(4,128)} copy(f32[1024,4,128]{2,0,1:T(8,128)} %slice.132) | data formatting | bytes 4194304 | tf_op jit(solution)/shard_map/slice | solution.py:163
  254.7 3.1 reshape.373
  257.9 53.2 %while.67 = (s32[]{:T(128)}, f32[256,512]{1,0:T(8,128)S(1)}, f32[256,512]{1,0:T(8,128)S(1)}, f32[4,256,512]{2,1,0:T(8,128)}, f32[4,256,512]{2,1,0:T(8,128)S(1)},...) while((s32[]{:T(128)}, f32[256,512]{1,0:T(8,128)S(1)}, f32[256,512]{1,0:T(8,128)S(1)}, ...), condition=%wide.region_11.12_spmd, body=%wide.region_10.11_spmd.sunk | while | flops 262150 | bytes 7340259 | solution.py:106
  259.0 6.9 %collective-permute-start.2 = (f32[256,512]{1,0:T(8,128)S(1)}, f32[256,512]{1,0:T(8,128)S(1)}, u32[]{:S(2)}, u32[]{:S(2)}) collective-permute-start(f32[256,512]{1,0:T(8,128)S(1)} %bitcast_add_fusion.6), channel_id=1, source_target_pairs={{1,0},{2,1},{3,2},{4,3},{5,4},{6,5},{7,6},{8,7},{9,8},{10,9},{11,1... | collective-permute-start | bytes 1572872 | tf_op jit(solution)/shard_map/while/body/eval_jaxpr/ppermute | solution.py:18
  269.5 7.0 %collective-permute-done.3 = f32[256,512]{1,0:T(8,128)S(1)} collective-permute-done((f32[256,512]{1,0:T(8,128)S(1)}, f32[256,512]{1,0:T(8,128)S(1)}, u32[]{:S(2)}, u32[]{:S(2)}) %collective-permute-start.3) | collective-permute-done | bytes 524320 | tf_op jit(solution)/shard_map/while/body/eval_jaxpr/ppermute | solution.py:18
  281.7 6.5 %collective-permute-done.2 = f32[256,512]{1,0:T(8,128)S(1)} collective-permute-done((f32[256,512]{1,0:T(8,128)S(1)}, f32[256,512]{1,0:T(8,128)S(1)}, u32[]{:S(2)}, u32[]{:S(2)}) %collective-permute-start.2) | collective-permute-done | bytes 524320 | tf_op jit(solution)/shard_map/while/body/eval_jaxpr/ppermute | solution.py:18
  288.2 5.6 %collective-permute-done.3 = f32[256,512]{1,0:T(8,128)S(1)} collective-permute-done((f32[256,512]{1,0:T(8,128)S(1)}, f32[256,512]{1,0:T(8,128)S(1)}, u32[]{:S(2)}, u32[]{:S(2)}) %collective-permute-start.3) | collective-permute-done | bytes 524320 | tf_op jit(solution)/shard_map/while/body/eval_jaxpr/ppermute | solution.py:18
  298.9 6.5 %collective-permute-done.2 = f32[256,512]{1,0:T(8,128)S(1)} collective-permute-done((f32[256,512]{1,0:T(8,128)S(1)}, f32[256,512]{1,0:T(8,128)S(1)}, u32[]{:S(2)}, u32[]{:S(2)}) %collective-permute-start.2) | collective-permute-done | bytes 524320 | tf_op jit(solution)/shard_map/while/body/eval_jaxpr/ppermute | solution.py:18
  305.4 5.6 %collective-permute-done.3 = f32[256,512]{1,0:T(8,128)S(1)} collective-permute-done((f32[256,512]{1,0:T(8,128)S(1)}, f32[256,512]{1,0:T(8,128)S(1)}, u32[]{:S(2)}, u32[]{:S(2)}) %collective-permute-start.3) | collective-permute-done | bytes 524320 | tf_op jit(solution)/shard_map/while/body/eval_jaxpr/ppermute | solution.py:18
  (197 shorter events, 140.5 us)
Async XLA Ops:
  7.2 310.5 %all-reduce.8.cloned.1.call-start = ((), (), s32[]{:S(2)}) async-start(), calls=%async_computation | async-start | bytes 262144
  55.5 43.7 %copy-start.5 = (f32[256,64]{0,1:T(8,128)}, f32[256,64]{0,1:T(8,128)S(1)}, u32[]{:S(2)}) copy-start(f32[256,64]{0,1:T(8,128)S(1)} %get-tuple-element.523) | copy-start | bytes 196612
  59.2 6.9 %collective-permute-start.1 = (bf16[256,512]{1,0:T(8,128)(2,1)}, bf16[256,512]{1,0:T(8,128)(2,1)S(1)}, u32[]{:S(2)}, u32[]{:S(2)}) collective-permute-start(bf16[256,512]{1,0:T(8,128)(2,1)} %get-tuple-element.721), channel_id=1, source_target_pairs={{0,1},{1,2},{2,3},{3,4},{4,5},{5,6},{6,7},{7,8},{8,9},{9,10},{10,1... | collective-permute-start | bytes 786440 | tf_op jit(solution)/shard_map/while/body/eval_jaxpr/ppermute | solution.py:18
  62.5 6.3 %collective-permute-start = (bf16[256,512]{1,0:T(8,128)(2,1)S(1)}, bf16[256,512]{1,0:T(8,128)(2,1)S(1)}, u32[]{:S(2)}, u32[]{:S(2)}) collective-permute-start(bf16[256,512]{1,0:T(8,128)(2,1)S(1)} %get-tuple-element.720), channel_id=1, source_target_pairs={{0,1},{1,2},{2,3},{3,4},{4,5},{5,6},{6,7},{7,8},{8,9},{9,10},{10,1... | collective-permute-start | bytes 786440 | tf_op jit(solution)/shard_map/while/body/eval_jaxpr/ppermute | solution.py:18
  68.9 8.0 %collective-permute-start.1 = (bf16[256,512]{1,0:T(8,128)(2,1)}, bf16[256,512]{1,0:T(8,128)(2,1)S(1)}, u32[]{:S(2)}, u32[]{:S(2)}) collective-permute-start(bf16[256,512]{1,0:T(8,128)(2,1)} %get-tuple-element.721), channel_id=1, source_target_pairs={{0,1},{1,2},{2,3},{3,4},{4,5},{5,6},{6,7},{7,8},{8,9},{9,10},{10,1... | collective-permute-start | bytes 786440 | tf_op jit(solution)/shard_map/while/body/eval_jaxpr/ppermute | solution.py:18
  73.3 6.3 %collective-permute-start = (bf16[256,512]{1,0:T(8,128)(2,1)S(1)}, bf16[256,512]{1,0:T(8,128)(2,1)S(1)}, u32[]{:S(2)}, u32[]{:S(2)}) collective-permute-start(bf16[256,512]{1,0:T(8,128)(2,1)S(1)} %get-tuple-element.720), channel_id=1, source_target_pairs={{0,1},{1,2},{2,3},{3,4},{4,5},{5,6},{6,7},{7,8},{8,9},{9,10},{10,1... | collective-permute-start | bytes 786440 | tf_op jit(solution)/shard_map/while/body/eval_jaxpr/ppermute | solution.py:18
  79.7 8.0 %collective-permute-start.1 = (bf16[256,512]{1,0:T(8,128)(2,1)}, bf16[256,512]{1,0:T(8,128)(2,1)S(1)}, u32[]{:S(2)}, u32[]{:S(2)}) collective-permute-start(bf16[256,512]{1,0:T(8,128)(2,1)} %get-tuple-element.721), channel_id=1, source_target_pairs={{0,1},{1,2},{2,3},{3,4},{4,5},{5,6},{6,7},{7,8},{8,9},{9,10},{10,1... | collective-permute-start | bytes 786440 | tf_op jit(solution)/shard_map/while/body/eval_jaxpr/ppermute | solution.py:18
  84.1 6.3 %collective-permute-start = (bf16[256,512]{1,0:T(8,128)(2,1)S(1)}, bf16[256,512]{1,0:T(8,128)(2,1)S(1)}, u32[]{:S(2)}, u32[]{:S(2)}) collective-permute-start(bf16[256,512]{1,0:T(8,128)(2,1)S(1)} %get-tuple-element.720), channel_id=1, source_target_pairs={{0,1},{1,2},{2,3},{3,4},{4,5},{5,6},{6,7},{7,8},{8,9},{9,10},{10,1... | collective-permute-start | bytes 786440 | tf_op jit(solution)/shard_map/while/body/eval_jaxpr/ppermute | solution.py:18
  99.8 2.4 copy-start.7
  100.6 2.1 copy-start.10
  131.7 2.0 copy-start.1
  144.8 2.0 copy-start.1
  157.9 2.0 copy-start.1
  171.0 2.0 copy-start.1
  180.3 2.3 copy-start.3
  182.6 3.1 copy-start.2
  259.0 10.5 %collective-permute-start.2 = (f32[256,512]{1,0:T(8,128)S(1)}, f32[256,512]{1,0:T(8,128)S(1)}, u32[]{:S(2)}, u32[]{:S(2)}) collective-permute-start(f32[256,512]{1,0:T(8,128)S(1)} %bitcast_add_fusion.6), channel_id=1, source_target_pairs={{1,0},{2,1},{3,2},{4,3},{5,4},{6,5},{7,6},{8,7},{9,8},{10,9},{11,1... | collective-permute-start | bytes 1572872 | tf_op jit(solution)/shard_map/while/body/eval_jaxpr/ppermute | solution.py:18
  266.1 10.5 %collective-permute-start.3 = (f32[256,512]{1,0:T(8,128)S(1)}, f32[256,512]{1,0:T(8,128)S(1)}, u32[]{:S(2)}, u32[]{:S(2)}) collective-permute-start(f32[256,512]{1,0:T(8,128)S(1)} %bitcast_add_fusion.7), channel_id=1, source_target_pairs={{1,0},{2,1},{3,2},{4,3},{5,4},{6,5},{7,6},{8,7},{9,8},{10,9},{11,1... | collective-permute-start | bytes 1572872 | tf_op jit(solution)/shard_map/while/body/eval_jaxpr/ppermute | solution.py:18
  277.7 10.5 %collective-permute-start.2 = (f32[256,512]{1,0:T(8,128)S(1)}, f32[256,512]{1,0:T(8,128)S(1)}, u32[]{:S(2)}, u32[]{:S(2)}) collective-permute-start(f32[256,512]{1,0:T(8,128)S(1)} %bitcast_add_fusion.6), channel_id=1, source_target_pairs={{1,0},{2,1},{3,2},{4,3},{5,4},{6,5},{7,6},{8,7},{9,8},{10,9},{11,1... | collective-permute-start | bytes 1572872 | tf_op jit(solution)/shard_map/while/body/eval_jaxpr/ppermute | solution.py:18
  279.7 14.1 %collective-permute-start.3 = (f32[256,512]{1,0:T(8,128)S(1)}, f32[256,512]{1,0:T(8,128)S(1)}, u32[]{:S(2)}, u32[]{:S(2)}) collective-permute-start(f32[256,512]{1,0:T(8,128)S(1)} %bitcast_add_fusion.7), channel_id=1, source_target_pairs={{1,0},{2,1},{3,2},{4,3},{5,4},{6,5},{7,6},{8,7},{9,8},{10,9},{11,1... | collective-permute-start | bytes 1572872 | tf_op jit(solution)/shard_map/while/body/eval_jaxpr/ppermute | solution.py:18
  294.9 10.5 %collective-permute-start.2 = (f32[256,512]{1,0:T(8,128)S(1)}, f32[256,512]{1,0:T(8,128)S(1)}, u32[]{:S(2)}, u32[]{:S(2)}) collective-permute-start(f32[256,512]{1,0:T(8,128)S(1)} %bitcast_add_fusion.6), channel_id=1, source_target_pairs={{1,0},{2,1},{3,2},{4,3},{5,4},{6,5},{7,6},{8,7},{9,8},{10,9},{11,1... | collective-permute-start | bytes 1572872 | tf_op jit(solution)/shard_map/while/body/eval_jaxpr/ppermute | solution.py:18
  297.0 14.1 %collective-permute-start.3 = (f32[256,512]{1,0:T(8,128)S(1)}, f32[256,512]{1,0:T(8,128)S(1)}, u32[]{:S(2)}, u32[]{:S(2)}) collective-permute-start(f32[256,512]{1,0:T(8,128)S(1)} %bitcast_add_fusion.7), channel_id=1, source_target_pairs={{1,0},{2,1},{3,2},{4,3},{5,4},{6,5},{7,6},{8,7},{9,8},{10,9},{11,1... | collective-permute-start | bytes 1572872 | tf_op jit(solution)/shard_map/while/body/eval_jaxpr/ppermute | solution.py:18
  311.1 3.1 copy-start.6
  314.0 1.8 copy-start.11
  (7 other events, 8.5 us)
Sparse Core Ops, SparseCore 0:
  178.8 87.9 all-reduce.7
where the time goes:
time: 328 us; the launch traced here: 326 us
  blocking collectives  95.5 us (29%)
  matrix products  60.2 us (18%)
  local copies, waits for them, and re-layouts  53.6 us (16%)
  waiting for transfers between devices  43.6 us (13%)
  starting transfers between devices  34.7 us (11%)
  other arithmetic  22.6 us (7%)
  between operations  15 us (5%)
    unnamed x1, blocking collectives  54.5 us
    ppermute x12, waiting for transfers between devices, passed_along(): lax.ppermute(value, axis, [(source, source + steps) for source in range(i...  43.6 us
    ppermute x12, starting transfers between devices, passed_along(): lax.ppermute(value, axis, [(source, source + steps) for source in range(i...  34.7 us
    all_gather x1, blocking collectives, local(): lax.all_gather(pk_rot, 'ctx', axis=0, tiled=True)  23.1 us
    all_gather x1, blocking collectives, local(): lax.all_gather(prompt_values, 'ctx', axis=0, tiled=True)  17.9 us
    dot_general x8, matrix products, head_scores(): jnp.einsum('tgd,kd->gtk', head_q, head_k, preferred_element_type=jnp.floa...  17.7 us
    dot_general x4, matrix products, head_forward(): jnp.einsum('gtk,kd->tgd', weights, head_v, preferred_element_type=jnp.flo...  11.2 us
    unnamed x31, local copies, waits for them, and re-layouts  10.6 us
  transfers between devices with their start and end apart: 13, of which 12 were waited for; matrix products, arithmetic and copies ran while one was open for 11% of the time, Pallas kernels for 0%

commit v1 on v0

v1 whole, which is shorter than its diff:
```python
import functools

import jax
import jax.numpy as jnp
from jax import lax
from jax.experimental import pallas as pl
from jax.experimental.pallas import tpu as pltpu
from jax.sharding import PartitionSpec as P

QH = 20
KVH = 4
GROUP = QH // KVH
HD = 128
SPAN = 4
SCALE = HD**-0.5
LOG2E = 1.4426950408889634
HIDDEN = -1e30

rope_base = 1000000.0

f32 = jnp.float32
bf16 = jnp.bfloat16


def permute(value, pairs):
    return lax.ppermute(value, "ctx", pairs)


def angle_tables(places):
    half = HD // 2
    freqs = rope_base ** (-(2.0 * jnp.arange(half, dtype=f32)) / HD)
    angles = places.astype(f32)[:, None] * freqs[None, :]
    cosine, sine = jnp.cos(angles), jnp.sin(angles)
    return jnp.concatenate([cosine, cosine], axis=1), jnp.concatenate([-sine, sine], axis=1)


def rotate(values, cosine, sine):
    rows = values.shape[0]
    split = values.astype(f32).reshape(rows, -1, HD)
    swapped = jnp.concatenate([split[..., HD // 2 :], split[..., : HD // 2]], axis=-1)
    return (split * cosine[:, None] + swapped * sine[:, None]).reshape(rows, -1)


def dot(a, b, ca, cb):
    return lax.dot_general(a, b, (((ca,), (cb,)), ((), ())), preferred_element_type=f32)


def turn(x, cosine, sine):
    return x * cosine + pltpu.roll(x, HD // 2, 1) * sine


def attend_kernel(
    seen, q_ref, g_ref, cos_ref, sin_ref, own_ref, w1_ref, w2_ref, w3_ref, pr_ref,
    o_ref, dq_ref, d0_ref, d1_ref, d2_ref, d3_ref, dp_ref,
    k_buf, v_buf, dk_buf, dv_buf,
):
    rows = q_ref.shape[0]
    width = KVH * HD
    col = pl.program_id(0) * HD
    k_at = pl.ds(pl.multiple_of(col, HD), HD)
    v_at = pl.ds(pl.multiple_of(col + width, HD), HD)
    parts = [own_ref, w1_ref, w2_ref, w3_ref, pr_ref]
    starts = [0, rows, 2 * rows, 3 * rows, 4 * rows]
    for part, start in zip(parts, starts):
        count = part.shape[0]
        k_buf[start : start + count, :] = part[:, k_at]
        v_buf[start : start + count, :] = part[:, v_at]
    k, v = k_buf[...], v_buf[...]
    cosine, sine = cos_ref[...], sin_ref[...]
    lower = lax.broadcasted_iota(jnp.int32, (rows, rows), 1) <= lax.broadcasted_iota(
        jnp.int32, (rows, rows), 0
    )
    bias = [jnp.where(seen[i] > 0, 0.0, HIDDEN).astype(f32) for i in range(3)]
    for h in range(GROUP):
        cols = slice(h * HD, (h + 1) * HD)
        q = turn(q_ref[:, cols].astype(f32), cosine, sine).astype(bf16)
        g = g_ref[:, cols]
        s = dot(q, k, 1, 1)
        s_own = jnp.where(lower, s[:, :rows], HIDDEN)
        s_win = [s[:, rows * (i + 1) : rows * (i + 2)] for i in range(3)]
        s_pr = s[:, 4 * rows :]
        peak = jnp.maximum(
            jnp.max(s_own, axis=1, keepdims=True), jnp.max(s_pr, axis=1, keepdims=True)
        )
        for i in range(3):
            peak = jnp.maximum(peak, jnp.max(s_win[i], axis=1, keepdims=True) + bias[i])
        base = peak * (SCALE * LOG2E)
        e = (
            [jnp.exp2(s_own * (SCALE * LOG2E) - base)]
            + [jnp.exp2(s_win[i] * (SCALE * LOG2E) - (base - bias[i])) for i in range(3)]
            + [jnp.exp2(s_pr * (SCALE * LOG2E) - base)]
        )
        total = sum(jnp.sum(x, axis=1, keepdims=True) for x in e)
        w = jnp.concatenate(e, axis=1) * (1.0 / total)
        wb = w.astype(bf16)
        o = dot(wb, v, 1, 0).astype(bf16)
        o_ref[:, cols] = o
        delta = jnp.sum(o.astype(f32) * g.astype(f32), axis=1, keepdims=True)
        dw = dot(g, v, 1, 1)
        ds = (w * (dw - delta) * SCALE).astype(bf16)
        dq_ref[:, cols] = turn(dot(ds, k, 1, 0), cosine, -sine).astype(bf16)
        dk, dv = dot(ds, q, 0, 0), dot(wb, g, 0, 0)
        if h == 0:
            dk_buf[...] = dk
            dv_buf[...] = dv
        else:
            dk_buf[...] += dk
            dv_buf[...] += dv
    outs = [d0_ref, d1_ref, d2_ref, d3_ref, dp_ref]
    for out, start in zip(outs, starts):
        count = out.shape[0]
        out[:, k_at] = dk_buf[start : start + count, :].astype(out.dtype)
        out[:, v_at] = dv_buf[start : start + count, :].astype(out.dtype)


def attend(seen, queries, grads, cosine, sine, own, w1, w2, w3, prompt):
    rows = queries.shape[0]
    wide = own.shape[1]
    count = prompt.shape[0]
    keys = SPAN * rows + count
    head = pl.BlockSpec((rows, GROUP * HD), lambda i, s: (0, i))

    def whole(shape):
        return pl.BlockSpec(shape, lambda i, s: (0, 0))

    block = whole((rows, wide))
    return pl.pallas_call(
        attend_kernel,
        grid_spec=pltpu.PrefetchScalarGridSpec(
            num_scalar_prefetch=1,
            grid=(KVH,),
            in_specs=[head, head, whole((rows, HD)), whole((rows, HD))]
            + [block] * 4
            + [whole((count, wide))],
            out_specs=[head, head] + [block] * 4 + [whole((count, wide))],
            scratch_shapes=[pltpu.VMEM((keys, HD), bf16)] * 2 + [pltpu.VMEM((keys, HD), f32)] * 2,
        ),
        out_shape=[
            jax.ShapeDtypeStruct(queries.shape, bf16),
            jax.ShapeDtypeStruct(queries.shape, bf16),
            jax.ShapeDtypeStruct((rows, wide), f32),
            jax.ShapeDtypeStruct((rows, wide), bf16),
            jax.ShapeDtypeStruct((rows, wide), f32),
            jax.ShapeDtypeStruct((rows, wide), bf16),
            jax.ShapeDtypeStruct((count, wide), f32),
        ],
        compiler_params=pltpu.CompilerParams(vmem_limit_bytes=56 * 2**20),
        name="attend",
    )(seen, queries, grads, cosine, sine, own, w1, w2, w3, prompt)


def local(
    queries, answer_keys, answer_values, prompt_keys, prompt_values, positions, ancestry, out_grad
):
    n = lax.axis_size("ctx")
    width = answer_keys.shape[1]
    me = lax.axis_index("ctx")
    core = me % 2
    swap = [(i, i ^ 1) for i in range(n)]
    ahead = [(i, i + 2) for i in range(n - 2)]
    across = [(i, i + 1) for i in range(0, n, 2)] + [(i, i + 3) for i in range(1, n - 3, 2)]

    def back(pairs):
        return [(b, a) for a, b in pairs]

    prompt_rows = prompt_keys.shape[0]
    prompt_places = me * prompt_rows + jnp.arange(prompt_rows, dtype=jnp.int32)
    pcos, psin = angle_tables(prompt_places)
    mine = jnp.concatenate([rotate(prompt_keys, pcos, psin).astype(bf16), prompt_values], axis=1)
    chip = jnp.concatenate([mine, permute(mine, swap)], axis=0)

    cosine, sine = angle_tables(positions)
    own = jnp.concatenate([rotate(answer_keys, cosine, sine).astype(bf16), answer_values], axis=1)
    w2 = permute(own, ahead)
    w1 = permute(own, across)
    w3 = permute(w2, swap)
    rounds = [[(i, (i + 2 * k) % n) for i in range(n)] for k in range(1, n // 2)]
    prompt = jnp.concatenate([chip] + [permute(chip, pairs) for pairs in rounds], axis=0)

    table = ancestry[0]
    steps = jnp.stack([3 - 2 * core, 2 + 0 * core, 1 + 2 * core])
    match = jnp.arange(table.shape[0], dtype=jnp.int32)[None, :] == (me - steps)[:, None]
    seen = jnp.sum(jnp.where(match, table[None, :], 0), axis=1).astype(jnp.int32)

    attended, grad_queries, d0, d1, d2, d3, dp = attend(
        seen, queries, out_grad, cosine, sine, own, w1, w2, w3, prompt
    )
    r3 = permute(d3, swap)
    r1 = permute(d1, back(across))
    r2 = permute((d2 + r3.astype(f32)).astype(bf16), back(ahead))
    terms = dp.reshape(n // 2, 2 * prompt_rows, 2 * width)
    total = terms[0]
    for k, pairs in enumerate(rounds):
        total = total + permute(terms[k + 1], back(pairs))
    prompt_sum = total[:prompt_rows] + permute(total[prompt_rows:], swap)

    summed = d0 + (r1.astype(f32) + r2.astype(f32))
    grad_keys = rotate(summed[:, :width], cosine, -sine).astype(bf16)
    grad_values = summed[:, width:].astype(bf16)
    grad_prompt_keys = rotate(prompt_sum[:, :width], pcos, -psin).astype(bf16)
    grad_prompt_values = prompt_sum[:, width:].astype(bf16)
    return (attended, grad_queries, grad_keys, grad_values, grad_prompt_keys, grad_prompt_values)


def solution(mesh):
    rows = P(("groups", "ctx"), None)
    return jax.shard_map(
        local,
        mesh=mesh,
        in_specs=(rows, rows, rows, rows, rows, P(("groups", "ctx")), rows, rows),
        out_specs=(rows,) * 6,
        check_vma=False,
    )
```

time: 328 us -> 126 us (0.38)
  the two profiles are of different devices: /device:TPU:1 before, /device:TPU:0 now
where the time goes in v1:
time: 126 us; the launch traced here: 123 us
  Pallas kernels  37 us (29%)
  starting transfers between devices  33.5 us (27%)
  waiting for transfers between devices  32.9 us (26%)
  local copies, waits for them, and re-layouts  11.6 us (9%)
  other arithmetic  7.23 us (6%)
    pallas_call x1, Pallas kernels, attend(): pl.pallas_call(attend_kernel, grid_spec=pltpu.PrefetchScalarGridSpec(num_...  37 us
    ppermute x22, starting transfers between devices, permute(): return lax.ppermute(value, 'ctx', pairs)  33.5 us
    ppermute x22, waiting for transfers between devices, permute(): return lax.ppermute(value, 'ctx', pairs)  32.9 us
    concatenate x1, local copies, waits for them, and re-layouts, local(): jnp.concatenate([chip] + [permute(chip, pairs) for pairs in rounds], axis=0)  4.83 us
  transfers between devices with their start and end apart: 22, of which 10 were waited for; matrix products, arithmetic and copies ran while one was open for 8% of the time, Pallas kernels for 0%

profile of v1, /device:TPU:0, one launch (start us, length us, event | category | flops | bytes accessed | tf_op | source)
XLA Modules:
  0.0 123.2 jit_solution(1384952184188780444)
XLA Ops:
  4.9 4.9 %collective-permute-start.1 = (bf16[256,1024]{1,0:T(8,128)(2,1)S(1)}, bf16[256,1024]{1,0:T(8,128)(2,1)S(1)}, u32[]{:S(2)}, u32[]{:S(2)}) collective-permute-start(bf16[256,1024]{1,0:T(8,128)(2,1)S(1)} %pad_maximum_fusion.own_ref), channel_id=1, source_target_pairs={{0,2},{1,3},{2,4},{3,5},{4,6},{5,7},{6,8},{7,9},{8,10},{9,11},{10,... | collective-permute-start | bytes 1572872 | tf_op jit(solution)/shard_map/ppermute | solution.py:26
  9.8 1.5 %collective-permute-start = (bf16[256,1024]{1,0:T(8,128)(2,1)S(1)}, bf16[256,1024]{1,0:T(8,128)(2,1)S(1)}, u32[]{:S(2)}, u32[]{:S(2)}) collective-permute-start(bf16[256,1024]{1,0:T(8,128)(2,1)S(1)} %pad_maximum_fusion.own_ref), channel_id=1, source_target_pairs={{0,1},{2,3},{4,5},{6,7},{8,9},{10,11},{12,13},{14,15},{1,4},{3,6},... | collective-permute-start | bytes 1572872 | tf_op jit(solution)/shard_map/ppermute | solution.py:26
  11.7 9.3 %collective-permute-done.1.w2_ref = bf16[256,1024]{1,0:T(8,128)(2,1)S(1)} collective-permute-done((bf16[256,1024]{1,0:T(8,128)(2,1)S(1)}, bf16[256,1024]{1,0:T(8,128)(2,1)S(1)}, u32[]{:S(2)}, u32[]{:S(2)}) %collective-permute-start.1) | collective-permute-done | bytes 524320 | tf_op jit(solution)/shard_map/ppermute | solution.py:26
  21.6 1.3 %collective-permute-done.3 = bf16[4,1024]{1,0:T(4,128)(2,1)S(1)} collective-permute-done((bf16[4,1024]{1,0:T(4,128)(2,1)S(1)}, bf16[4,1024]{1,0:T(4,128)(2,1)S(1)}, u32[]{:S(2)}, u32[]{:S(2)}) %collective-permute-start.3) | collective-permute-done | bytes 8224 | tf_op jit(solution)/shard_map/ppermute | solution.py:26
  22.9 5.6 %collective-permute-start.10 = (bf16[8,1024]{1,0:T(8,128)(2,1)S(1)}, bf16[8,1024]{1,0:T(8,128)(2,1)S(1)}, u32[]{:S(2)}, u32[]{:S(2)}) collective-permute-start(bf16[8,1024]{1,0:T(8,128)(2,1)S(1)} %pad_maximum_fusion.3), channel_id=1, source_target_pairs={{0,14},{1,15},{2,0},{3,1},{4,2},{5,3},{6,4},{7,5},{8,6},{9,7},{10,... | collective-permute-start | bytes 49160 | tf_op jit(solution)/shard_map/ppermute | solution.py:26
  28.5 1.2 collective-permute-start.9
  30.5 3.5 %collective-permute-start.7 = (bf16[8,1024]{1,0:T(8,128)(2,1)S(1)}, bf16[8,1024]{1,0:T(8,128)(2,1)S(1)}, u32[]{:S(2)}, u32[]{:S(2)}) collective-permute-start(bf16[8,1024]{1,0:T(8,128)(2,1)S(1)} %pad_maximum_fusion.3), channel_id=1, source_target_pairs={{0,8},{1,9},{2,10},{3,11},{4,12},{5,13},{6,14},{7,15},{8,0},{9,1},... | collective-permute-start | bytes 49160 | tf_op jit(solution)/shard_map/ppermute | solution.py:26
  34.0 1.5 %collective-permute-start.6 = (bf16[8,1024]{1,0:T(8,128)(2,1)S(1)}, bf16[8,1024]{1,0:T(8,128)(2,1)S(1)}, u32[]{:S(2)}, u32[]{:S(2)}) collective-permute-start(bf16[8,1024]{1,0:T(8,128)(2,1)S(1)} %pad_maximum_fusion.3), channel_id=1, source_target_pairs={{0,6},{1,7},{2,8},{3,9},{4,10},{5,11},{6,12},{7,13},{8,14},{9,15},... | collective-permute-start | bytes 49160 | tf_op jit(solution)/shard_map/ppermute | solution.py:26
  35.8 1.4 %collective-permute-start.4 = (bf16[8,1024]{1,0:T(8,128)(2,1)S(1)}, bf16[8,1024]{1,0:T(8,128)(2,1)S(1)}, u32[]{:S(2)}, u32[]{:S(2)}) collective-permute-start(bf16[8,1024]{1,0:T(8,128)(2,1)S(1)} %pad_maximum_fusion.3), channel_id=1, source_target_pairs={{0,2},{1,3},{2,4},{3,5},{4,6},{5,7},{6,8},{7,9},{8,10},{9,11},{10,... | collective-permute-start | bytes 49160 | tf_op jit(solution)/shard_map/ppermute | solution.py:26
  37.9 1.8 %collective-permute-done.6 = bf16[8,1024]{1,0:T(8,128)(2,1)S(1)} collective-permute-done((bf16[8,1024]{1,0:T(8,128)(2,1)S(1)}, bf16[8,1024]{1,0:T(8,128)(2,1)S(1)}, u32[]{:S(2)}, u32[]{:S(2)}) %collective-permute-start.6) | collective-permute-done | bytes 16416 | tf_op jit(solution)/shard_map/ppermute | solution.py:26
  39.7 1.4 %collective-permute-done.5 = bf16[8,1024]{1,0:T(8,128)(2,1)S(1)} collective-permute-done((bf16[8,1024]{1,0:T(8,128)(2,1)S(1)}, bf16[8,1024]{1,0:T(8,128)(2,1)S(1)}, u32[]{:S(2)}, u32[]{:S(2)}) %collective-permute-start.5) | collective-permute-done | bytes 16416 | tf_op jit(solution)/shard_map/ppermute | solution.py:26
  41.1 1.2 collective-permute-done.4
  42.3 4.8 %concatenate.58.pr_ref = bf16[64,1024]{1,0:T(8,128)(2,1)} concatenate(bf16[4,1024]{1,0:T(4,128)(2,1)S(1)} %pad_maximum_fusion.4, bf16[4,1024]{1,0:T(4,128)(2,1)S(1)} %collective-permute-done.3, bf16[8,1024]{1,0:T(8,128)(2,1)S(1)} %collective-permute-done.4, bf16[8,1024]{1,0:T(8,128)(2,1)S(1)} %collective-permute-done.5, bf16[8,1024]{1,0:T(8,128)(2,1)S(1)} %collective-permute-done.6, ...), dimensions={0} | concatenate | bytes 262144 | tf_op jit(solution)/shard_map/concatenate | solution.py:178
  48.7 37.0 %attend.1 = (bf16[256,2560]{1,0:T(8,128)(2,1)}, bf16[256,2560]{1,0:T(8,128)(2,1)}, f32[256,1024]{1,0:T(8,128)}, bf16[256,1024]{1,0:T(8,128)(2,1)}, f32[256,1024]...) custom-call(s32[3]{0:T(128)} %select_reduce_fusion.seen, bf16[256,2560]{1,0:T(8,128)(2,1)} %q_ref.1, ...), custom_call_target="tpu_custom_call" | custom-call | tf_op jit(solution)/shard_map/attend/pallas_call | solution.py:127
  86.6 1.9 %collective-permute-start.14 = (f32[8,1024]{1,0:T(8,128)S(1)}, f32[8,1024]{1,0:T(8,128)S(1)}, u32[]{:S(2)}, u32[]{:S(2)}) collective-permute-start(f32[8,1024]{1,0:T(8,128)S(1)} %get-tuple-element.28), channel_id=1, source_target_pairs={{2,0},{3,1},{4,2},{5,3},{6,4},{7,5},{8,6},{9,7},{10,8},{11,9},{12,... | collective-permute-start | bytes 98312 | tf_op jit(solution)/shard_map/ppermute | solution.py:26
  88.7 1.8 %collective-permute-start.18 = (f32[8,1024]{1,0:T(8,128)S(1)}, f32[8,1024]{1,0:T(8,128)S(1)}, u32[]{:S(2)}, u32[]{:S(2)}) collective-permute-start(f32[8,1024]{1,0:T(8,128)S(1)} %get-tuple-element.31), channel_id=1, source_target_pairs={{10,0},{11,1},{12,2},{13,3},{14,4},{15,5},{0,6},{1,7},{2,8},{3,9},... | collective-permute-start | bytes 98312 | tf_op jit(solution)/shard_map/ppermute | solution.py:26
  90.5 3.3 %collective-permute-start.17 = (f32[8,1024]{1,0:T(8,128)S(1)}, f32[8,1024]{1,0:T(8,128)S(1)}, u32[]{:S(2)}, u32[]{:S(2)}) collective-permute-start(f32[8,1024]{1,0:T(8,128)S(1)} %get-tuple-element.32), channel_id=1, source_target_pairs={{8,0},{9,1},{10,2},{11,3},{12,4},{13,5},{14,6},{15,7},{0,8},{1,9},... | collective-permute-start | bytes 98312 | tf_op jit(solution)/shard_map/ppermute | solution.py:26
  93.8 1.4 %collective-permute-done.20 = f32[8,1024]{1,0:T(8,128)S(1)} collective-permute-done((f32[8,1024]{1,0:T(8,128)S(1)}, f32[8,1024]{1,0:T(8,128)S(1)}, u32[]{:S(2)}, u32[]{:S(2)}) %collective-permute-start.20) | collective-permute-done | bytes 32800 | tf_op jit(solution)/shard_map/ppermute | solution.py:26
  95.3 2.8 %collective-permute-start.15 = (f32[8,1024]{1,0:T(8,128)S(1)}, f32[8,1024]{1,0:T(8,128)S(1)}, u32[]{:S(2)}, u32[]{:S(2)}) collective-permute-start(f32[8,1024]{1,0:T(8,128)S(1)} %get-tuple-element.34), channel_id=1, source_target_pairs={{4,0},{5,1},{6,2},{7,3},{8,4},{9,5},{10,6},{11,7},{12,8},{13,9},{1... | collective-permute-start | bytes 98312 | tf_op jit(solution)/shard_map/ppermute | solution.py:26
  98.1 2.3 %collective-permute-done.16 = f32[8,1024]{1,0:T(8,128)S(1)} collective-permute-done((f32[8,1024]{1,0:T(8,128)S(1)}, f32[8,1024]{1,0:T(8,128)S(1)}, u32[]{:S(2)}, u32[]{:S(2)}) %collective-permute-start.16) | collective-permute-done | bytes 32800 | tf_op jit(solution)/shard_map/ppermute | solution.py:26
  101.2 1.3 %collective-permute-start.11 = (bf16[256,1024]{1,0:T(8,128)(2,1)}, bf16[256,1024]{1,0:T(8,128)(2,1)S(1)}, u32[]{:S(2)}, u32[]{:S(2)}) collective-permute-start(bf16[256,1024]{1,0:T(8,128)(2,1)} %get-tuple-element.16), channel_id=1, source_target_pairs={{1,0},{3,2},{5,4},{7,6},{9,8},{11,10},{13,12},{15,14},{4,1},{6,3},... | collective-permute-start | bytes 1572872 | tf_op jit(solution)/shard_map/ppermute | solution.py:26
  102.6 1.4 %add_convert_fusion = bf16[256,1024]{1,0:T(8,128)(2,1)S(1)} fusion(f32[256,1024]{1,0:T(8,128)} %get-tuple-element.17, bf16[256,1024]{1,0:T(8,128)(2,1)S(1)} %collective-permute-done.12), kind=kLoop, calls=%fused_computation.1 | loop fusion | flops 786432 | bytes 2097152 | tf_op jit(solution)/shard_map/convert_element_type | solution.py:190
  103.9 1.3 %collective-permute-start.13 = (bf16[256,1024]{1,0:T(8,128)(2,1)S(1)}, bf16[256,1024]{1,0:T(8,128)(2,1)S(1)}, u32[]{:S(2)}, u32[]{:S(2)}) collective-permute-start(bf16[256,1024]{1,0:T(8,128)(2,1)S(1)} %add_convert_fusion), channel_id=1, source_target_pairs={{2,0},{3,1},{4,2},{5,3},{6,4},{7,5},{8,6},{9,7},{10,8},{11,9},{12,... | collective-permute-start | bytes 1572872 | tf_op jit(solution)/shard_map/ppermute | solution.py:26
  106.6 13.9 %collective-permute-done.13 = bf16[256,1024]{1,0:T(8,128)(2,1)S(1)} collective-permute-done((bf16[256,1024]{1,0:T(8,128)(2,1)S(1)}, bf16[256,1024]{1,0:T(8,128)(2,1)S(1)}, u32[]{:S(2)}, u32[]{:S(2)}) %collective-permute-start.13) | collective-permute-done | bytes 524320 | tf_op jit(solution)/shard_map/ppermute | solution.py:26
  (86 shorter events, 14.7 us)
Async XLA Ops:
  4.5 32.7 %copy-start.11 = (s32[1,16]{1,0:T(1,128)S(1)}, s32[1,16]{1,0:T(1,128)}, u32[]{:S(2)}) copy-start(s32[1,16]{1,0:T(1,128)} %param.14) | copy-start | bytes 196
  4.9 42.2 %copy-start = (bf16[256,1024]{1,0:T(8,128)(2,1)}, bf16[256,1024]{1,0:T(8,128)(2,1)S(1)}, u32[]{:S(2)}) copy-start(bf16[256,1024]{1,0:T(8,128)(2,1)S(1)} %pad_maximum_fusion.own_ref) | copy-start | bytes 1572868
  4.9 16.0 %collective-permute-start.1 = (bf16[256,1024]{1,0:T(8,128)(2,1)S(1)}, bf16[256,1024]{1,0:T(8,128)(2,1)S(1)}, u32[]{:S(2)}, u32[]{:S(2)}) collective-permute-start(bf16[256,1024]{1,0:T(8,128)(2,1)S(1)} %pad_maximum_fusion.own_ref), channel_id=1, source_target_pairs={{0,2},{1,3},{2,4},{3,5},{4,6},{5,7},{6,8},{7,9},{8,10},{9,11},{10,... | collective-permute-start | bytes 1572872 | tf_op jit(solution)/shard_map/ppermute | solution.py:26
  9.8 37.3 %collective-permute-start = (bf16[256,1024]{1,0:T(8,128)(2,1)S(1)}, bf16[256,1024]{1,0:T(8,128)(2,1)S(1)}, u32[]{:S(2)}, u32[]{:S(2)}) collective-permute-start(bf16[256,1024]{1,0:T(8,128)(2,1)S(1)} %pad_maximum_fusion.own_ref), channel_id=1, source_target_pairs={{0,1},{2,3},{4,5},{6,7},{8,9},{10,11},{12,13},{14,15},{1,4},{3,6},... | collective-permute-start | bytes 1572872 | tf_op jit(solution)/shard_map/ppermute | solution.py:26
  21.0 26.1 %collective-permute-start.2 = (bf16[256,1024]{1,0:T(8,128)(2,1)S(1)}, bf16[256,1024]{1,0:T(8,128)(2,1)S(1)}, u32[]{:S(2)}, u32[]{:S(2)}) collective-permute-start(bf16[256,1024]{1,0:T(8,128)(2,1)S(1)} %collective-permute-done.1.w2_ref), channel_id=1, source_target_pairs={{0,1},{1,0},{2,3},{3,2},{4,5},{5,4},{6,7},{7,6},{8,9},{9,8},{10,11... | collective-permute-start | bytes 1572872 | tf_op jit(solution)/shard_map/ppermute | solution.py:26
  21.0 1.9 %collective-permute-start.3 = (bf16[4,1024]{1,0:T(4,128)(2,1)S(1)}, bf16[4,1024]{1,0:T(4,128)(2,1)S(1)}, u32[]{:S(2)}, u32[]{:S(2)}) collective-permute-start(bf16[4,1024]{1,0:T(4,128)(2,1)S(1)} %pad_maximum_fusion.4), channel_id=1, source_target_pairs={{0,1},{1,0},{2,3},{3,2},{4,5},{5,4},{6,7},{7,6},{8,9},{9,8},{10,11... | collective-permute-start | bytes 24584 | tf_op jit(solution)/shard_map/ppermute | solution.py:26
  22.9 7.6 %collective-permute-start.10 = (bf16[8,1024]{1,0:T(8,128)(2,1)S(1)}, bf16[8,1024]{1,0:T(8,128)(2,1)S(1)}, u32[]{:S(2)}, u32[]{:S(2)}) collective-permute-start(bf16[8,1024]{1,0:T(8,128)(2,1)S(1)} %pad_maximum_fusion.3), channel_id=1, source_target_pairs={{0,14},{1,15},{2,0},{3,1},{4,2},{5,3},{6,4},{7,5},{8,6},{9,7},{10,... | collective-permute-start | bytes 49160 | tf_op jit(solution)/shard_map/ppermute | solution.py:26
  28.5 5.6 %collective-permute-start.9 = (bf16[8,1024]{1,0:T(8,128)(2,1)S(1)}, bf16[8,1024]{1,0:T(8,128)(2,1)S(1)}, u32[]{:S(2)}, u32[]{:S(2)}) collective-permute-start(bf16[8,1024]{1,0:T(8,128)(2,1)S(1)} %pad_maximum_fusion.3), channel_id=1, source_target_pairs={{0,12},{1,13},{2,14},{3,15},{4,0},{5,1},{6,2},{7,3},{8,4},{9,5},{1... | collective-permute-start | bytes 49160 | tf_op jit(solution)/shard_map/ppermute | solution.py:26
  29.6 5.9 %collective-permute-start.8 = (bf16[8,1024]{1,0:T(8,128)(2,1)S(1)}, bf16[8,1024]{1,0:T(8,128)(2,1)S(1)}, u32[]{:S(2)}, u32[]{:S(2)}) collective-permute-start(bf16[8,1024]{1,0:T(8,128)(2,1)S(1)} %pad_maximum_fusion.3), channel_id=1, source_target_pairs={{0,10},{1,11},{2,12},{3,13},{4,14},{5,15},{6,0},{7,1},{8,2},{9,3},... | collective-permute-start | bytes 49160 | tf_op jit(solution)/shard_map/ppermute | solution.py:26
  30.5 5.4 %collective-permute-start.7 = (bf16[8,1024]{1,0:T(8,128)(2,1)S(1)}, bf16[8,1024]{1,0:T(8,128)(2,1)S(1)}, u32[]{:S(2)}, u32[]{:S(2)}) collective-permute-start(bf16[8,1024]{1,0:T(8,128)(2,1)S(1)} %pad_maximum_fusion.3), channel_id=1, source_target_pairs={{0,8},{1,9},{2,10},{3,11},{4,12},{5,13},{6,14},{7,15},{8,0},{9,1},... | collective-permute-start | bytes 49160 | tf_op jit(solution)/shard_map/ppermute | solution.py:26
  34.0 5.7 %collective-permute-start.6 = (bf16[8,1024]{1,0:T(8,128)(2,1)S(1)}, bf16[8,1024]{1,0:T(8,128)(2,1)S(1)}, u32[]{:S(2)}, u32[]{:S(2)}) collective-permute-start(bf16[8,1024]{1,0:T(8,128)(2,1)S(1)} %pad_maximum_fusion.3), channel_id=1, source_target_pairs={{0,6},{1,7},{2,8},{3,9},{4,10},{5,11},{6,12},{7,13},{8,14},{9,15},... | collective-permute-start | bytes 49160 | tf_op jit(solution)/shard_map/ppermute | solution.py:26
  35.5 5.5 %collective-permute-start.5 = (bf16[8,1024]{1,0:T(8,128)(2,1)S(1)}, bf16[8,1024]{1,0:T(8,128)(2,1)S(1)}, u32[]{:S(2)}, u32[]{:S(2)}) collective-permute-start(bf16[8,1024]{1,0:T(8,128)(2,1)S(1)} %pad_maximum_fusion.3), channel_id=1, source_target_pairs={{0,4},{1,5},{2,6},{3,7},{4,8},{5,9},{6,10},{7,11},{8,12},{9,13},{1... | collective-permute-start | bytes 49160 | tf_op jit(solution)/shard_map/ppermute | solution.py:26
  35.8 6.4 %collective-permute-start.4 = (bf16[8,1024]{1,0:T(8,128)(2,1)S(1)}, bf16[8,1024]{1,0:T(8,128)(2,1)S(1)}, u32[]{:S(2)}, u32[]{:S(2)}) collective-permute-start(bf16[8,1024]{1,0:T(8,128)(2,1)S(1)} %pad_maximum_fusion.3), channel_id=1, source_target_pairs={{0,2},{1,3},{2,4},{3,5},{4,6},{5,7},{6,8},{7,9},{8,10},{9,11},{10,... | collective-permute-start | bytes 49160 | tf_op jit(solution)/shard_map/ppermute | solution.py:26
  86.6 4.0 %collective-permute-start.14 = (f32[8,1024]{1,0:T(8,128)S(1)}, f32[8,1024]{1,0:T(8,128)S(1)}, u32[]{:S(2)}, u32[]{:S(2)}) collective-permute-start(f32[8,1024]{1,0:T(8,128)S(1)} %get-tuple-element.28), channel_id=1, source_target_pairs={{2,0},{3,1},{4,2},{5,3},{6,4},{7,5},{8,6},{9,7},{10,8},{11,9},{12,... | collective-permute-start | bytes 98312 | tf_op jit(solution)/shard_map/ppermute | solution.py:26
  88.5 6.8 %collective-permute-start.20 = (f32[8,1024]{1,0:T(8,128)S(1)}, f32[8,1024]{1,0:T(8,128)S(1)}, u32[]{:S(2)}, u32[]{:S(2)}) collective-permute-start(f32[8,1024]{1,0:T(8,128)S(1)} %get-tuple-element.29), channel_id=1, source_target_pairs={{14,0},{15,1},{0,2},{1,3},{2,4},{3,5},{4,6},{5,7},{6,8},{7,9},{8,1... | collective-permute-start | bytes 98312 | tf_op jit(solution)/shard_map/ppermute | solution.py:26
  88.7 6.6 %collective-permute-start.19 = (f32[8,1024]{1,0:T(8,128)S(1)}, f32[8,1024]{1,0:T(8,128)S(1)}, u32[]{:S(2)}, u32[]{:S(2)}) collective-permute-start(f32[8,1024]{1,0:T(8,128)S(1)} %get-tuple-element.30), channel_id=1, source_target_pairs={{12,0},{13,1},{14,2},{15,3},{0,4},{1,5},{2,6},{3,7},{4,8},{5,9},{6... | collective-permute-start | bytes 98312 | tf_op jit(solution)/shard_map/ppermute | solution.py:26
  88.7 13.8 %collective-permute-start.12 = (bf16[256,1024]{1,0:T(8,128)(2,1)}, bf16[256,1024]{1,0:T(8,128)(2,1)S(1)}, u32[]{:S(2)}, u32[]{:S(2)}) collective-permute-start(bf16[256,1024]{1,0:T(8,128)(2,1)} %get-tuple-element.18), channel_id=1, source_target_pairs={{0,1},{1,0},{2,3},{3,2},{4,5},{5,4},{6,7},{7,6},{8,9},{9,8},{10,11... | collective-permute-start | bytes 1572872 | tf_op jit(solution)/shard_map/ppermute | solution.py:26
  88.7 9.3 %collective-permute-start.18 = (f32[8,1024]{1,0:T(8,128)S(1)}, f32[8,1024]{1,0:T(8,128)S(1)}, u32[]{:S(2)}, u32[]{:S(2)}) collective-permute-start(f32[8,1024]{1,0:T(8,128)S(1)} %get-tuple-element.31), channel_id=1, source_target_pairs={{10,0},{11,1},{12,2},{13,3},{14,4},{15,5},{0,6},{1,7},{2,8},{3,9},... | collective-permute-start | bytes 98312 | tf_op jit(solution)/shard_map/ppermute | solution.py:26
  90.5 7.5 %collective-permute-start.17 = (f32[8,1024]{1,0:T(8,128)S(1)}, f32[8,1024]{1,0:T(8,128)S(1)}, u32[]{:S(2)}, u32[]{:S(2)}) collective-permute-start(f32[8,1024]{1,0:T(8,128)S(1)} %get-tuple-element.32), channel_id=1, source_target_pairs={{8,0},{9,1},{10,2},{11,3},{12,4},{13,5},{14,6},{15,7},{0,8},{1,9},... | collective-permute-start | bytes 98312 | tf_op jit(solution)/shard_map/ppermute | solution.py:26
  95.3 5.0 %collective-permute-start.16 = (f32[8,1024]{1,0:T(8,128)S(1)}, f32[8,1024]{1,0:T(8,128)S(1)}, u32[]{:S(2)}, u32[]{:S(2)}) collective-permute-start(f32[8,1024]{1,0:T(8,128)S(1)} %get-tuple-element.33), channel_id=1, source_target_pairs={{6,0},{7,1},{8,2},{9,3},{10,4},{11,5},{12,6},{13,7},{14,8},{15,9},... | collective-permute-start | bytes 98312 | tf_op jit(solution)/shard_map/ppermute | solution.py:26
  95.3 5.0 %collective-permute-start.15 = (f32[8,1024]{1,0:T(8,128)S(1)}, f32[8,1024]{1,0:T(8,128)S(1)}, u32[]{:S(2)}, u32[]{:S(2)}) collective-permute-start(f32[8,1024]{1,0:T(8,128)S(1)} %get-tuple-element.34), channel_id=1, source_target_pairs={{4,0},{5,1},{6,2},{7,3},{8,4},{9,5},{10,6},{11,7},{12,8},{13,9},{1... | collective-permute-start | bytes 98312 | tf_op jit(solution)/shard_map/ppermute | solution.py:26
  101.1 1.4 %collective-permute-start.21 = (f32[4,1024]{1,0:T(4,128)S(1)}, f32[4,1024]{1,0:T(4,128)S(1)}, u32[]{:S(2)}, u32[]{:S(2)}) collective-permute-start(f32[4,1024]{1,0:T(4,128)S(1)} %slice.107), channel_id=1, source_target_pairs={{0,1},{1,0},{2,3},{3,2},{4,5},{5,4},{6,7},{7,6},{8,9},{9,8},{10,11... | collective-permute-start | bytes 49160 | tf_op jit(solution)/shard_map/ppermute | solution.py:26
  101.2 5.4 %collective-permute-start.11 = (bf16[256,1024]{1,0:T(8,128)(2,1)}, bf16[256,1024]{1,0:T(8,128)(2,1)S(1)}, u32[]{:S(2)}, u32[]{:S(2)}) collective-permute-start(bf16[256,1024]{1,0:T(8,128)(2,1)} %get-tuple-element.16), channel_id=1, source_target_pairs={{1,0},{3,2},{5,4},{7,6},{9,8},{11,10},{13,12},{15,14},{4,1},{6,3},... | collective-permute-start | bytes 1572872 | tf_op jit(solution)/shard_map/ppermute | solution.py:26
  103.9 16.5 %collective-permute-start.13 = (bf16[256,1024]{1,0:T(8,128)(2,1)S(1)}, bf16[256,1024]{1,0:T(8,128)(2,1)S(1)}, u32[]{:S(2)}, u32[]{:S(2)}) collective-permute-start(bf16[256,1024]{1,0:T(8,128)(2,1)S(1)} %add_convert_fusion), channel_id=1, source_target_pairs={{2,0},{3,1},{4,2},{5,3},{6,4},{7,5},{8,6},{9,7},{10,8},{11,9},{12,... | collective-permute-start | bytes 1572872 | tf_op jit(solution)/shard_map/ppermute | solution.py:26
  (10 other events, 87.4 us)

commit v2 on v1

v2 whole, which is shorter than its diff:
```python
import jax
import jax.numpy as jnp
from jax import lax
from jax.experimental import pallas as pl
from jax.experimental.pallas import tpu as pltpu
from jax.sharding import PartitionSpec as P

QH = 20
KVH = 4
GROUP = QH // KVH
HD = 128
WIDTH = KVH * HD
SPAN = 4
SCALE = HD**-0.5
LOG2E = 1.4426950408889634
HIDDEN = -1e30

rope_base = 1000000.0

f32 = jnp.float32
bf16 = jnp.bfloat16


def permute(value, pairs):
    return lax.ppermute(value, "ctx", pairs)


def back(pairs):
    return [(b, a) for a, b in pairs]


def angle_tables(places):
    lane = jnp.arange(HD, dtype=jnp.int32)
    freqs = rope_base ** (-(2.0 * (lane % (HD // 2)).astype(f32)) / HD)
    angles = places.astype(f32)[:, None] * freqs[None, :]
    sign = jnp.where(lane < HD // 2, -1.0, 1.0).astype(f32)
    return jnp.cos(angles), jnp.sin(angles) * sign[None, :]


def dot(a, b, ca, cb):
    return lax.dot_general(a, b, (((ca,), (cb,)), ((), ())), preferred_element_type=f32)


def turn(x, cosine, sine):
    return x * cosine + pltpu.roll(x, HD // 2, 1) * sine


def attend_kernel(*refs, pieces):
    seen, q_ref, g_ref, cos_ref, sin_ref = refs[:5]
    blocks = refs[5:9]
    prompts = refs[9 : 9 + pieces]
    o_ref, dq_ref, d0_ref, d1_ref, d2_ref, d3_ref, dp_ref = refs[9 + pieces : 16 + pieces]
    k_buf, v_buf, dk_buf, dv_buf, pk_buf, pv_buf = refs[16 + pieces :]
    rows = q_ref.shape[0]
    count = prompts[0].shape[0]
    half = count // 2
    col = pl.program_id(0) * HD
    k_at = pl.ds(pl.multiple_of(col, HD), HD)
    v_at = pl.ds(pl.multiple_of(col + WIDTH, HD), HD)
    for j, part in enumerate(blocks):
        span = slice(j * rows, (j + 1) * rows)
        raw = part[:, k_at].astype(f32)
        k_buf[span, :] = turn(raw, cos_ref[span, :], sin_ref[span, :]).astype(bf16)
        v_buf[span, :] = part[:, v_at]
    for j, part in enumerate(prompts):
        span = slice(j * count, (j + 1) * count)
        pk_buf[span, :] = part[:, k_at].astype(f32)
        pv_buf[span, :] = part[:, v_at].astype(f32)
    span = slice(SPAN * rows, SPAN * rows + pieces * count)
    k_buf[span, :] = turn(pk_buf[...], cos_ref[span, :], sin_ref[span, :]).astype(bf16)
    v_buf[span, :] = pv_buf[...].astype(bf16)
    k, v = k_buf[...], v_buf[...]
    cosine, sine = cos_ref[:rows, :], sin_ref[:rows, :]
    lower = lax.broadcasted_iota(jnp.int32, (rows, rows), 1) <= lax.broadcasted_iota(
        jnp.int32, (rows, rows), 0
    )
    bias = [jnp.where(seen[i] > 0, 0.0, HIDDEN).astype(f32) for i in range(3)]
    for h in range(GROUP):
        cols = slice(h * HD, (h + 1) * HD)
        q = turn(q_ref[:, cols].astype(f32), cosine, sine).astype(bf16)
        g = g_ref[:, cols]
        s = dot(q, k, 1, 1)
        s_own = jnp.where(lower, s[:, :rows], HIDDEN)
        s_win = [s[:, rows * (i + 1) : rows * (i + 2)] for i in range(3)]
        s_pr = s[:, 4 * rows :]
        peak = jnp.maximum(
            jnp.max(s_own, axis=1, keepdims=True), jnp.max(s_pr, axis=1, keepdims=True)
        )
        for i in range(3):
            peak = jnp.maximum(peak, jnp.max(s_win[i], axis=1, keepdims=True) + bias[i])
        base = peak * (SCALE * LOG2E)
        e = (
            [jnp.exp2(s_own * (SCALE * LOG2E) - base)]
            + [jnp.exp2(s_win[i] * (SCALE * LOG2E) - (base - bias[i])) for i in range(3)]
            + [jnp.exp2(s_pr * (SCALE * LOG2E) - base)]
        )
        total = sum(jnp.sum(x, axis=1, keepdims=True) for x in e)
        w = jnp.concatenate(e, axis=1) * (1.0 / total)
        wb = w.astype(bf16)
        o = dot(wb, v, 1, 0).astype(bf16)
        o_ref[:, cols] = o
        delta = jnp.sum(o.astype(f32) * g.astype(f32), axis=1, keepdims=True)
        dw = dot(g, v, 1, 1)
        ds = (w * (dw - delta) * SCALE).astype(bf16)
        dq_ref[:, cols] = turn(dot(ds, k, 1, 0), cosine, -sine).astype(bf16)
        dk, dv = dot(ds, q, 0, 0), dot(wb, g, 0, 0)
        if h == 0:
            dk_buf[...] = dk
            dv_buf[...] = dv
        else:
            dk_buf[...] += dk
            dv_buf[...] += dv
    outs = [d0_ref, d1_ref, d2_ref, d3_ref]
    for at, buf in ((k_at, dk_buf), (v_at, dv_buf)):
        for j, out in enumerate(outs):
            out[:rows, at] = buf[j * rows : (j + 1) * rows, :].astype(out.dtype)
        for j in range(pieces):
            start = SPAN * rows + j * count
            dp_ref[j * half : (j + 1) * half, at] = buf[start : start + half, :]
            d3_ref[rows + j * half : rows + (j + 1) * half, at] = buf[
                start + half : start + count, :
            ]


def attend(seen, queries, grads, cosine, sine, blocks, prompts):
    rows = queries.shape[0]
    wide = blocks[0].shape[1]
    pieces, count = len(prompts), prompts[0].shape[0]
    keys = SPAN * rows + pieces * count
    half = pieces * count // 2
    head = pl.BlockSpec((rows, GROUP * HD), lambda i, s: (0, i))

    def whole(*shape):
        return pl.BlockSpec(shape, lambda i, s: (0, 0))

    def body(*refs):
        attend_kernel(*refs, pieces=pieces)

    outs = [(rows, f32), (rows, bf16), (rows, f32), (rows + half, f32), (half, f32)]
    return pl.pallas_call(
        body,
        grid_spec=pltpu.PrefetchScalarGridSpec(
            num_scalar_prefetch=1,
            grid=(KVH,),
            in_specs=[head, head, whole(keys, HD), whole(keys, HD)]
            + [whole(rows, wide)] * 4
            + [whole(count, wide)] * pieces,
            out_specs=[head, head] + [whole(r, wide) for r, _ in outs],
            scratch_shapes=[pltpu.VMEM((keys, HD), bf16)] * 2
            + [pltpu.VMEM((keys, HD), f32)] * 2
            + [pltpu.VMEM((pieces * count, HD), f32)] * 2,
        ),
        out_shape=[jax.ShapeDtypeStruct(queries.shape, bf16)] * 2
        + [jax.ShapeDtypeStruct((r, wide), t) for r, t in outs],
        compiler_params=pltpu.CompilerParams(vmem_limit_bytes=56 * 2**20),
        name="attend",
    )(seen, queries, grads, cosine, sine, *blocks, *prompts)


def merge_kernel(d2_ref, r3_ref, dp_ref, x2_ref, *outs):
    rows = d2_ref.shape[0]
    x2_ref[...] = (d2_ref[...] + r3_ref[:rows, :]).astype(bf16)
    for j, out in enumerate(outs):
        step = out.shape[0]
        span = slice(j * step, (j + 1) * step)
        out[...] = dp_ref[span, :] + r3_ref[rows + j * step : rows + (j + 1) * step, :]


def merge(d2, r3, dp, pieces):
    rows, wide = d2.shape
    return pl.pallas_call(
        merge_kernel,
        out_shape=[jax.ShapeDtypeStruct((rows, wide), bf16)]
        + [jax.ShapeDtypeStruct((dp.shape[0] // pieces, wide), f32)] * pieces,
        name="merge",
    )(d2, r3, dp)


def finish_kernel(*refs, pieces):
    d0_ref, r1_ref, r2_ref, cos_ref, sin_ref, pcos_ref, psin_ref = refs[:7]
    terms = refs[7 : 7 + pieces]
    gk_ref, gv_ref, gpk_ref, gpv_ref = refs[7 + pieces :]
    rows = d0_ref.shape[0]
    cosine, sine = cos_ref[:rows, :], -sin_ref[:rows, :]
    pcos, psin = pcos_ref[...], -psin_ref[...]
    for h in range(KVH):
        at = slice(h * HD, (h + 1) * HD)
        vat = slice(WIDTH + h * HD, WIDTH + (h + 1) * HD)
        for cols, out in ((at, gk_ref), (vat, gv_ref)):
            total = d0_ref[:, cols] + (r1_ref[:, cols].astype(f32) + r2_ref[:, cols].astype(f32))
            out[:, at] = (turn(total, cosine, sine) if out is gk_ref else total).astype(bf16)
        for cols, out in ((at, gpk_ref), (vat, gpv_ref)):
            total = terms[0][:, cols]
            for term in terms[1:]:
                total = total + term[:, cols]
            out[:, at] = (turn(total, pcos, psin) if out is gpk_ref else total).astype(bf16)


def finish(d0, r1, r2, cosine, sine, pcos, psin, terms):
    rows = d0.shape[0]
    few = terms[0].shape[0]
    pieces = len(terms)

    def body(*refs):
        finish_kernel(*refs, pieces=pieces)

    return pl.pallas_call(
        body,
        out_shape=[jax.ShapeDtypeStruct((r, WIDTH), bf16) for r in (rows, rows, few, few)],
        name="finish",
    )(d0, r1, r2, cosine, sine, pcos, psin, *terms)


def local(
    queries, answer_keys, answer_values, prompt_keys, prompt_values, positions, ancestry, out_grad
):
    n = lax.axis_size("ctx")
    rows = queries.shape[0]
    me = lax.axis_index("ctx")
    core = me & 1
    swap = [(i, i ^ 1) for i in range(n)]
    ahead = [(i, i + 2) for i in range(n - 2)]
    across = [(i, i + 1) for i in range(0, n, 2)] + [(i, i + 3) for i in range(1, n - 3, 2)]
    rounds = [[(i, (i + 2 * k) % n) for i in range(n)] for k in range(1, n // 2)]

    mine = jnp.concatenate([prompt_keys, prompt_values], axis=1)
    chip = jnp.concatenate([mine, permute(mine, swap)], axis=0)
    own = jnp.concatenate([answer_keys, answer_values], axis=1)
    w2 = permute(own, ahead)
    w1 = permute(own, across)
    prompts = [chip] + [permute(chip, pairs) for pairs in rounds]
    w3 = permute(w2, swap)

    few = prompt_keys.shape[0]
    table = ancestry[0]
    column = jnp.arange(table.shape[0], dtype=jnp.int32)[None, :]
    steps = jnp.arange(SPAN, dtype=jnp.int32)
    steps = jnp.where((core == 0) & (steps > 0), SPAN - steps, steps)
    first = me - steps
    seen = jnp.sum(jnp.where(column == first[:, None], table[None, :], 0), axis=1)
    apart = jnp.sum(
        jnp.where((column >= first[:, None]) & (column < me), table[None, :], 0), axis=1
    )
    places = (positions[None, :] - rows * apart[:, None]).reshape(-1)
    chips = (me // 2 - jnp.arange(n // 2, dtype=jnp.int32)) % (n // 2)
    sides = jnp.stack([core, 1 - core])
    devices = 2 * chips[:, None] + sides[None, :]
    prompt_places = (devices[:, :, None] * few + jnp.arange(few, dtype=jnp.int32)).reshape(-1)
    cosine, sine = angle_tables(jnp.concatenate([places, prompt_places]))
    pcos, psin = cosine[SPAN * rows : SPAN * rows + few], sine[SPAN * rows : SPAN * rows + few]

    attended, grad_queries, d0, d1, d2, d3, dp = attend(
        seen[1:], queries, out_grad, cosine, sine, [own, w1, w2, w3], prompts
    )
    r3 = permute(d3, swap)
    r1 = permute(d1, back(across))
    x2, *terms = merge(d2, r3, dp, n // 2)
    r2 = permute(x2, back(ahead))
    terms = [terms[0]] + [permute(t, back(pairs)) for t, pairs in zip(terms[1:], rounds)]
    grad_keys, grad_values, grad_prompt_keys, grad_prompt_values = finish(
        d0, r1, r2, cosine, sine, pcos, psin, terms
    )
    return (attended, grad_queries, grad_keys, grad_values, grad_prompt_keys, grad_prompt_values)


def solution(mesh):
    rows = P(("groups", "ctx"), None)
    return jax.shard_map(
        local,
        mesh=mesh,
        in_specs=(rows, rows, rows, rows, rows, P(("groups", "ctx")), rows, rows),
        out_specs=(rows,) * 6,
        check_vma=False,
    )
```

time: 126 us -> 112 us (0.89); the launches traced: 123 us -> 112 us
  waiting for transfers between devices: 32.9 us -> 12.1 us
  starting transfers between devices: 33.5 us -> 41.3 us
  Pallas kernels: 37 us -> 43.3 us
  local copies, waits for them, and re-layouts: 11.6 us -> 9.22 us
  other arithmetic: 7.23 us -> 5.09 us
    ppermute x22 -> x21, waiting for transfers between devices: 32.9 us -> 12.1 us  [permute(): return lax.ppermute(value, 'ctx', pairs)]
    ppermute x22 -> x21, starting transfers between devices: 33.5 us -> 41.3 us  [permute(): return lax.ppermute(value, 'ctx', pairs)]
    pallas_call x1 -> x3, Pallas kernels: 37 us -> 43.3 us  [the longest x1 37.8 us: attend(): pl.pallas_call(body, grid_spec=pltpu.PrefetchScalarGridSpec(num_scalar_pr...]
    concatenate x1 -> x2, local copies, waits for them, and re-layouts: 4.83 us -> 1.67 us  [the longest x1 0.98 us: local(): own = jnp.concatenate([answer_keys, answer_values], axis=1)]
    convert_element_type x5 -> x0, other arithmetic: 2.95 us -> none  [the longest x1 1.37 us: local(): r2 = permute((d2 + r3.astype(f32)).astype(bf16), back(ahead))]
    mul x2 -> x4, other arithmetic: 0.71 us -> 3.27 us  [the longest x1 3.19 us: angle_tables(): return (jnp.cos(angles), jnp.sin(angles) * sign[None, :])]
    unnamed x25 -> x47, local copies, waits for them, and re-layouts: 2.31 us -> 4.37 us
    reshape x4 -> x0, local copies, waits for them, and re-layouts: 1.32 us -> none  [rotate(): split = values.astype(f32).reshape(rows, -1, HD)]
  transfers between devices with their start and end apart: 22 -> 21, of which waited for: 10 -> 5; matrix products, arithmetic and copies ran while one was open for 8% -> 9% of each run, Pallas kernels for 0% -> 2%
where the time goes in v2:
time: 112 us
  Pallas kernels  43.3 us (39%)
  starting transfers between devices  41.3 us (37%)
  waiting for transfers between devices  12.1 us (11%)
  local copies, waits for them, and re-layouts  9.22 us (8%)
  other arithmetic  5.09 us (5%)
    ppermute x21, starting transfers between devices, permute(): return lax.ppermute(value, 'ctx', pairs)  41.3 us
    pallas_call x1, Pallas kernels, attend(): pl.pallas_call(body, grid_spec=pltpu.PrefetchScalarGridSpec(num_scalar_pr...  37.8 us
    ppermute x21, waiting for transfers between devices, permute(): return lax.ppermute(value, 'ctx', pairs)  12.1 us
    unnamed x47, local copies, waits for them, and re-layouts  4.37 us
    mul x1, other arithmetic, angle_tables(): return (jnp.cos(angles), jnp.sin(angles) * sign[None, :])  3.19 us
    pallas_call x1, Pallas kernels, finish(): pl.pallas_call(body, out_shape=[jax.ShapeDtypeStruct((r, WIDTH), bf16) fo...  3.04 us
    pallas_call x1, Pallas kernels, merge(): pl.pallas_call(merge_kernel, out_shape=[jax.ShapeDtypeStruct((rows, wide)...  2.5 us
  transfers between devices with their start and end apart: 21, of which 5 were waited for; matrix products, arithmetic and copies ran while one was open for 9% of the time, Pallas kernels for 2%

profile of v2, /device:TPU:0, one launch (start us, length us, event | category | flops | bytes accessed | tf_op | source)
XLA Modules:
  0.0 112.0 jit_solution(17307522922847977889)
XLA Ops:
  2.6 4.9 %collective-permute-start.1 = (bf16[256,1024]{1,0:T(8,128)(2,1)S(1)}, bf16[256,1024]{1,0:T(8,128)(2,1)S(1)}, u32[]{:S(2)}, u32[]{:S(2)}) collective-permute-start(bf16[256,1024]{1,0:T(8,128)(2,1)S(1)} %constant_dynamic-update-slice_fusion.refs_5_), channel_id=1, source_target_pairs={{0,2},{1,3},{2,4},{3,5},{4,6},{5,7},{6,8},{7,9},{8,10},{9,11},{10,... | collective-permute-start | bytes 1572872 | tf_op jit(solution)/shard_map/ppermute | solution.py:25
  7.5 1.5 %collective-permute-start = (bf16[256,1024]{1,0:T(8,128)(2,1)S(1)}, bf16[256,1024]{1,0:T(8,128)(2,1)S(1)}, u32[]{:S(2)}, u32[]{:S(2)}) collective-permute-start(bf16[256,1024]{1,0:T(8,128)(2,1)S(1)} %constant_dynamic-update-slice_fusion.refs_5_), channel_id=1, source_target_pairs={{0,1},{2,3},{4,5},{6,7},{8,9},{10,11},{12,13},{14,15},{1,4},{3,6},... | collective-permute-start | bytes 1572872 | tf_op jit(solution)/shard_map/ppermute | solution.py:25
  10.4 2.1 %collective-permute-start.3 = (bf16[4,1024]{1,0:T(4,128)(2,1)S(1)}, bf16[4,1024]{1,0:T(4,128)(2,1)S(1)}, u32[]{:S(2)}, u32[]{:S(2)}) collective-permute-start(bf16[4,1024]{1,0:T(4,128)(2,1)S(1)} %constant_dynamic-update-slice_fusion.2), channel_id=1, source_target_pairs={{0,1},{1,0},{2,3},{3,2},{4,5},{5,4},{6,7},{7,6},{8,9},{9,8},{10,11... | collective-permute-start | bytes 24584 | tf_op jit(solution)/shard_map/ppermute | solution.py:25
  16.6 1.6 %collective-permute-start.5 = (bf16[8,1024]{1,0:T(8,128)(2,1)S(1)}, bf16[8,1024]{1,0:T(8,128)(2,1)S(1)}, u32[]{:S(2)}, u32[]{:S(2)}) collective-permute-start(bf16[8,1024]{1,0:T(8,128)(2,1)S(1)} %pad_maximum_fusion.refs_9_), channel_id=1, source_target_pairs={{0,4},{1,5},{2,6},{3,7},{4,8},{5,9},{6,10},{7,11},{8,12},{9,13},{1... | collective-permute-start | bytes 49160 | tf_op jit(solution)/shard_map/ppermute | solution.py:25
  18.3 3.5 %collective-permute-start.6 = (bf16[8,1024]{1,0:T(8,128)(2,1)S(1)}, bf16[8,1024]{1,0:T(8,128)(2,1)S(1)}, u32[]{:S(2)}, u32[]{:S(2)}) collective-permute-start(bf16[8,1024]{1,0:T(8,128)(2,1)S(1)} %pad_maximum_fusion.refs_9_), channel_id=1, source_target_pairs={{0,6},{1,7},{2,8},{3,9},{4,10},{5,11},{6,12},{7,13},{8,14},{9,15},... | collective-permute-start | bytes 49160 | tf_op jit(solution)/shard_map/ppermute | solution.py:25
  21.9 2.7 %collective-permute-start.7 = (bf16[8,1024]{1,0:T(8,128)(2,1)S(1)}, bf16[8,1024]{1,0:T(8,128)(2,1)S(1)}, u32[]{:S(2)}, u32[]{:S(2)}) collective-permute-start(bf16[8,1024]{1,0:T(8,128)(2,1)S(1)} %pad_maximum_fusion.refs_9_), channel_id=1, source_target_pairs={{0,8},{1,9},{2,10},{3,11},{4,12},{5,13},{6,14},{7,15},{8,0},{9,1},... | collective-permute-start | bytes 49160 | tf_op jit(solution)/shard_map/ppermute | solution.py:25
  24.6 1.9 %collective-permute-start.8 = (bf16[8,1024]{1,0:T(8,128)(2,1)S(1)}, bf16[8,1024]{1,0:T(8,128)(2,1)S(1)}, u32[]{:S(2)}, u32[]{:S(2)}) collective-permute-start(bf16[8,1024]{1,0:T(8,128)(2,1)S(1)} %pad_maximum_fusion.refs_9_), channel_id=1, source_target_pairs={{0,10},{1,11},{2,12},{3,13},{4,14},{5,15},{6,0},{7,1},{8,2},{9,3},... | collective-permute-start | bytes 49160 | tf_op jit(solution)/shard_map/ppermute | solution.py:25
  26.6 3.2 %collective-permute-start.9 = (bf16[8,1024]{1,0:T(8,128)(2,1)S(1)}, bf16[8,1024]{1,0:T(8,128)(2,1)S(1)}, u32[]{:S(2)}, u32[]{:S(2)}) collective-permute-start(bf16[8,1024]{1,0:T(8,128)(2,1)S(1)} %pad_maximum_fusion.refs_9_), channel_id=1, source_target_pairs={{0,12},{1,13},{2,14},{3,15},{4,0},{5,1},{6,2},{7,3},{8,4},{9,5},{1... | collective-permute-start | bytes 49160 | tf_op jit(solution)/shard_map/ppermute | solution.py:25
  29.7 3.2 %fusion = (f32[1088,128]{1,0:T(8,128)}, f32[1088,128]{1,0:T(8,128)}) fusion(f32[128]{0:T(128)S(1)} %get-tuple-element.50, f32[128]{0:T(128)S(1)} %get-tuple-element.51, f32[1088]{0:T(1024)S(1)} %add_convert_fusion), kind=kLoop, calls=%fused_computation.2 | loop fusion | flops 278528 | bytes 1119488 | tf_op jit(solution)/shard_map/mul | solution.py:37
  34.5 37.8 %attend.1 = (bf16[256,2560]{1,0:T(8,128)(2,1)}, bf16[256,2560]{1,0:T(8,128)(2,1)}, f32[256,1024]{1,0:T(8,128)}, bf16[256,1024]{1,0:T(8,128)(2,1)}, f32[256,1024]...) custom-call(s32[3]{0:T(128)} %slice.9.refs_0_, bf16[256,2560]{1,0:T(8,128)(2,1)} %refs_1_.1, ...), custom_call_target="tpu_custom_call" | custom-call | tf_op jit(solution)/shard_map/attend/pallas_call | solution.py:140
  72.3 1.3 %collective-permute-start.12 = (f32[288,1024]{1,0:T(8,128)}, f32[288,1024]{1,0:T(8,128)S(1)}, u32[]{:S(2)}, u32[]{:S(2)}) collective-permute-start(f32[288,1024]{1,0:T(8,128)} %get-tuple-element.31), channel_id=1, source_target_pairs={{0,1},{1,0},{2,3},{3,2},{4,5},{5,4},{6,7},{7,6},{8,9},{9,8},{10,11... | collective-permute-start | bytes 3538952 | tf_op jit(solution)/shard_map/ppermute | solution.py:25
  74.9 1.4 %collective-permute-done.12.r3_ref = f32[288,1024]{1,0:T(8,128)S(1)} collective-permute-done((f32[288,1024]{1,0:T(8,128)}, f32[288,1024]{1,0:T(8,128)S(1)}, u32[]{:S(2)}, u32[]{:S(2)}) %collective-permute-start.12) | collective-permute-done | bytes 1179680 | tf_op jit(solution)/shard_map/ppermute | solution.py:25
  77.3 2.5 %merge.1 = (bf16[256,1024]{1,0:T(8,128)(2,1)}, f32[4,1024]{1,0:T(4,128)}, f32[4,1024]{1,0:T(4,128)}, f32[4,1024]{1,0:T(4,128)}, f32[4,1024]{1,0:T(4,128)}, /*ind...) custom-call(f32[256,1024]{1,0:T(8,128)} %get-tuple-element.30.d2_ref, ...), custom_call_target="tpu_custom_call" | custom-call | tf_op jit(solution)/shard_map/merge/pallas_call | solution.py:171
  79.8 1.3 %collective-permute-start.13 = (bf16[256,1024]{1,0:T(8,128)(2,1)}, bf16[256,1024]{1,0:T(8,128)(2,1)S(1)}, u32[]{:S(2)}, u32[]{:S(2)}) collective-permute-start(bf16[256,1024]{1,0:T(8,128)(2,1)} %get-tuple-element.33), channel_id=1, source_target_pairs={{2,0},{3,1},{4,2},{5,3},{6,4},{7,5},{8,6},{9,7},{10,8},{11,9},{12,... | collective-permute-start | bytes 1572872 | tf_op jit(solution)/shard_map/ppermute | solution.py:25
  81.1 3.7 %collective-permute-start.14 = (f32[4,1024]{1,0:T(4,128)}, f32[4,1024]{1,0:T(4,128)S(1)}, u32[]{:S(2)}, u32[]{:S(2)}) collective-permute-start(f32[4,1024]{1,0:T(4,128)} %get-tuple-element.35), channel_id=1, source_target_pairs={{2,0},{3,1},{4,2},{5,3},{6,4},{7,5},{8,6},{9,7},{10,8},{11,9},{12,... | collective-permute-start | bytes 49160 | tf_op jit(solution)/shard_map/ppermute | solution.py:25
  84.8 1.3 %collective-permute-start.15 = (f32[4,1024]{1,0:T(4,128)}, f32[4,1024]{1,0:T(4,128)S(1)}, u32[]{:S(2)}, u32[]{:S(2)}) collective-permute-start(f32[4,1024]{1,0:T(4,128)} %get-tuple-element.36), channel_id=1, source_target_pairs={{4,0},{5,1},{6,2},{7,3},{8,4},{9,5},{10,6},{11,7},{12,8},{13,9},{1... | collective-permute-start | bytes 49160 | tf_op jit(solution)/shard_map/ppermute | solution.py:25
  86.1 1.7 %collective-permute-start.16 = (f32[4,1024]{1,0:T(4,128)}, f32[4,1024]{1,0:T(4,128)S(1)}, u32[]{:S(2)}, u32[]{:S(2)}) collective-permute-start(f32[4,1024]{1,0:T(4,128)} %get-tuple-element.37), channel_id=1, source_target_pairs={{6,0},{7,1},{8,2},{9,3},{10,4},{11,5},{12,6},{13,7},{14,8},{15,9},... | collective-permute-start | bytes 49160 | tf_op jit(solution)/shard_map/ppermute | solution.py:25
  87.8 2.6 %collective-permute-start.17 = (f32[4,1024]{1,0:T(4,128)}, f32[4,1024]{1,0:T(4,128)S(1)}, u32[]{:S(2)}, u32[]{:S(2)}) collective-permute-start(f32[4,1024]{1,0:T(4,128)} %get-tuple-element.38), channel_id=1, source_target_pairs={{8,0},{9,1},{10,2},{11,3},{12,4},{13,5},{14,6},{15,7},{0,8},{1,9},... | collective-permute-start | bytes 49160 | tf_op jit(solution)/shard_map/ppermute | solution.py:25
  90.4 6.4 %collective-permute-done.14.refs_8_ = f32[4,1024]{1,0:T(4,128)S(1)} collective-permute-done((f32[4,1024]{1,0:T(4,128)}, f32[4,1024]{1,0:T(4,128)S(1)}, u32[]{:S(2)}, u32[]{:S(2)}) %collective-permute-start.14) | collective-permute-done | bytes 16416 | tf_op jit(solution)/shard_map/ppermute | solution.py:25
  96.8 3.0 %collective-permute-start.18 = (f32[4,1024]{1,0:T(4,128)}, f32[4,1024]{1,0:T(4,128)S(1)}, u32[]{:S(2)}, u32[]{:S(2)}) collective-permute-start(f32[4,1024]{1,0:T(4,128)} %get-tuple-element.39), channel_id=1, source_target_pairs={{10,0},{11,1},{12,2},{13,3},{14,4},{15,5},{0,6},{1,7},{2,8},{3,9},... | collective-permute-start | bytes 49160 | tf_op jit(solution)/shard_map/ppermute | solution.py:25
  99.9 1.7 %collective-permute-start.19 = (f32[4,1024]{1,0:T(4,128)}, f32[4,1024]{1,0:T(4,128)S(1)}, u32[]{:S(2)}, u32[]{:S(2)}) collective-permute-start(f32[4,1024]{1,0:T(4,128)} %get-tuple-element.40), channel_id=1, source_target_pairs={{12,0},{13,1},{14,2},{15,3},{0,4},{1,5},{2,6},{3,7},{4,8},{5,9},{6... | collective-permute-start | bytes 49160 | tf_op jit(solution)/shard_map/ppermute | solution.py:25
  104.0 1.6 %collective-permute-done.19.refs_13_ = f32[4,1024]{1,0:T(4,128)S(1)} collective-permute-done((f32[4,1024]{1,0:T(4,128)}, f32[4,1024]{1,0:T(4,128)S(1)}, u32[]{:S(2)}, u32[]{:S(2)}) %collective-permute-start.19) | collective-permute-done | bytes 16416 | tf_op jit(solution)/shard_map/ppermute | solution.py:25
  105.6 2.6 %collective-permute-done.20.refs_14_ = f32[4,1024]{1,0:T(4,128)S(1)} collective-permute-done((f32[4,1024]{1,0:T(4,128)}, f32[4,1024]{1,0:T(4,128)S(1)}, u32[]{:S(2)}, u32[]{:S(2)}) %collective-permute-start.20) | collective-permute-done | bytes 16416 | tf_op jit(solution)/shard_map/ppermute | solution.py:25
  109.0 3.0 %finish.1 = (bf16[256,512]{1,0:T(8,128)(2,1)}, bf16[256,512]{1,0:T(8,128)(2,1)}, bf16[4,512]{1,0:T(4,128)(2,1)}, bf16[4,512]{1,0:T(4,128)(2,1)}) custom-call(f32[256,1024]{1,0:T(8,128)} %get-tuple-element.28.refs_0_, bf16[256,1024]{1,0:T(8,128)(2,1)} %copy-done.4, bf16[256,1024]{1,0:T(8,128)(2,1)} %copy-done.5, f32[1088,128]{1,0:T(8,128)} %get-tuple-element.49.refs_3_, ...), custom_call_target="tpu_custom_call" | custom-call | tf_op jit(solution)/shard_map/finish/pallas_call | solution.py:207
  (87 shorter events, 14.7 us)
Async XLA Ops:
  2.6 31.0 %copy-start = (bf16[256,1024]{1,0:T(8,128)(2,1)}, bf16[256,1024]{1,0:T(8,128)(2,1)S(1)}, u32[]{:S(2)}) copy-start(bf16[256,1024]{1,0:T(8,128)(2,1)S(1)} %constant_dynamic-update-slice_fusion.refs_5_) | copy-start | bytes 1572868
  2.6 19.3 %collective-permute-start.1 = (bf16[256,1024]{1,0:T(8,128)(2,1)S(1)}, bf16[256,1024]{1,0:T(8,128)(2,1)S(1)}, u32[]{:S(2)}, u32[]{:S(2)}) collective-permute-start(bf16[256,1024]{1,0:T(8,128)(2,1)S(1)} %constant_dynamic-update-slice_fusion.refs_5_), channel_id=1, source_target_pairs={{0,2},{1,3},{2,4},{3,5},{4,6},{5,7},{6,8},{7,9},{8,10},{9,11},{10,... | collective-permute-start | bytes 1572872 | tf_op jit(solution)/shard_map/ppermute | solution.py:25
  7.5 26.0 %collective-permute-start = (bf16[256,1024]{1,0:T(8,128)(2,1)S(1)}, bf16[256,1024]{1,0:T(8,128)(2,1)S(1)}, u32[]{:S(2)}, u32[]{:S(2)}) collective-permute-start(bf16[256,1024]{1,0:T(8,128)(2,1)S(1)} %constant_dynamic-update-slice_fusion.refs_5_), channel_id=1, source_target_pairs={{0,1},{2,3},{4,5},{6,7},{8,9},{10,11},{12,13},{14,15},{1,4},{3,6},... | collective-permute-start | bytes 1572872 | tf_op jit(solution)/shard_map/ppermute | solution.py:25
  10.4 4.1 %collective-permute-start.3 = (bf16[4,1024]{1,0:T(4,128)(2,1)S(1)}, bf16[4,1024]{1,0:T(4,128)(2,1)S(1)}, u32[]{:S(2)}, u32[]{:S(2)}) collective-permute-start(bf16[4,1024]{1,0:T(4,128)(2,1)S(1)} %constant_dynamic-update-slice_fusion.2), channel_id=1, source_target_pairs={{0,1},{1,0},{2,3},{3,2},{4,5},{5,4},{6,7},{7,6},{8,9},{9,8},{10,11... | collective-permute-start | bytes 24584 | tf_op jit(solution)/shard_map/ppermute | solution.py:25
  14.5 19.1 %copy-start.7 = (bf16[8,1024]{1,0:T(8,128)(2,1)}, bf16[8,1024]{1,0:T(8,128)(2,1)S(1)}, u32[]{:S(2)}) copy-start(bf16[8,1024]{1,0:T(8,128)(2,1)S(1)} %pad_maximum_fusion.refs_9_) | copy-start | bytes 49156
  14.5 3.8 %collective-permute-start.10 = (bf16[8,1024]{1,0:T(8,128)(2,1)S(1)}, bf16[8,1024]{1,0:T(8,128)(2,1)S(1)}, u32[]{:S(2)}, u32[]{:S(2)}) collective-permute-start(bf16[8,1024]{1,0:T(8,128)(2,1)S(1)} %pad_maximum_fusion.refs_9_), channel_id=1, source_target_pairs={{0,14},{1,15},{2,0},{3,1},{4,2},{5,3},{6,4},{7,5},{8,6},{9,7},{10,... | collective-permute-start | bytes 49160 | tf_op jit(solution)/shard_map/ppermute | solution.py:25
  15.3 6.5 %collective-permute-start.4 = (bf16[8,1024]{1,0:T(8,128)(2,1)S(1)}, bf16[8,1024]{1,0:T(8,128)(2,1)S(1)}, u32[]{:S(2)}, u32[]{:S(2)}) collective-permute-start(bf16[8,1024]{1,0:T(8,128)(2,1)S(1)} %pad_maximum_fusion.refs_9_), channel_id=1, source_target_pairs={{0,2},{1,3},{2,4},{3,5},{4,6},{5,7},{6,8},{7,9},{8,10},{9,11},{10,... | collective-permute-start | bytes 49160 | tf_op jit(solution)/shard_map/ppermute | solution.py:25
  16.6 8.0 %collective-permute-start.5 = (bf16[8,1024]{1,0:T(8,128)(2,1)S(1)}, bf16[8,1024]{1,0:T(8,128)(2,1)S(1)}, u32[]{:S(2)}, u32[]{:S(2)}) collective-permute-start(bf16[8,1024]{1,0:T(8,128)(2,1)S(1)} %pad_maximum_fusion.refs_9_), channel_id=1, source_target_pairs={{0,4},{1,5},{2,6},{3,7},{4,8},{5,9},{6,10},{7,11},{8,12},{9,13},{1... | collective-permute-start | bytes 49160 | tf_op jit(solution)/shard_map/ppermute | solution.py:25
  18.3 8.2 %collective-permute-start.6 = (bf16[8,1024]{1,0:T(8,128)(2,1)S(1)}, bf16[8,1024]{1,0:T(8,128)(2,1)S(1)}, u32[]{:S(2)}, u32[]{:S(2)}) collective-permute-start(bf16[8,1024]{1,0:T(8,128)(2,1)S(1)} %pad_maximum_fusion.refs_9_), channel_id=1, source_target_pairs={{0,6},{1,7},{2,8},{3,9},{4,10},{5,11},{6,12},{7,13},{8,14},{9,15},... | collective-permute-start | bytes 49160 | tf_op jit(solution)/shard_map/ppermute | solution.py:25
  21.9 11.7 %collective-permute-start.2 = (bf16[256,1024]{1,0:T(8,128)(2,1)S(1)}, bf16[256,1024]{1,0:T(8,128)(2,1)S(1)}, u32[]{:S(2)}, u32[]{:S(2)}) collective-permute-start(bf16[256,1024]{1,0:T(8,128)(2,1)S(1)} %collective-permute-done.1.refs_7_), channel_id=1, source_target_pairs={{0,1},{1,0},{2,3},{3,2},{4,5},{5,4},{6,7},{7,6},{8,9},{9,8},{10,11... | collective-permute-start | bytes 1572872 | tf_op jit(solution)/shard_map/ppermute | solution.py:25
  21.9 11.6 %collective-permute-start.7 = (bf16[8,1024]{1,0:T(8,128)(2,1)S(1)}, bf16[8,1024]{1,0:T(8,128)(2,1)S(1)}, u32[]{:S(2)}, u32[]{:S(2)}) collective-permute-start(bf16[8,1024]{1,0:T(8,128)(2,1)S(1)} %pad_maximum_fusion.refs_9_), channel_id=1, source_target_pairs={{0,8},{1,9},{2,10},{3,11},{4,12},{5,13},{6,14},{7,15},{8,0},{9,1},... | collective-permute-start | bytes 49160 | tf_op jit(solution)/shard_map/ppermute | solution.py:25
  24.6 8.9 %collective-permute-start.8 = (bf16[8,1024]{1,0:T(8,128)(2,1)S(1)}, bf16[8,1024]{1,0:T(8,128)(2,1)S(1)}, u32[]{:S(2)}, u32[]{:S(2)}) collective-permute-start(bf16[8,1024]{1,0:T(8,128)(2,1)S(1)} %pad_maximum_fusion.refs_9_), channel_id=1, source_target_pairs={{0,10},{1,11},{2,12},{3,13},{4,14},{5,15},{6,0},{7,1},{8,2},{9,3},... | collective-permute-start | bytes 49160 | tf_op jit(solution)/shard_map/ppermute | solution.py:25
  26.6 7.0 %collective-permute-start.9 = (bf16[8,1024]{1,0:T(8,128)(2,1)S(1)}, bf16[8,1024]{1,0:T(8,128)(2,1)S(1)}, u32[]{:S(2)}, u32[]{:S(2)}) collective-permute-start(bf16[8,1024]{1,0:T(8,128)(2,1)S(1)} %pad_maximum_fusion.refs_9_), channel_id=1, source_target_pairs={{0,12},{1,13},{2,14},{3,15},{4,0},{5,1},{6,2},{7,3},{8,4},{9,5},{1... | collective-permute-start | bytes 49160 | tf_op jit(solution)/shard_map/ppermute | solution.py:25
  72.3 4.0 %collective-permute-start.12 = (f32[288,1024]{1,0:T(8,128)}, f32[288,1024]{1,0:T(8,128)S(1)}, u32[]{:S(2)}, u32[]{:S(2)}) collective-permute-start(f32[288,1024]{1,0:T(8,128)} %get-tuple-element.31), channel_id=1, source_target_pairs={{0,1},{1,0},{2,3},{3,2},{4,5},{5,4},{6,7},{7,6},{8,9},{9,8},{10,11... | collective-permute-start | bytes 3538952 | tf_op jit(solution)/shard_map/ppermute | solution.py:25
  73.6 14.2 %collective-permute-start.11 = (bf16[256,1024]{1,0:T(8,128)(2,1)}, bf16[256,1024]{1,0:T(8,128)(2,1)S(1)}, u32[]{:S(2)}, u32[]{:S(2)}) collective-permute-start(bf16[256,1024]{1,0:T(8,128)(2,1)} %get-tuple-element.29), channel_id=1, source_target_pairs={{1,0},{3,2},{5,4},{7,6},{9,8},{11,10},{13,12},{15,14},{4,1},{6,3},... | collective-permute-start | bytes 1572872 | tf_op jit(solution)/shard_map/ppermute | solution.py:25
  79.8 28.4 %collective-permute-start.13 = (bf16[256,1024]{1,0:T(8,128)(2,1)}, bf16[256,1024]{1,0:T(8,128)(2,1)S(1)}, u32[]{:S(2)}, u32[]{:S(2)}) collective-permute-start(bf16[256,1024]{1,0:T(8,128)(2,1)} %get-tuple-element.33), channel_id=1, source_target_pairs={{2,0},{3,1},{4,2},{5,3},{6,4},{7,5},{8,6},{9,7},{10,8},{11,9},{12,... | collective-permute-start | bytes 1572872 | tf_op jit(solution)/shard_map/ppermute | solution.py:25
  81.1 15.7 %collective-permute-start.14 = (f32[4,1024]{1,0:T(4,128)}, f32[4,1024]{1,0:T(4,128)S(1)}, u32[]{:S(2)}, u32[]{:S(2)}) collective-permute-start(f32[4,1024]{1,0:T(4,128)} %get-tuple-element.35), channel_id=1, source_target_pairs={{2,0},{3,1},{4,2},{5,3},{6,4},{7,5},{8,6},{9,7},{10,8},{11,9},{12,... | collective-permute-start | bytes 49160 | tf_op jit(solution)/shard_map/ppermute | solution.py:25
  84.8 15.1 %collective-permute-start.15 = (f32[4,1024]{1,0:T(4,128)}, f32[4,1024]{1,0:T(4,128)S(1)}, u32[]{:S(2)}, u32[]{:S(2)}) collective-permute-start(f32[4,1024]{1,0:T(4,128)} %get-tuple-element.36), channel_id=1, source_target_pairs={{4,0},{5,1},{6,2},{7,3},{8,4},{9,5},{10,6},{11,7},{12,8},{13,9},{1... | collective-permute-start | bytes 49160 | tf_op jit(solution)/shard_map/ppermute | solution.py:25
  86.1 15.4 %collective-permute-start.16 = (f32[4,1024]{1,0:T(4,128)}, f32[4,1024]{1,0:T(4,128)S(1)}, u32[]{:S(2)}, u32[]{:S(2)}) collective-permute-start(f32[4,1024]{1,0:T(4,128)} %get-tuple-element.37), channel_id=1, source_target_pairs={{6,0},{7,1},{8,2},{9,3},{10,4},{11,5},{12,6},{13,7},{14,8},{15,9},... | collective-permute-start | bytes 49160 | tf_op jit(solution)/shard_map/ppermute | solution.py:25
  87.8 20.4 %copy-start.4 = (bf16[256,1024]{1,0:T(8,128)(2,1)}, bf16[256,1024]{1,0:T(8,128)(2,1)S(1)}, u32[]{:S(2)}) copy-start(bf16[256,1024]{1,0:T(8,128)(2,1)S(1)} %collective-permute-done.11.refs_1_) | copy-start | bytes 1572868
  87.8 16.2 %collective-permute-start.17 = (f32[4,1024]{1,0:T(4,128)}, f32[4,1024]{1,0:T(4,128)S(1)}, u32[]{:S(2)}, u32[]{:S(2)}) collective-permute-start(f32[4,1024]{1,0:T(4,128)} %get-tuple-element.38), channel_id=1, source_target_pairs={{8,0},{9,1},{10,2},{11,3},{12,4},{13,5},{14,6},{15,7},{0,8},{1,9},... | collective-permute-start | bytes 49160 | tf_op jit(solution)/shard_map/ppermute | solution.py:25
  96.8 7.2 %collective-permute-start.18 = (f32[4,1024]{1,0:T(4,128)}, f32[4,1024]{1,0:T(4,128)S(1)}, u32[]{:S(2)}, u32[]{:S(2)}) collective-permute-start(f32[4,1024]{1,0:T(4,128)} %get-tuple-element.39), channel_id=1, source_target_pairs={{10,0},{11,1},{12,2},{13,3},{14,4},{15,5},{0,6},{1,7},{2,8},{3,9},... | collective-permute-start | bytes 49160 | tf_op jit(solution)/shard_map/ppermute | solution.py:25
  99.9 5.7 %collective-permute-start.19 = (f32[4,1024]{1,0:T(4,128)}, f32[4,1024]{1,0:T(4,128)S(1)}, u32[]{:S(2)}, u32[]{:S(2)}) collective-permute-start(f32[4,1024]{1,0:T(4,128)} %get-tuple-element.40), channel_id=1, source_target_pairs={{12,0},{13,1},{14,2},{15,3},{0,4},{1,5},{2,6},{3,7},{4,8},{5,9},{6... | collective-permute-start | bytes 49160 | tf_op jit(solution)/shard_map/ppermute | solution.py:25
  101.5 6.6 %collective-permute-start.20 = (f32[4,1024]{1,0:T(4,128)}, f32[4,1024]{1,0:T(4,128)S(1)}, u32[]{:S(2)}, u32[]{:S(2)}) collective-permute-start(f32[4,1024]{1,0:T(4,128)} %get-tuple-element.41), channel_id=1, source_target_pairs={{14,0},{15,1},{0,2},{1,3},{2,4},{3,5},{4,6},{5,7},{6,8},{7,9},{8,1... | collective-permute-start | bytes 49160 | tf_op jit(solution)/shard_map/ppermute | solution.py:25
  (19 other events, 98.2 us)

commit v3 on v2

v3 whole, which is shorter than its diff:
```python
import jax
import jax.numpy as jnp
from jax import lax
from jax.experimental import pallas as pl
from jax.experimental.pallas import tpu as pltpu
from jax.sharding import PartitionSpec as P

QH = 20
KVH = 4
GROUP = QH // KVH
HD = 128
WIDTH = KVH * HD
SPAN = 4
SCALE = HD**-0.5
LOG2E = 1.4426950408889634
HIDDEN = -1e30

rope_base = 1000000.0

f32 = jnp.float32
bf16 = jnp.bfloat16


def permute(value, pairs):
    return lax.ppermute(value, "ctx", pairs)


def back(pairs):
    return [(b, a) for a, b in pairs]


def angle_tables(places):
    lane = jnp.arange(HD, dtype=jnp.int32)
    freqs = rope_base ** (-(2.0 * (lane % (HD // 2)).astype(f32)) / HD)
    angles = places.astype(f32)[:, None] * freqs[None, :]
    sign = jnp.where(lane < HD // 2, -1.0, 1.0).astype(f32)
    return jnp.cos(angles), jnp.sin(angles) * sign[None, :]


def dot(a, b, ca, cb):
    return lax.dot_general(a, b, (((ca,), (cb,)), ((), ())), preferred_element_type=f32)


def turn(x, cosine, sine):
    return x * cosine + pltpu.roll(x, HD // 2, 1) * sine


IN_VMEM = pl.BlockSpec(memory_space=pltpu.VMEM)


def stack(a, b):
    return jnp.concatenate([a, b], axis=0)


def pack_kernel(k_ref, v_ref, pk_ref, pv_ref, own_ref, mine_ref):
    own_ref[:, :WIDTH] = k_ref[...]
    own_ref[:, WIDTH:] = v_ref[...]
    mine_ref[:, :WIDTH] = pk_ref[...]
    mine_ref[:, WIDTH:] = pv_ref[...]


def pack(keys, values, prompt_keys, prompt_values):
    return pl.pallas_call(
        pack_kernel,
        out_shape=[
            jax.ShapeDtypeStruct((keys.shape[0], 2 * WIDTH), bf16),
            jax.ShapeDtypeStruct((prompt_keys.shape[0], 2 * WIDTH), bf16),
        ],
        out_specs=[IN_VMEM, IN_VMEM],
        name="pack",
    )(keys, values, prompt_keys, prompt_values)


def attend_kernel(
    seen, q_ref, g_ref, cos_ref, sin_ref, own_ref, w1_ref, w2_ref, w3_ref, pa_ref, pb_ref,
    o_ref, dq_ref, d0_ref, d1_ref, d2_ref, d3_ref, dp_ref,
    k_buf, v_buf, dk_buf, dv_buf, p_buf,
):
    rows = q_ref.shape[0]
    half = pa_ref.shape[0]
    core = seen[3]
    col = pl.program_id(0) * HD
    k_at = pl.ds(pl.multiple_of(col, HD), HD)
    v_at = pl.ds(pl.multiple_of(col + WIDTH, HD), HD)
    for j, part in enumerate((own_ref, w1_ref, w2_ref, w3_ref)):
        span = slice(j * rows, (j + 1) * rows)
        raw = part[:, k_at].astype(f32)
        k_buf[span, :] = turn(raw, cos_ref[span, :], sin_ref[span, :]).astype(bf16)
        v_buf[span, :] = part[:, v_at]
    mine = pl.ds(pl.multiple_of(core * half, half), half)
    other = pl.ds(pl.multiple_of((1 - core) * half, half), half)
    span = slice(SPAN * rows, SPAN * rows + 2 * half)
    p_buf[mine, :] = pa_ref[:, k_at].astype(f32)
    p_buf[other, :] = pb_ref[:, k_at].astype(f32)
    k_buf[span, :] = turn(p_buf[...], cos_ref[span, :], sin_ref[span, :]).astype(bf16)
    p_buf[mine, :] = pa_ref[:, v_at].astype(f32)
    p_buf[other, :] = pb_ref[:, v_at].astype(f32)
    v_buf[span, :] = p_buf[...].astype(bf16)
    k, v = k_buf[...], v_buf[...]
    cosine, sine = cos_ref[:rows, :], sin_ref[:rows, :]
    lower = lax.broadcasted_iota(jnp.int32, (rows, rows), 1) <= lax.broadcasted_iota(
        jnp.int32, (rows, rows), 0
    )
    bias = [jnp.where(seen[i] > 0, 0.0, HIDDEN).astype(f32) for i in range(3)]

    def cols(h):
        return slice(h * HD, (h + 1) * HD)

    def open_head(h):
        q = turn(q_ref[:, cols(h)].astype(f32), cosine, sine).astype(bf16)
        g = g_ref[:, cols(h)]
        return q, g, dot(q, k, 1, 1), dot(g, v, 1, 1)

    def weigh(s):
        s_own = jnp.where(lower, s[:, :rows], HIDDEN)
        s_win = [s[:, rows * (i + 1) : rows * (i + 2)] for i in range(3)]
        s_pr = s[:, SPAN * rows :]
        peak = jnp.maximum(
            jnp.max(s_own, axis=1, keepdims=True), jnp.max(s_pr, axis=1, keepdims=True)
        )
        for i in range(3):
            peak = jnp.maximum(peak, jnp.max(s_win[i], axis=1, keepdims=True) + bias[i])
        base = peak * (SCALE * LOG2E)
        e = (
            [jnp.exp2(s_own * (SCALE * LOG2E) - base)]
            + [jnp.exp2(s_win[i] * (SCALE * LOG2E) - (base - bias[i])) for i in range(3)]
            + [jnp.exp2(s_pr * (SCALE * LOG2E) - base)]
        )
        total = sum(jnp.sum(x, axis=1, keepdims=True) for x in e)
        return jnp.concatenate(e, axis=1) * (1.0 / total)

    def close_head(h, ds, wb, q, g):
        dq_ref[:, cols(h)] = turn(dot(ds, k, 1, 0), cosine, -sine).astype(bf16)
        dk, dv = dot(ds, q, 0, 0), dot(wb, g, 0, 0)
        if h == 0:
            dk_buf[...] = dk
            dv_buf[...] = dv
        else:
            dk_buf[...] += dk
            dv_buf[...] += dv

    ahead, behind = open_head(0), None
    for h in range(GROUP):
        q, g, s, dw = ahead
        if h + 1 < GROUP:
            ahead = open_head(h + 1)
        if behind is not None:
            close_head(*behind)
        w = weigh(s)
        wb = w.astype(bf16)
        o = dot(wb, v, 1, 0).astype(bf16)
        o_ref[:, cols(h)] = o
        delta = jnp.sum(o.astype(f32) * g.astype(f32), axis=1, keepdims=True)
        behind = (h, (w * (dw - delta) * SCALE).astype(bf16), wb, q, g)
    close_head(*behind)

    start = SPAN * rows
    for at, buf in ((k_at, dk_buf), (v_at, dv_buf)):
        for j, out in enumerate((d0_ref, d1_ref, d2_ref, d3_ref)):
            out[:rows, at] = buf[j * rows : (j + 1) * rows, :].astype(out.dtype)
        dp_ref[:, at] = buf[pl.ds(pl.multiple_of(start + core * half, 8), half), :]
        d3_ref[rows:, at] = buf[pl.ds(pl.multiple_of(start + (1 - core) * half, 8), half), :]


def attend(seen, queries, grads, cosine, sine, blocks, prompts):
    rows = queries.shape[0]
    wide = blocks[0].shape[1]
    half = prompts[0].shape[0]
    keys = SPAN * rows + 2 * half
    head = pl.BlockSpec((rows, GROUP * HD), lambda i, s: (0, i))
    outs = [(rows, f32), (rows, bf16), (rows, f32), (rows + half, f32), (half, f32)]
    return pl.pallas_call(
        attend_kernel,
        grid_spec=pltpu.PrefetchScalarGridSpec(
            num_scalar_prefetch=1,
            grid=(KVH,),
            in_specs=[head, head] + [IN_VMEM] * 8,
            out_specs=[head, head] + [IN_VMEM] * 5,
            scratch_shapes=[pltpu.VMEM((keys, HD), bf16)] * 2
            + [pltpu.VMEM((keys, HD), f32)] * 2
            + [pltpu.VMEM((2 * half, HD), f32)],
        ),
        out_shape=[jax.ShapeDtypeStruct(queries.shape, bf16)] * 2
        + [jax.ShapeDtypeStruct((r, wide), t) for r, t in outs],
        compiler_params=pltpu.CompilerParams(vmem_limit_bytes=40 * 2**20),
        name="attend",
    )(seen, queries, grads, cosine, sine, *blocks, *prompts)


def merge_kernel(d2_ref, r3_ref, dp_ref, x2_ref, *outs):
    rows = d2_ref.shape[0]
    x2_ref[...] = (d2_ref[...] + r3_ref[:rows, :]).astype(bf16)
    for j, out in enumerate(outs):
        step = out.shape[0]
        span = slice(j * step, (j + 1) * step)
        out[...] = dp_ref[span, :] + r3_ref[rows + j * step : rows + (j + 1) * step, :]


def merge(d2, r3, dp, pieces):
    rows, wide = d2.shape
    return pl.pallas_call(
        merge_kernel,
        in_specs=[IN_VMEM] * 3,
        out_specs=[IN_VMEM] * (1 + pieces),
        out_shape=[jax.ShapeDtypeStruct((rows, wide), bf16)]
        + [jax.ShapeDtypeStruct((dp.shape[0] // pieces, wide), f32)] * pieces,
        name="merge",
    )(d2, r3, dp)


def tally_kernel(core_ref, *refs):
    terms, keep_ref, send_ref = refs[:-2], refs[-2], refs[-1]
    few = keep_ref.shape[0]
    total = terms[0][...]
    for term in terms[1:]:
        total = total + term[...]
    first = core_ref[0] == 0
    keep_ref[...] = jnp.where(first, total[:few], total[few:])
    send_ref[...] = jnp.where(first, total[few:], total[:few])


def tally(core, terms):
    few, wide = terms[0].shape
    return pl.pallas_call(
        tally_kernel,
        in_specs=[pl.BlockSpec(memory_space=pltpu.SMEM)] + [IN_VMEM] * len(terms),
        out_specs=[IN_VMEM] * 2,
        out_shape=[jax.ShapeDtypeStruct((few // 2, wide), f32)] * 2,
        name="tally",
    )(core, *terms)


def finish_kernel(
    d0_ref, r1_ref, r2_ref, cos_ref, sin_ref, pcos_ref, psin_ref, keep_ref, got_ref,
    gk_ref, gv_ref, gpk_ref, gpv_ref,
):
    rows = d0_ref.shape[0]
    cosine, sine = cos_ref[:rows, :], -sin_ref[:rows, :]
    pcos, psin = pcos_ref[...], -psin_ref[...]
    for h in range(KVH):
        at = slice(h * HD, (h + 1) * HD)
        vat = slice(WIDTH + h * HD, WIDTH + (h + 1) * HD)
        for cols, out in ((at, gk_ref), (vat, gv_ref)):
            total = d0_ref[:, cols] + (r1_ref[:, cols].astype(f32) + r2_ref[:, cols].astype(f32))
            out[:, at] = (turn(total, cosine, sine) if out is gk_ref else total).astype(bf16)
        for cols, out in ((at, gpk_ref), (vat, gpv_ref)):
            total = keep_ref[:, cols] + got_ref[:, cols]
            out[:, at] = (turn(total, pcos, psin) if out is gpk_ref else total).astype(bf16)


def finish(d0, r1, r2, cosine, sine, pcos, psin, keep, got):
    rows, few = d0.shape[0], keep.shape[0]
    return pl.pallas_call(
        finish_kernel,
        in_specs=[IN_VMEM] * 9,
        out_shape=[jax.ShapeDtypeStruct((r, WIDTH), bf16) for r in (rows, rows, few, few)],
        name="finish",
    )(d0, r1, r2, cosine, sine, pcos, psin, keep, got)


def local(
    queries, answer_keys, answer_values, prompt_keys, prompt_values, positions, ancestry, out_grad
):
    n = lax.axis_size("ctx")
    chips = n // 2
    rows = queries.shape[0]
    few = prompt_keys.shape[0]
    me = lax.axis_index("ctx")
    core = me & 1
    swap = [(i, i ^ 1) for i in range(n)]
    ahead = [(i, i + 2) for i in range(n - 2)]
    across = [(i, i + 1) for i in range(0, n, 2)] + [(i, i + 3) for i in range(1, n - 3, 2)]
    reach = [[j, (j + chips // 2) % chips] for j in range(1, chips // 2 + 1)]
    rounds = [[(i, (i + 2 * k[i % 2]) % n) for i in range(n)] for k in reach]

    own, mine = pack(answer_keys, answer_values, prompt_keys, prompt_values)
    w2 = permute(own, ahead)
    w1 = permute(own, across)
    theirs = permute(mine, swap)
    chip = jnp.where(core == 0, stack(mine, theirs), stack(theirs, mine))
    near = jnp.concatenate([permute(chip, pairs) for pairs in rounds], axis=0)
    w3 = permute(w2, swap)
    far = permute(near, swap)

    table = ancestry[0]
    column = jnp.arange(table.shape[0], dtype=jnp.int32)[None, :]
    steps = jnp.arange(SPAN, dtype=jnp.int32)
    steps = jnp.where((core == 0) & (steps > 0), SPAN - steps, steps)
    first = me - steps
    seen = jnp.sum(jnp.where(column == first[:, None], table[None, :], 0), axis=1)
    apart = jnp.sum(
        jnp.where((column >= first[:, None]) & (column < me), table[None, :], 0), axis=1
    )
    places = (positions[None, :] - rows * apart[:, None]).reshape(-1)
    away = jnp.array([k[0] for k in reach] + [k[1] for k in reach], dtype=jnp.int32)
    homes = (me // 2 - away + chips) % chips
    prompt_places = homes[:, None] * (2 * few) + jnp.arange(2 * few, dtype=jnp.int32)
    cosine, sine = angle_tables(jnp.concatenate([places, prompt_places.reshape(-1)]))
    pcos, psin = angle_tables(me * few + jnp.arange(few, dtype=jnp.int32))
    scalars = jnp.concatenate([seen[1:], core[None]]).astype(jnp.int32)

    attended, grad_queries, d0, d1, d2, d3, dp = attend(
        scalars, queries, out_grad, cosine, sine, [own, w1, w2, w3], [near, far]
    )
    r3 = permute(d3, swap)
    r1 = permute(d1, back(across))
    x2, *terms = merge(d2, r3, dp, chips // 2)
    r2 = permute(x2, back(ahead))
    keep, send = tally(
        core[None].astype(jnp.int32), [permute(t, back(p)) for t, p in zip(terms, rounds)]
    )
    got = permute(send, swap)
    grad_keys, grad_values, grad_prompt_keys, grad_prompt_values = finish(
        d0, r1, r2, cosine, sine, pcos, psin, keep, got
    )
    return (attended, grad_queries, grad_keys, grad_values, grad_prompt_keys, grad_prompt_values)


def solution(mesh):
    rows = P(("groups", "ctx"), None)
    return jax.shard_map(
        local,
        mesh=mesh,
        in_specs=(rows, rows, rows, rows, rows, P(("groups", "ctx")), rows, rows),
        out_specs=(rows,) * 6,
        check_vma=False,
    )
```

time: 112 us -> 100 us (0.89)
  starting transfers between devices: 41.3 us -> 33 us
  Pallas kernels: 43.3 us -> 36.3 us
  waiting for transfers between devices: 12.1 us -> 16.7 us
  local copies, waits for them, and re-layouts: 9.22 us -> 6.58 us
    ppermute x21 -> x17, starting transfers between devices: 41.3 us -> 33 us  [permute(): return lax.ppermute(value, 'ctx', pairs)]
    pallas_call x3 -> x5, Pallas kernels: 43.3 us -> 36.3 us  [the longest x1 27.4 us: attend(): pl.pallas_call(attend_kernel, grid_spec=pltpu.PrefetchScalarGridSpec(num_...]
    ppermute x21 -> x17, waiting for transfers between devices: 12.1 us -> 16.7 us  [permute(): return lax.ppermute(value, 'ctx', pairs)]
    slice x3 -> x1, local copies, waits for them, and re-layouts: 3.08 us -> 0.07 us  [local(): scalars = jnp.concatenate([seen[1:], core[None]]).astype(jnp.int32)]
    unnamed x47 -> x36, local copies, waits for them, and re-layouts: 4.37 us -> 6.42 us
    concatenate x2 -> x1, local copies, waits for them, and re-layouts: 1.67 us -> 0.01 us  [local(): near = jnp.concatenate([permute(chip, pairs) for pairs in rounds], axis=0)]
    mul x1 -> x2, other arithmetic: 3.19 us -> 2.71 us  [angle_tables(): return (jnp.cos(angles), jnp.sin(angles) * sign[None, :])]
  transfers between devices with their start and end apart: 21 -> 17, of which waited for: 5 -> 7; matrix products, arithmetic and copies ran while one was open for 9% -> 6% of each run, Pallas kernels for 2% -> 4%
where the time goes in v3:
time: 100 us; the launch traced here: 99.5 us
  Pallas kernels  36.3 us (36%)
  starting transfers between devices  33 us (33%)
  waiting for transfers between devices  16.7 us (17%)
  local copies, waits for them, and re-layouts  6.58 us (7%)
  other arithmetic  5.98 us (6%)
    ppermute x17, starting transfers between devices, permute(): return lax.ppermute(value, 'ctx', pairs)  33 us
    pallas_call x1, Pallas kernels, attend(): pl.pallas_call(attend_kernel, grid_spec=pltpu.PrefetchScalarGridSpec(num_...  27.4 us
    ppermute x17, waiting for transfers between devices, permute(): return lax.ppermute(value, 'ctx', pairs)  16.7 us
    unnamed x36, local copies, waits for them, and re-layouts  6.42 us
    pallas_call x1, Pallas kernels, finish(): pl.pallas_call(finish_kernel, in_specs=[IN_VMEM] * 9, out_shape=[jax.Shap...  2.99 us
    mul x2, other arithmetic, angle_tables(): return (jnp.cos(angles), jnp.sin(angles) * sign[None, :])  2.71 us
    pallas_call x1, Pallas kernels, merge(): pl.pallas_call(merge_kernel, in_specs=[IN_VMEM] * 3, out_specs=[IN_VMEM]...  2.51 us
  transfers between devices with their start and end apart: 17, of which 7 were waited for; matrix products, arithmetic and copies ran while one was open for 6% of the time, Pallas kernels for 4%

profile of v3, /device:TPU:0, one launch (start us, length us, event | category | flops | bytes accessed | tf_op | source)
XLA Modules:
  0.0 99.5 jit_solution(4761179788644669466)
XLA Ops:
  0.6 2.0 %pack.1 = (bf16[256,1024]{1,0:T(8,128)(2,1)}, bf16[4,1024]{1,0:T(4,128)(2,1)}) custom-call(bf16[256,512]{1,0:T(8,128)(2,1)} %k_ref.1, bf16[256,512]{1,0:T(8,128)(2,1)} %v_ref.1, bf16[4,512]{1,0:T(4,128)(2,1)} %pk_ref.1, bf16[4,512]{1,0:T(4,128)(2,1)} %pv_ref.1), custom_call_target="tpu_custom_call" | custom-call | tf_op jit(solution)/shard_map/pack/pallas_call | solution.py:63
  2.6 5.0 %collective-permute-start.1 = (bf16[256,1024]{1,0:T(8,128)(2,1)}, bf16[256,1024]{1,0:T(8,128)(2,1)S(1)}, u32[]{:S(2)}, u32[]{:S(2)}) collective-permute-start(bf16[256,1024]{1,0:T(8,128)(2,1)} %get-tuple-element.26.own_ref), channel_id=1, source_target_pairs={{0,2},{1,3},{2,4},{3,5},{4,6},{5,7},{6,8},{7,9},{8,10},{9,11},{10,... | collective-permute-start | bytes 1572872 | tf_op jit(solution)/shard_map/ppermute | solution.py:25
  7.6 2.3 %collective-permute-start = (bf16[256,1024]{1,0:T(8,128)(2,1)}, bf16[256,1024]{1,0:T(8,128)(2,1)}, u32[]{:S(2)}, u32[]{:S(2)}) collective-permute-start(bf16[256,1024]{1,0:T(8,128)(2,1)} %get-tuple-element.26.own_ref), channel_id=1, source_target_pairs={{0,1},{2,3},{4,5},{6,7},{8,9},{10,11},{12,13},{14,15},{1,4},{3,6},... | collective-permute-start | bytes 1572872 | tf_op jit(solution)/shard_map/ppermute | solution.py:25
  9.9 1.4 %collective-permute-start.3 = (bf16[4,1024]{1,0:T(4,128)(2,1)}, bf16[4,1024]{1,0:T(4,128)(2,1)S(1)}, u32[]{:S(2)}, u32[]{:S(2)}) collective-permute-start(bf16[4,1024]{1,0:T(4,128)(2,1)} %get-tuple-element.27), channel_id=1, source_target_pairs={{0,1},{1,0},{2,3},{3,2},{4,5},{5,4},{6,7},{7,6},{8,9},{9,8},{10,11... | collective-permute-start | bytes 24584 | tf_op jit(solution)/shard_map/ppermute | solution.py:25
  14.6 1.6 %collective-permute-start.4 = (bf16[8,1024]{1,0:T(8,128)(2,1)S(1)}, bf16[8,1024]{1,0:T(8,128)(2,1)S(1)}, u32[]{:S(2)}, u32[]{:S(2)}) collective-permute-start(bf16[8,1024]{1,0:T(8,128)(2,1)S(1)} %maximum_select_fusion), channel_id=1, source_target_pairs={{0,2},{1,11},{2,4},{3,13},{4,6},{5,15},{6,8},{7,1},{8,10},{9,3},{1... | collective-permute-start | bytes 49160 | tf_op jit(solution)/shard_map/ppermute | solution.py:25
  16.2 2.0 %fusion = (f32[1088,128]{1,0:T(8,128)S(1)}, f32[1088,128]{1,0:T(8,128)S(1)}) fusion(f32[128]{0:T(128)S(1)} %get-tuple-element.52, f32[128]{0:T(128)S(1)} %get-tuple-element.53, f32[1088]{0:T(1024)S(1)} %add_convert_fusion), kind=kLoop, calls=%fused_computation.2 | loop fusion | flops 278528 | bytes 1119488 | tf_op jit(solution)/shard_map/mul | solution.py:37
  18.3 1.6 %collective-permute-start.5 = (bf16[8,1024]{1,0:T(8,128)(2,1)S(1)}, bf16[8,1024]{1,0:T(8,128)(2,1)S(1)}, u32[]{:S(2)}, u32[]{:S(2)}) collective-permute-start(bf16[8,1024]{1,0:T(8,128)(2,1)S(1)} %maximum_select_fusion), channel_id=1, source_target_pairs={{0,4},{1,13},{2,6},{3,15},{4,8},{5,1},{6,10},{7,3},{8,12},{9,5},{1... | collective-permute-start | bytes 49160 | tf_op jit(solution)/shard_map/ppermute | solution.py:25
  19.9 1.0 %collective-permute-start.6 = (bf16[8,1024]{1,0:T(8,128)(2,1)S(1)}, bf16[8,1024]{1,0:T(8,128)(2,1)S(1)}, u32[]{:S(2)}, u32[]{:S(2)}) collective-permute-start(bf16[8,1024]{1,0:T(8,128)(2,1)S(1)} %maximum_select_fusion), channel_id=1, source_target_pairs={{0,6},{1,15},{2,8},{3,1},{4,10},{5,3},{6,12},{7,5},{8,14},{9,7},{1... | collective-permute-start | bytes 49160 | tf_op jit(solution)/shard_map/ppermute | solution.py:25
  21.1 5.9 %collective-permute-start.7 = (bf16[8,1024]{1,0:T(8,128)(2,1)S(1)}, bf16[8,1024]{1,0:T(8,128)(2,1)S(1)}, u32[]{:S(2)}, u32[]{:S(2)}) collective-permute-start(bf16[8,1024]{1,0:T(8,128)(2,1)S(1)} %maximum_select_fusion), channel_id=1, source_target_pairs={{0,8},{1,1},{2,10},{3,3},{4,12},{5,5},{6,14},{7,7},{8,0},{9,9},{10... | collective-permute-start | bytes 49160 | tf_op jit(solution)/shard_map/ppermute | solution.py:25
  27.1 1.6 %collective-permute-done.7 = bf16[8,1024]{1,0:T(8,128)(2,1)S(1)} collective-permute-done((bf16[8,1024]{1,0:T(8,128)(2,1)S(1)}, bf16[8,1024]{1,0:T(8,128)(2,1)S(1)}, u32[]{:S(2)}, u32[]{:S(2)}) %collective-permute-start.7) | collective-permute-done | bytes 16416 | tf_op jit(solution)/shard_map/ppermute | solution.py:25
  28.7 1.2 %collective-permute-done.8.pb_ref = bf16[32,1024]{1,0:T(8,128)(2,1)S(1)} collective-permute-done((bf16[32,1024]{1,0:T(8,128)(2,1)S(1)}, bf16[32,1024]{1,0:T(8,128)(2,1)S(1)}, u32[]{:S(2)}, u32[]{:S(2)}) %collective-permute-start.8) | collective-permute-done | bytes 65568 | tf_op jit(solution)/shard_map/ppermute | solution.py:25
  30.0 1.3 %copy-done.3 = bf16[256,2560]{1,0:T(8,128)(2,1)S(1)} copy-done((bf16[256,2560]{1,0:T(8,128)(2,1)S(1)}, bf16[256,2560]{1,0:T(8,128)(2,1)}, u32[]{:S(2)}) %copy-start.3) | copy-done | bytes 1310744
  31.3 27.4 %attend.1 = (bf16[256,2560]{1,0:T(8,128)(2,1)}, bf16[256,2560]{1,0:T(8,128)(2,1)}, f32[256,1024]{1,0:T(8,128)S(1)}, bf16[256,1024]{1,0:T(8,128)(2,1)}, f32[256,1...) custom-call(s32[4]{0:T(128)S(1)} %pad_add_fusion.seen, bf16[256,2560]{1,0:T(8,128)(2,1)S(1)} %copy-done.2, ...), custom_call_target="tpu_custom_call" | custom-call | tf_op jit(solution)/shard_map/attend/pallas_call | solution.py:172
  61.5 1.3 %collective-permute-start.9 = (bf16[256,1024]{1,0:T(8,128)(2,1)}, bf16[256,1024]{1,0:T(8,128)(2,1)S(1)}, u32[]{:S(2)}, u32[]{:S(2)}) collective-permute-start(bf16[256,1024]{1,0:T(8,128)(2,1)} %get-tuple-element.31), channel_id=1, source_target_pairs={{1,0},{3,2},{5,4},{7,6},{9,8},{11,10},{13,12},{15,14},{4,1},{6,3},... | collective-permute-start | bytes 1572872 | tf_op jit(solution)/shard_map/ppermute | solution.py:25
  62.8 1.4 %collective-permute-done.10.r3_ref = f32[288,1024]{1,0:T(8,128)S(1)} collective-permute-done((f32[288,1024]{1,0:T(8,128)S(1)}, f32[288,1024]{1,0:T(8,128)S(1)}, u32[]{:S(2)}, u32[]{:S(2)}) %collective-permute-start.10) | collective-permute-done | bytes 1179680 | tf_op jit(solution)/shard_map/ppermute | solution.py:25
  64.2 1.0 %copy-done.8 = f32[288,1024]{1,0:T(8,128)} copy-done((f32[288,1024]{1,0:T(8,128)}, f32[288,1024]{1,0:T(8,128)S(1)}, u32[]{:S(2)}) %copy-start.8) | copy-done | bytes 1179672
  65.2 2.5 %merge.1 = (bf16[256,1024]{1,0:T(8,128)(2,1)}, f32[8,1024]{1,0:T(8,128)}, f32[8,1024]{1,0:T(8,128)}, f32[8,1024]{1,0:T(8,128)}, f32[8,1024]{1,0:T(8,128)}) custom-call(f32[256,1024]{1,0:T(8,128)} %copy-done.5, f32[288,1024]{1,0:T(8,128)} %copy-done.8, f32[32,1024]{1,0:T(8,128)} %copy-done.7), custom_call_target="tpu_custom_call" | custom-call | tf_op jit(solution)/shard_map/merge/pallas_call | solution.py:201
  67.7 1.3 %collective-permute-start.11 = (bf16[256,1024]{1,0:T(8,128)(2,1)}, bf16[256,1024]{1,0:T(8,128)(2,1)S(1)}, u32[]{:S(2)}, u32[]{:S(2)}) collective-permute-start(bf16[256,1024]{1,0:T(8,128)(2,1)} %get-tuple-element.35), channel_id=1, source_target_pairs={{2,0},{3,1},{4,2},{5,3},{6,4},{7,5},{8,6},{9,7},{10,8},{11,9},{12,... | collective-permute-start | bytes 1572872 | tf_op jit(solution)/shard_map/ppermute | solution.py:25
  69.0 6.1 %collective-permute-start.12 = (f32[8,1024]{1,0:T(8,128)}, f32[8,1024]{1,0:T(8,128)S(1)}, u32[]{:S(2)}, u32[]{:S(2)}) collective-permute-start(f32[8,1024]{1,0:T(8,128)} %get-tuple-element.36), channel_id=1, source_target_pairs={{2,0},{11,1},{4,2},{13,3},{6,4},{15,5},{8,6},{1,7},{10,8},{3,9},{1... | collective-permute-start | bytes 98312 | tf_op jit(solution)/shard_map/ppermute | solution.py:25
  75.6 9.6 %collective-permute-done.12.refs_0_ = f32[8,1024]{1,0:T(8,128)S(1)} collective-permute-done((f32[8,1024]{1,0:T(8,128)}, f32[8,1024]{1,0:T(8,128)S(1)}, u32[]{:S(2)}, u32[]{:S(2)}) %collective-permute-start.12) | collective-permute-done | bytes 32800 | tf_op jit(solution)/shard_map/ppermute | solution.py:25
  85.2 4.9 %collective-permute-start.15 = (f32[8,1024]{1,0:T(8,128)}, f32[8,1024]{1,0:T(8,128)S(1)}, u32[]{:S(2)}, u32[]{:S(2)}) collective-permute-start(f32[8,1024]{1,0:T(8,128)} %get-tuple-element.39), channel_id=1, source_target_pairs={{8,0},{1,1},{10,2},{3,3},{12,4},{5,5},{14,6},{7,7},{0,8},{9,9},{2,... | collective-permute-start | bytes 98312 | tf_op jit(solution)/shard_map/ppermute | solution.py:25
  90.2 2.0 %collective-permute-done.15.refs_3_ = f32[8,1024]{1,0:T(8,128)S(1)} collective-permute-done((f32[8,1024]{1,0:T(8,128)}, f32[8,1024]{1,0:T(8,128)S(1)}, u32[]{:S(2)}, u32[]{:S(2)}) %collective-permute-start.15) | collective-permute-done | bytes 32800 | tf_op jit(solution)/shard_map/ppermute | solution.py:25
  92.8 1.4 %tally.1 = (f32[4,1024]{1,0:T(4,128)}, f32[4,1024]{1,0:T(4,128)}) custom-call(s32[1]{0:T(128)} %bitcast.1.core_ref, f32[8,1024]{1,0:T(8,128)} %copy-done.11, f32[8,1024]{1,0:T(8,128)} %copy-done.12, f32[8,1024]{1,0:T(8,128)} %copy-done.13, f32[8,1024]{1,0:T(8,128)} %copy-done.14), custom_call_target="tpu_custom_call" | custom-call | tf_op jit(solution)/shard_map/tally/pallas_call | solution.py:224
  96.5 3.0 %finish.1 = (bf16[256,512]{1,0:T(8,128)(2,1)}, bf16[256,512]{1,0:T(8,128)(2,1)}, bf16[4,512]{1,0:T(4,128)(2,1)}, bf16[4,512]{1,0:T(4,128)(2,1)}) custom-call(f32[256,1024]{1,0:T(8,128)} %copy-done.4, bf16[256,1024]{1,0:T(8,128)(2,1)} %copy-done.9, bf16[256,1024]{1,0:T(8,128)(2,1)} %copy-done.10, f32[1088,128]{1,0:T(8,128)} %copy-done.1, ...), custom_call_target="tpu_custom_call" | custom-call | tf_op jit(solution)/shard_map/finish/pallas_call | solution.py:253
  (68 shorter events, 9.8 us)
Async XLA Ops:
  0.6 29.3 %copy-start.2 = (bf16[256,2560]{1,0:T(8,128)(2,1)S(1)}, bf16[256,2560]{1,0:T(8,128)(2,1)}, u32[]{:S(2)}) copy-start(bf16[256,2560]{1,0:T(8,128)(2,1)} %q_ref.1) | copy-start | bytes 3932164
  2.6 27.3 %copy-start.6 = (bf16[256,1024]{1,0:T(8,128)(2,1)S(1)}, bf16[256,1024]{1,0:T(8,128)(2,1)}, u32[]{:S(2)}) copy-start(bf16[256,1024]{1,0:T(8,128)(2,1)} %get-tuple-element.26.own_ref) | copy-start | bytes 1572868
  2.6 24.3 %collective-permute-start.1 = (bf16[256,1024]{1,0:T(8,128)(2,1)}, bf16[256,1024]{1,0:T(8,128)(2,1)S(1)}, u32[]{:S(2)}, u32[]{:S(2)}) collective-permute-start(bf16[256,1024]{1,0:T(8,128)(2,1)} %get-tuple-element.26.own_ref), channel_id=1, source_target_pairs={{0,2},{1,3},{2,4},{3,5},{4,6},{5,7},{6,8},{7,9},{8,10},{9,11},{10,... | collective-permute-start | bytes 1572872 | tf_op jit(solution)/shard_map/ppermute | solution.py:25
  7.6 22.3 %collective-permute-start = (bf16[256,1024]{1,0:T(8,128)(2,1)}, bf16[256,1024]{1,0:T(8,128)(2,1)}, u32[]{:S(2)}, u32[]{:S(2)}) collective-permute-start(bf16[256,1024]{1,0:T(8,128)(2,1)} %get-tuple-element.26.own_ref), channel_id=1, source_target_pairs={{0,1},{2,3},{4,5},{6,7},{8,9},{10,11},{12,13},{14,15},{1,4},{3,6},... | collective-permute-start | bytes 1572872 | tf_op jit(solution)/shard_map/ppermute | solution.py:25
  9.9 3.9 %collective-permute-start.3 = (bf16[4,1024]{1,0:T(4,128)(2,1)}, bf16[4,1024]{1,0:T(4,128)(2,1)S(1)}, u32[]{:S(2)}, u32[]{:S(2)}) collective-permute-start(bf16[4,1024]{1,0:T(4,128)(2,1)} %get-tuple-element.27), channel_id=1, source_target_pairs={{0,1},{1,0},{2,3},{3,2},{4,5},{5,4},{6,7},{7,6},{8,9},{9,8},{10,11... | collective-permute-start | bytes 24584 | tf_op jit(solution)/shard_map/ppermute | solution.py:25
  14.6 6.5 %collective-permute-start.4 = (bf16[8,1024]{1,0:T(8,128)(2,1)S(1)}, bf16[8,1024]{1,0:T(8,128)(2,1)S(1)}, u32[]{:S(2)}, u32[]{:S(2)}) collective-permute-start(bf16[8,1024]{1,0:T(8,128)(2,1)S(1)} %maximum_select_fusion), channel_id=1, source_target_pairs={{0,2},{1,11},{2,4},{3,13},{4,6},{5,15},{6,8},{7,1},{8,10},{9,3},{1... | collective-permute-start | bytes 49160 | tf_op jit(solution)/shard_map/ppermute | solution.py:25
  18.2 40.5 %copy-start = (f32[1088,128]{1,0:T(8,128)}, f32[1088,128]{1,0:T(8,128)S(1)}, u32[]{:S(2)}) copy-start(f32[1088,128]{1,0:T(8,128)S(1)} %get-tuple-element.48.sin_ref) | copy-start | bytes 1671172
  18.2 40.5 %copy-start.1 = (f32[1088,128]{1,0:T(8,128)}, f32[1088,128]{1,0:T(8,128)S(1)}, u32[]{:S(2)}) copy-start(f32[1088,128]{1,0:T(8,128)S(1)} %get-tuple-element.49.cos_ref) | copy-start | bytes 1671172
  18.3 8.8 %collective-permute-start.5 = (bf16[8,1024]{1,0:T(8,128)(2,1)S(1)}, bf16[8,1024]{1,0:T(8,128)(2,1)S(1)}, u32[]{:S(2)}, u32[]{:S(2)}) collective-permute-start(bf16[8,1024]{1,0:T(8,128)(2,1)S(1)} %maximum_select_fusion), channel_id=1, source_target_pairs={{0,4},{1,13},{2,6},{3,15},{4,8},{5,1},{6,10},{7,3},{8,12},{9,5},{1... | collective-permute-start | bytes 49160 | tf_op jit(solution)/shard_map/ppermute | solution.py:25
  19.9 7.2 %collective-permute-start.6 = (bf16[8,1024]{1,0:T(8,128)(2,1)S(1)}, bf16[8,1024]{1,0:T(8,128)(2,1)S(1)}, u32[]{:S(2)}, u32[]{:S(2)}) collective-permute-start(bf16[8,1024]{1,0:T(8,128)(2,1)S(1)} %maximum_select_fusion), channel_id=1, source_target_pairs={{0,6},{1,15},{2,8},{3,1},{4,10},{5,3},{6,12},{7,5},{8,14},{9,7},{1... | collective-permute-start | bytes 49160 | tf_op jit(solution)/shard_map/ppermute | solution.py:25
  21.1 7.6 %collective-permute-start.7 = (bf16[8,1024]{1,0:T(8,128)(2,1)S(1)}, bf16[8,1024]{1,0:T(8,128)(2,1)S(1)}, u32[]{:S(2)}, u32[]{:S(2)}) collective-permute-start(bf16[8,1024]{1,0:T(8,128)(2,1)S(1)} %maximum_select_fusion), channel_id=1, source_target_pairs={{0,8},{1,1},{2,10},{3,3},{4,12},{5,5},{6,14},{7,7},{8,0},{9,9},{10... | collective-permute-start | bytes 49160 | tf_op jit(solution)/shard_map/ppermute | solution.py:25
  27.0 3.0 %collective-permute-start.2 = (bf16[256,1024]{1,0:T(8,128)(2,1)S(1)}, bf16[256,1024]{1,0:T(8,128)(2,1)S(1)}, u32[]{:S(2)}, u32[]{:S(2)}) collective-permute-start(bf16[256,1024]{1,0:T(8,128)(2,1)S(1)} %collective-permute-done.1.w2_ref), channel_id=1, source_target_pairs={{0,1},{1,0},{2,3},{3,2},{4,5},{5,4},{6,7},{7,6},{8,9},{9,8},{10,11... | collective-permute-start | bytes 1572872 | tf_op jit(solution)/shard_map/ppermute | solution.py:25
  28.7 1.3 %collective-permute-start.8 = (bf16[32,1024]{1,0:T(8,128)(2,1)S(1)}, bf16[32,1024]{1,0:T(8,128)(2,1)S(1)}, u32[]{:S(2)}, u32[]{:S(2)}) collective-permute-start(bf16[32,1024]{1,0:T(8,128)(2,1)S(1)} %constant_dynamic-update-slice_fusion.pa_ref), channel_id=1, source_target_pairs={{0,1},{1,0},{2,3},{3,2},{4,5},{5,4},{6,7},{7,6},{8,9},{9,8},{10,11... | collective-permute-start | bytes 196616 | tf_op jit(solution)/shard_map/ppermute | solution.py:25
  61.3 2.8 %collective-permute-start.10 = (f32[288,1024]{1,0:T(8,128)S(1)}, f32[288,1024]{1,0:T(8,128)S(1)}, u32[]{:S(2)}, u32[]{:S(2)}) collective-permute-start(f32[288,1024]{1,0:T(8,128)S(1)} %get-tuple-element.33), channel_id=1, source_target_pairs={{0,1},{1,0},{2,3},{3,2},{4,5},{5,4},{6,7},{7,6},{8,9},{9,8},{10,11... | collective-permute-start | bytes 3538952 | tf_op jit(solution)/shard_map/ppermute | solution.py:25
  61.5 33.5 %collective-permute-start.9 = (bf16[256,1024]{1,0:T(8,128)(2,1)}, bf16[256,1024]{1,0:T(8,128)(2,1)S(1)}, u32[]{:S(2)}, u32[]{:S(2)}) collective-permute-start(bf16[256,1024]{1,0:T(8,128)(2,1)} %get-tuple-element.31), channel_id=1, source_target_pairs={{1,0},{3,2},{5,4},{7,6},{9,8},{11,10},{13,12},{15,14},{4,1},{6,3},... | collective-permute-start | bytes 1572872 | tf_op jit(solution)/shard_map/ppermute | solution.py:25
  67.7 28.0 %collective-permute-start.11 = (bf16[256,1024]{1,0:T(8,128)(2,1)}, bf16[256,1024]{1,0:T(8,128)(2,1)S(1)}, u32[]{:S(2)}, u32[]{:S(2)}) collective-permute-start(bf16[256,1024]{1,0:T(8,128)(2,1)} %get-tuple-element.35), channel_id=1, source_target_pairs={{2,0},{3,1},{4,2},{5,3},{6,4},{7,5},{8,6},{9,7},{10,8},{11,9},{12,... | collective-permute-start | bytes 1572872 | tf_op jit(solution)/shard_map/ppermute | solution.py:25
  69.0 16.2 %collective-permute-start.12 = (f32[8,1024]{1,0:T(8,128)}, f32[8,1024]{1,0:T(8,128)S(1)}, u32[]{:S(2)}, u32[]{:S(2)}) collective-permute-start(f32[8,1024]{1,0:T(8,128)} %get-tuple-element.36), channel_id=1, source_target_pairs={{2,0},{11,1},{4,2},{13,3},{6,4},{15,5},{8,6},{1,7},{10,8},{3,9},{1... | collective-permute-start | bytes 98312 | tf_op jit(solution)/shard_map/ppermute | solution.py:25
  75.1 15.0 %collective-permute-start.13 = (f32[8,1024]{1,0:T(8,128)}, f32[8,1024]{1,0:T(8,128)S(1)}, u32[]{:S(2)}, u32[]{:S(2)}) collective-permute-start(f32[8,1024]{1,0:T(8,128)} %get-tuple-element.37), channel_id=1, source_target_pairs={{4,0},{13,1},{6,2},{15,3},{8,4},{1,5},{10,6},{3,7},{12,8},{5,9},{1... | collective-permute-start | bytes 98312 | tf_op jit(solution)/shard_map/ppermute | solution.py:25
  75.6 14.6 %collective-permute-start.14 = (f32[8,1024]{1,0:T(8,128)}, f32[8,1024]{1,0:T(8,128)S(1)}, u32[]{:S(2)}, u32[]{:S(2)}) collective-permute-start(f32[8,1024]{1,0:T(8,128)} %get-tuple-element.38), channel_id=1, source_target_pairs={{6,0},{15,1},{8,2},{1,3},{10,4},{3,5},{12,6},{5,7},{14,8},{7,9},{0... | collective-permute-start | bytes 98312 | tf_op jit(solution)/shard_map/ppermute | solution.py:25
  85.2 7.0 %copy-start.11 = (f32[8,1024]{1,0:T(8,128)}, f32[8,1024]{1,0:T(8,128)S(1)}, u32[]{:S(2)}) copy-start(f32[8,1024]{1,0:T(8,128)S(1)} %collective-permute-done.12.refs_0_) | copy-start | bytes 98308
  85.2 7.0 %collective-permute-start.15 = (f32[8,1024]{1,0:T(8,128)}, f32[8,1024]{1,0:T(8,128)S(1)}, u32[]{:S(2)}, u32[]{:S(2)}) collective-permute-start(f32[8,1024]{1,0:T(8,128)} %get-tuple-element.39), channel_id=1, source_target_pairs={{8,0},{1,1},{10,2},{3,3},{12,4},{5,5},{14,6},{7,7},{0,8},{9,9},{2,... | collective-permute-start | bytes 98312 | tf_op jit(solution)/shard_map/ppermute | solution.py:25
  90.2 2.1 %copy-start.12 = (f32[8,1024]{1,0:T(8,128)}, f32[8,1024]{1,0:T(8,128)S(1)}, u32[]{:S(2)}) copy-start(f32[8,1024]{1,0:T(8,128)S(1)} %collective-permute-done.13.refs_1_) | copy-start | bytes 98308
  90.2 2.1 %copy-start.13 = (f32[8,1024]{1,0:T(8,128)}, f32[8,1024]{1,0:T(8,128)S(1)}, u32[]{:S(2)}) copy-start(f32[8,1024]{1,0:T(8,128)S(1)} %collective-permute-done.14.refs_2_) | copy-start | bytes 98308
  94.3 1.4 %collective-permute-start.16 = (f32[4,1024]{1,0:T(4,128)}, f32[4,1024]{1,0:T(4,128)S(1)}, u32[]{:S(2)}, u32[]{:S(2)}) collective-permute-start(f32[4,1024]{1,0:T(4,128)} %get-tuple-element.41), channel_id=1, source_target_pairs={{0,1},{1,0},{2,3},{3,2},{4,5},{5,4},{6,7},{7,6},{8,9},{9,8},{10,11... | collective-permute-start | bytes 49160 | tf_op jit(solution)/shard_map/ppermute | solution.py:25
  (9 other events, 7.8 us)

commit v4 on v3

--- a/solution.py
+++ b/solution.py
@@ -48,54 +48,58 @@
 IN_VMEM = pl.BlockSpec(memory_space=pltpu.VMEM)
 
 
-def stack(a, b):
-    return jnp.concatenate([a, b], axis=0)
-
-
 def pack_kernel(k_ref, v_ref, pk_ref, pv_ref, own_ref, mine_ref):
-    own_ref[:, :WIDTH] = k_ref[...]
-    own_ref[:, WIDTH:] = v_ref[...]
+    rows, few = k_ref.shape[0], pk_ref.shape[0]
+    own_ref[:rows, :WIDTH] = k_ref[...]
+    own_ref[:rows, WIDTH:] = v_ref[...]
     mine_ref[:, :WIDTH] = pk_ref[...]
     mine_ref[:, WIDTH:] = pv_ref[...]
+    twice = jnp.concatenate([mine_ref[...].astype(f32)] * 2, axis=0)
+    own_ref[rows:, :] = twice.astype(bf16)
 
 
 def pack(keys, values, prompt_keys, prompt_values):
     return pl.pallas_call(
         pack_kernel,
         out_shape=[
-            jax.ShapeDtypeStruct((keys.shape[0], 2 * WIDTH), bf16),
+            jax.ShapeDtypeStruct((keys.shape[0] + 2 * prompt_keys.shape[0], 2 * WIDTH), bf16),
             jax.ShapeDtypeStruct((prompt_keys.shape[0], 2 * WIDTH), bf16),
         ],
         out_specs=[IN_VMEM, IN_VMEM],
+        compiler_params=pltpu.CompilerParams(vmem_limit_bytes=6 * 2**20),
         name="pack",
     )(keys, values, prompt_keys, prompt_values)
 
 
 def attend_kernel(
-    seen, q_ref, g_ref, cos_ref, sin_ref, own_ref, w1_ref, w2_ref, w3_ref, pa_ref, pb_ref,
+    seen, q_ref, g_ref, cos_ref, sin_ref, own_ref, w1_ref, w2_ref, w3_ref,
+    mine_ref, theirs_ref, near_ref, far_ref,
     o_ref, dq_ref, d0_ref, d1_ref, d2_ref, d3_ref, dp_ref,
     k_buf, v_buf, dk_buf, dv_buf, p_buf,
 ):
     rows = q_ref.shape[0]
-    half = pa_ref.shape[0]
-    core = seen[3]
+    few, half = mine_ref.shape[0], near_ref.shape[0]
     col = pl.program_id(0) * HD
     k_at = pl.ds(pl.multiple_of(col, HD), HD)
     v_at = pl.ds(pl.multiple_of(col + WIDTH, HD), HD)
     for j, part in enumerate((own_ref, w1_ref, w2_ref, w3_ref)):
         span = slice(j * rows, (j + 1) * rows)
-        raw = part[:, k_at].astype(f32)
+        raw = part[:rows, k_at].astype(f32)
         k_buf[span, :] = turn(raw, cos_ref[span, :], sin_ref[span, :]).astype(bf16)
-        v_buf[span, :] = part[:, v_at]
-    mine = pl.ds(pl.multiple_of(core * half, half), half)
-    other = pl.ds(pl.multiple_of((1 - core) * half, half), half)
-    span = slice(SPAN * rows, SPAN * rows + 2 * half)
-    p_buf[mine, :] = pa_ref[:, k_at].astype(f32)
-    p_buf[other, :] = pb_ref[:, k_at].astype(f32)
-    k_buf[span, :] = turn(p_buf[...], cos_ref[span, :], sin_ref[span, :]).astype(bf16)
-    p_buf[mine, :] = pa_ref[:, v_at].astype(f32)
-    p_buf[other, :] = pb_ref[:, v_at].astype(f32)
-    v_buf[span, :] = p_buf[...].astype(bf16)
+        v_buf[span, :] = part[:rows, v_at]
+    span = slice(SPAN * rows, SPAN * rows + 4 * few + 2 * half)
+
+    def gather(at):
+        p_buf[:few, :] = mine_ref[:, at].astype(f32)
+        p_buf[few : 2 * few, :] = theirs_ref[:, at].astype(f32)
+        p_buf[2 * few : 3 * few, :] = w2_ref[rows:, at].astype(f32)[:few]
+        p_buf[3 * few : 4 * few, :] = w3_ref[rows:, at].astype(f32)[:few]
+        p_buf[4 * few : 4 * few + half, :] = near_ref[:, at].astype(f32)
+        p_buf[4 * few + half :, :] = far_ref[:, at].astype(f32)
+        return p_buf[...]
+
+    k_buf[span, :] = turn(gather(k_at), cos_ref[span, :], sin_ref[span, :]).astype(bf16)
+    v_buf[span, :] = gather(v_at).astype(bf16)
     k, v = k_buf[...], v_buf[...]
     cosine, sine = cos_ref[:rows, :], sin_ref[:rows, :]
     lower = lax.broadcasted_iota(jnp.int32, (rows, rows), 1) <= lax.broadcasted_iota(
@@ -158,27 +162,33 @@
     for at, buf in ((k_at, dk_buf), (v_at, dv_buf)):
         for j, out in enumerate((d0_ref, d1_ref, d2_ref, d3_ref)):
             out[:rows, at] = buf[j * rows : (j + 1) * rows, :].astype(out.dtype)
-        dp_ref[:, at] = buf[pl.ds(pl.multiple_of(start + core * half, 8), half), :]
-        d3_ref[rows:, at] = buf[pl.ds(pl.multiple_of(start + (1 - core) * half, 8), half), :]
+        for j in range(2):
+            mid = start + 2 * few * j
+            dp_ref[j * few : (j + 1) * few, at] = buf[mid : mid + few, :]
+            d3_ref[rows + j * few : rows + (j + 1) * few, at] = buf[mid + few : mid + 2 * few, :]
+        mid = start + 4 * few
+        dp_ref[2 * few :, at] = buf[mid : mid + half, :]
+        d3_ref[rows + 2 * few :, at] = buf[mid + half :, :]
 
 
 def attend(seen, queries, grads, cosine, sine, blocks, prompts):
     rows = queries.shape[0]
     wide = blocks[0].shape[1]
-    half = prompts[0].shape[0]
-    keys = SPAN * rows + 2 * half
+    few, half = prompts[0].shape[0], prompts[2].shape[0]
+    keys = SPAN * rows + 4 * few + 2 * half
+    part = half + 2 * few
     head = pl.BlockSpec((rows, GROUP * HD), lambda i, s: (0, i))
-    outs = [(rows, f32), (rows, bf16), (rows, f32), (rows + half, f32), (half, f32)]
+    outs = [(rows, f32), (rows, bf16), (rows, f32), (rows + part, f32), (part, f32)]
     return pl.pallas_call(
         attend_kernel,
         grid_spec=pltpu.PrefetchScalarGridSpec(
             num_scalar_prefetch=1,
             grid=(KVH,),
-            in_specs=[head, head] + [IN_VMEM] * 8,
+            in_specs=[head, head] + [IN_VMEM] * 10,
             out_specs=[head, head] + [IN_VMEM] * 5,
             scratch_shapes=[pltpu.VMEM((keys, HD), bf16)] * 2
             + [pltpu.VMEM((keys, HD), f32)] * 2
-            + [pltpu.VMEM((2 * half, HD), f32)],
+            + [pltpu.VMEM((2 * part, HD), f32)],
         ),
         out_shape=[jax.ShapeDtypeStruct(queries.shape, bf16)] * 2
         + [jax.ShapeDtypeStruct((r, wide), t) for r, t in outs],
@@ -187,75 +197,88 @@
     )(seen, queries, grads, cosine, sine, *blocks, *prompts)
 
 
-def merge_kernel(d2_ref, r3_ref, dp_ref, x2_ref, *outs):
-    rows = d2_ref.shape[0]
-    x2_ref[...] = (d2_ref[...] + r3_ref[:rows, :]).astype(bf16)
+def merge_kernel(d2_ref, r3_ref, dp_ref, x2_ref, keep_ref, *outs):
+    rows, few = d2_ref.shape[0], keep_ref.shape[0]
+    x2_ref[:rows, :] = (d2_ref[...] + r3_ref[:rows, :]).astype(bf16)
+    keep_ref[...] = dp_ref[:few, :] + r3_ref[rows : rows + few, :]
+    near = dp_ref[few : 2 * few, :] + r3_ref[rows + few : rows + 2 * few, :]
+    high = near.astype(bf16).astype(f32)
+    x2_ref[rows:, :] = jnp.concatenate([high, near - high], axis=0).astype(bf16)
     for j, out in enumerate(outs):
         step = out.shape[0]
-        span = slice(j * step, (j + 1) * step)
-        out[...] = dp_ref[span, :] + r3_ref[rows + j * step : rows + (j + 1) * step, :]
-
-
-def merge(d2, r3, dp, pieces):
+        at = 2 * few + j * step
+        out[...] = dp_ref[at : at + step, :] + r3_ref[rows + at : rows + at + step, :]
+
+
+def merge(d2, r3, dp, few, pieces):
     rows, wide = d2.shape
     return pl.pallas_call(
         merge_kernel,
         in_specs=[IN_VMEM] * 3,
-        out_specs=[IN_VMEM] * (1 + pieces),
-        out_shape=[jax.ShapeDtypeStruct((rows, wide), bf16)]
-        + [jax.ShapeDtypeStruct((dp.shape[0] // pieces, wide), f32)] * pieces,
+        out_specs=[IN_VMEM] * (2 + pieces),
+        out_shape=[
+            jax.ShapeDtypeStruct((rows + 2 * few, wide), bf16),
+            jax.ShapeDtypeStruct((few, wide), f32),
+        ]
+        + [jax.ShapeDtypeStruct((2 * few, wide), f32)] * pieces,
+        compiler_params=pltpu.CompilerParams(vmem_limit_bytes=6 * 2**20),
         name="merge",
     )(d2, r3, dp)
 
 
-def tally_kernel(core_ref, *refs):
+def tally_kernel(*refs):
     terms, keep_ref, send_ref = refs[:-2], refs[-2], refs[-1]
     few = keep_ref.shape[0]
     total = terms[0][...]
     for term in terms[1:]:
         total = total + term[...]
-    first = core_ref[0] == 0
-    keep_ref[...] = jnp.where(first, total[:few], total[few:])
-    send_ref[...] = jnp.where(first, total[few:], total[:few])
-
-
-def tally(core, terms):
+    keep_ref[...] = total[:few]
+    send_ref[...] = total[few:]
+
+
+def tally(terms):
     few, wide = terms[0].shape
     return pl.pallas_call(
         tally_kernel,
-        in_specs=[pl.BlockSpec(memory_space=pltpu.SMEM)] + [IN_VMEM] * len(terms),
+        in_specs=[IN_VMEM] * len(terms),
         out_specs=[IN_VMEM] * 2,
         out_shape=[jax.ShapeDtypeStruct((few // 2, wide), f32)] * 2,
+        compiler_params=pltpu.CompilerParams(vmem_limit_bytes=2 * 2**20),
         name="tally",
-    )(core, *terms)
+    )(*terms)
 
 
 def finish_kernel(
-    d0_ref, r1_ref, r2_ref, cos_ref, sin_ref, pcos_ref, psin_ref, keep_ref, got_ref,
+    d0_ref, r1_ref, r2_ref, cos_ref, sin_ref, keep_ref, sum_ref, got_ref,
     gk_ref, gv_ref, gpk_ref, gpv_ref,
 ):
     rows = d0_ref.shape[0]
     cosine, sine = cos_ref[:rows, :], -sin_ref[:rows, :]
-    pcos, psin = pcos_ref[...], -psin_ref[...]
+    few = keep_ref.shape[0]
+    mine = slice(SPAN * rows, SPAN * rows + 2 * few)
+    pcos, psin = cos_ref[mine, :][:few], -sin_ref[mine, :][:few]
     for h in range(KVH):
         at = slice(h * HD, (h + 1) * HD)
         vat = slice(WIDTH + h * HD, WIDTH + (h + 1) * HD)
         for cols, out in ((at, gk_ref), (vat, gv_ref)):
-            total = d0_ref[:, cols] + (r1_ref[:, cols].astype(f32) + r2_ref[:, cols].astype(f32))
+            total = d0_ref[:, cols] + (r1_ref[:, cols].astype(f32) + r2_ref[:rows, cols].astype(f32))
             out[:, at] = (turn(total, cosine, sine) if out is gk_ref else total).astype(bf16)
         for cols, out in ((at, gpk_ref), (vat, gpv_ref)):
-            total = keep_ref[:, cols] + got_ref[:, cols]
+            pair = r2_ref[rows:, cols].astype(f32)
+            total = keep_ref[:, cols] + (pair[:few] + pair[few:])
+            total = total + (sum_ref[:, cols] + got_ref[:, cols])
             out[:, at] = (turn(total, pcos, psin) if out is gpk_ref else total).astype(bf16)
 
 
-def finish(d0, r1, r2, cosine, sine, pcos, psin, keep, got):
+def finish(d0, r1, r2, cosine, sine, keep, tallied, got):
     rows, few = d0.shape[0], keep.shape[0]
     return pl.pallas_call(
         finish_kernel,
-        in_specs=[IN_VMEM] * 9,
+        in_specs=[IN_VMEM] * 8,
         out_shape=[jax.ShapeDtypeStruct((r, WIDTH), bf16) for r in (rows, rows, few, few)],
+        compiler_params=pltpu.CompilerParams(vmem_limit_bytes=6 * 2**20),
         name="finish",
-    )(d0, r1, r2, cosine, sine, pcos, psin, keep, got)
+    )(d0, r1, r2, cosine, sine, keep, tallied, got)
 
 
 def local(
@@ -268,16 +291,17 @@
     me = lax.axis_index("ctx")
     core = me & 1
     swap = [(i, i ^ 1) for i in range(n)]
-    ahead = [(i, i + 2) for i in range(n - 2)]
+    ahead = [(i, (i + 2) % n) for i in range(n)]
     across = [(i, i + 1) for i in range(0, n, 2)] + [(i, i + 3) for i in range(1, n - 3, 2)]
-    reach = [[j, (j + chips // 2) % chips] for j in range(1, chips // 2 + 1)]
+    turns = chips // 2 - 1
+    reach = [(1 + j, 1 + j + turns) for j in range(1, turns + 1)]
     rounds = [[(i, (i + 2 * k[i % 2]) % n) for i in range(n)] for k in reach]
 
     own, mine = pack(answer_keys, answer_values, prompt_keys, prompt_values)
     w2 = permute(own, ahead)
     w1 = permute(own, across)
     theirs = permute(mine, swap)
-    chip = jnp.where(core == 0, stack(mine, theirs), stack(theirs, mine))
+    chip = jnp.concatenate([mine, theirs], axis=0)
     near = jnp.concatenate([permute(chip, pairs) for pairs in rounds], axis=0)
     w3 = permute(w2, swap)
     far = permute(near, swap)
@@ -292,26 +316,28 @@
         jnp.where((column >= first[:, None]) & (column < me), table[None, :], 0), axis=1
     )
     places = (positions[None, :] - rows * apart[:, None]).reshape(-1)
-    away = jnp.array([k[0] for k in reach] + [k[1] for k in reach], dtype=jnp.int32)
-    homes = (me // 2 - away + chips) % chips
-    prompt_places = homes[:, None] * (2 * few) + jnp.arange(2 * few, dtype=jnp.int32)
+    low = jnp.array([k[0] for k in reach], dtype=jnp.int32)
+    high = jnp.array([k[1] for k in reach], dtype=jnp.int32)
+    away = jnp.concatenate(
+        [jnp.array([0, 1], jnp.int32), jnp.where(core == 0, low, high), jnp.where(core == 0, high, low)]
+    )
+    first_core = jnp.concatenate([jnp.full((2 + turns,), core), jnp.full((turns,), 1 - core)])
+    homes = 2 * ((me // 2 - away + chips) % chips)
+    homes = jnp.stack([homes + first_core, homes + 1 - first_core], axis=1)
+    prompt_places = homes[:, :, None] * few + jnp.arange(few, dtype=jnp.int32)
     cosine, sine = angle_tables(jnp.concatenate([places, prompt_places.reshape(-1)]))
-    pcos, psin = angle_tables(me * few + jnp.arange(few, dtype=jnp.int32))
-    scalars = jnp.concatenate([seen[1:], core[None]]).astype(jnp.int32)
 
     attended, grad_queries, d0, d1, d2, d3, dp = attend(
-        scalars, queries, out_grad, cosine, sine, [own, w1, w2, w3], [near, far]
+        seen[1:], queries, out_grad, cosine, sine, [own, w1, w2, w3], [mine, theirs, near, far]
     )
     r3 = permute(d3, swap)
     r1 = permute(d1, back(across))
-    x2, *terms = merge(d2, r3, dp, chips // 2)
+    x2, keep, *terms = merge(d2, r3, dp, few, turns)
     r2 = permute(x2, back(ahead))
-    keep, send = tally(
-        core[None].astype(jnp.int32), [permute(t, back(p)) for t, p in zip(terms, rounds)]
-    )
+    tallied, send = tally([permute(t, back(p)) for t, p in zip(terms, rounds)])
     got = permute(send, swap)
     grad_keys, grad_values, grad_prompt_keys, grad_prompt_values = finish(
-        d0, r1, r2, cosine, sine, pcos, psin, keep, got
+        d0, r1, r2, cosine, sine, keep, tallied, got
     )
     return (attended, grad_queries, grad_keys, grad_values, grad_prompt_keys, grad_prompt_values)
 

time: 100 us -> 84.5 us (0.84)
  Pallas kernels: 36.3 us -> 27.6 us
  starting transfers between devices: 33 us -> 25.7 us
  waiting for transfers between devices: 16.7 us -> 20.2 us
  local copies, waits for them, and re-layouts: 6.58 us -> 4.85 us
  other arithmetic: 5.98 us -> 4.53 us
    ppermute x17 -> x15, starting transfers between devices: 33 us -> 25.7 us  [permute(): return lax.ppermute(value, 'ctx', pairs)]
    ppermute x17 -> x15, waiting for transfers between devices: 16.7 us -> 20.2 us  [permute(): return lax.ppermute(value, 'ctx', pairs)]
    pallas_call x2, Pallas kernels: 4.41 us -> 1.17 us  [the longest x1 1.16 us: finish(): pl.pallas_call(finish_kernel, in_specs=[IN_VMEM] * 8, out_shape=[jax.Shap...]
    pallas_call x1, Pallas kernels: 2.51 us -> 0.12 us  [merge(): pl.pallas_call(merge_kernel, in_specs=[IN_VMEM] * 3, out_specs=[IN_VMEM]...]
    pallas_call x1, Pallas kernels: 1.97 us -> 0.04 us  [pack(): pl.pallas_call(pack_kernel, out_shape=[jax.ShapeDtypeStruct((keys.shape[0...]
    unnamed x36 -> x15, local copies, waits for them, and re-layouts: 6.42 us -> 4.59 us
    pallas_call x1, Pallas kernels: 27.4 us -> 26.2 us  [attend(): pl.pallas_call(attend_kernel, grid_spec=pltpu.PrefetchScalarGridSpec(num_...]
    mul x2 -> x1, other arithmetic: 2.71 us -> 2.01 us  [angle_tables(): return (jnp.cos(angles), jnp.sin(angles) * sign[None, :])]
  transfers between devices with their start and end apart: 17 -> 15, of which waited for: 7 -> 5; matrix products, arithmetic and copies ran while one was open for 6% -> 6% of each run, Pallas kernels for 4% -> 0%
where the time goes in v4:
time: 84.5 us; the launch traced here: 83.6 us
  Pallas kernels  27.6 us (33%)
  starting transfers between devices  25.7 us (30%)
  waiting for transfers between devices  20.2 us (24%)
  local copies, waits for them, and re-layouts  4.85 us (6%)
  other arithmetic  4.53 us (5%)
    pallas_call x1, Pallas kernels, attend(): pl.pallas_call(attend_kernel, grid_spec=pltpu.PrefetchScalarGridSpec(num_...  26.2 us
    ppermute x15, starting transfers between devices, permute(): return lax.ppermute(value, 'ctx', pairs)  25.7 us
    ppermute x15, waiting for transfers between devices, permute(): return lax.ppermute(value, 'ctx', pairs)  20.2 us
    unnamed x15, local copies, waits for them, and re-layouts  4.59 us
    mul x1, other arithmetic, angle_tables(): return (jnp.cos(angles), jnp.sin(angles) * sign[None, :])  2.01 us
  transfers between devices with their start and end apart: 15, of which 5 were waited for; matrix products, arithmetic and copies ran while one was open for 6% of the time, Pallas kernels for 0%

profile of v4, /device:TPU:0, one launch (start us, length us, event | category | flops | bytes accessed | tf_op | source)
XLA Modules:
  0.0 83.6 jit_solution(289317701989833321)
XLA Ops:
  0.6 0.9 %copy-done.2 = bf16[256,512]{1,0:T(8,128)(2,1)S(1)} copy-done((bf16[256,512]{1,0:T(8,128)(2,1)S(1)}, bf16[256,512]{1,0:T(8,128)(2,1)}, u32[]{:S(2)}) %copy-start.2) | copy-done | bytes 262168
  1.6 0.9 %copy-done.3 = bf16[256,512]{1,0:T(8,128)(2,1)S(1)} copy-done((bf16[256,512]{1,0:T(8,128)(2,1)S(1)}, bf16[256,512]{1,0:T(8,128)(2,1)}, u32[]{:S(2)}) %copy-start.3) | copy-done | bytes 262168
  2.5 0.7 copy-done.4
  3.2 0.7 copy-done.5
  4.0 3.0 %collective-permute-start.1 = (bf16[264,1024]{1,0:T(8,128)(2,1)S(1)}, bf16[264,1024]{1,0:T(8,128)(2,1)S(1)}, u32[]{:S(2)}, u32[]{:S(2)}) collective-permute-start(bf16[264,1024]{1,0:T(8,128)(2,1)S(1)} %get-tuple-element.26.own_ref), channel_id=1, source_target_pairs={{0,2},{1,3},{2,4},{3,5},{4,6},{5,7},{6,8},{7,9},{8,10},{9,11},{10,... | collective-permute-start | bytes 1622024 | tf_op jit(solution)/shard_map/ppermute | solution.py:25
  7.0 1.5 %collective-permute-start = (bf16[264,1024]{1,0:T(8,128)(2,1)S(1)}, bf16[264,1024]{1,0:T(8,128)(2,1)S(1)}, u32[]{:S(2)}, u32[]{:S(2)}) collective-permute-start(bf16[264,1024]{1,0:T(8,128)(2,1)S(1)} %get-tuple-element.26.own_ref), channel_id=1, source_target_pairs={{0,1},{2,3},{4,5},{6,7},{8,9},{10,11},{12,13},{14,15},{1,4},{3,6},... | collective-permute-start | bytes 1622024 | tf_op jit(solution)/shard_map/ppermute | solution.py:25
  8.5 2.2 %collective-permute-start.3 = (bf16[4,1024]{1,0:T(4,128)(2,1)S(1)}, bf16[4,1024]{1,0:T(4,128)(2,1)S(1)}, u32[]{:S(2)}, u32[]{:S(2)}) collective-permute-start(bf16[4,1024]{1,0:T(4,128)(2,1)S(1)} %get-tuple-element.27.mine_ref), channel_id=1, source_target_pairs={{0,1},{1,0},{2,3},{3,2},{4,5},{5,4},{6,7},{7,6},{8,9},{9,8},{10,11... | collective-permute-start | bytes 24584 | tf_op jit(solution)/shard_map/ppermute | solution.py:25
  10.7 0.9 %select_reduce_fusion = (s32[4]{0:T(128)S(1)}, s32[4]{0:T(128)S(1)}) fusion(s32[16]{0:T(128)} %bitcast.9, s32[4]{0:T(128)S(1)} %fusion.10, pred[16]{0:T(512)(128)(4,1)S(1)} %iota_compare_fusion.2), kind=kLoop, calls=%fused_computation.12 | loop fusion | flops 440 | bytes 128 | tf_op jit(solution)/shard_map/reduce_sum | solution.py:315
  11.5 0.7 broadcast_select_fusion.1
  12.4 0.7 subtract_bitcast_fusion
  13.4 1.6 %collective-permute-start.4 = (bf16[8,1024]{1,0:T(8,128)(2,1)S(1)}, bf16[8,1024]{1,0:T(8,128)(2,1)S(1)}, u32[]{:S(2)}, u32[]{:S(2)}) collective-permute-start(bf16[8,1024]{1,0:T(8,128)(2,1)S(1)} %pad_maximum_fusion), channel_id=1, source_target_pairs={{0,4},{1,11},{2,6},{3,13},{4,8},{5,15},{6,10},{7,1},{8,12},{9,3},{... | collective-permute-start | bytes 49160 | tf_op jit(solution)/shard_map/ppermute | solution.py:25
  15.0 1.1 %collective-permute-start.6 = (bf16[8,1024]{1,0:T(8,128)(2,1)S(1)}, bf16[8,1024]{1,0:T(8,128)(2,1)S(1)}, u32[]{:S(2)}, u32[]{:S(2)}) collective-permute-start(bf16[8,1024]{1,0:T(8,128)(2,1)S(1)} %pad_maximum_fusion), channel_id=1, source_target_pairs={{0,8},{1,15},{2,10},{3,1},{4,12},{5,3},{6,14},{7,5},{8,0},{9,7},{1... | collective-permute-start | bytes 49160 | tf_op jit(solution)/shard_map/ppermute | solution.py:25
  16.1 2.7 %collective-permute-start.5 = (bf16[8,1024]{1,0:T(8,128)(2,1)S(1)}, bf16[8,1024]{1,0:T(8,128)(2,1)S(1)}, u32[]{:S(2)}, u32[]{:S(2)}) collective-permute-start(bf16[8,1024]{1,0:T(8,128)(2,1)S(1)} %pad_maximum_fusion), channel_id=1, source_target_pairs={{0,6},{1,13},{2,8},{3,15},{4,10},{5,1},{6,12},{7,3},{8,14},{9,5},{... | collective-permute-start | bytes 49160 | tf_op jit(solution)/shard_map/ppermute | solution.py:25
  19.0 4.5 %collective-permute-done.5 = bf16[8,1024]{1,0:T(8,128)(2,1)S(1)} collective-permute-done((bf16[8,1024]{1,0:T(8,128)(2,1)S(1)}, bf16[8,1024]{1,0:T(8,128)(2,1)S(1)}, u32[]{:S(2)}, u32[]{:S(2)}) %collective-permute-start.5) | collective-permute-done | bytes 16416 | tf_op jit(solution)/shard_map/ppermute | solution.py:25
  24.0 2.0 %fusion = (f32[1088,128]{1,0:T(8,128)S(1)}, f32[1088,128]{1,0:T(8,128)S(1)}) fusion(f32[128]{0:T(128)S(1)} %get-tuple-element.54, f32[128]{0:T(128)S(1)} %get-tuple-element.55, f32[1088]{0:T(1024)S(1)} %add_convert_fusion), kind=kLoop, calls=%fused_computation.2 | loop fusion | flops 278528 | bytes 1119488 | tf_op jit(solution)/shard_map/mul | solution.py:37
  26.2 1.3 %copy-done.1 = bf16[256,2560]{1,0:T(8,128)(2,1)S(1)} copy-done((bf16[256,2560]{1,0:T(8,128)(2,1)S(1)}, bf16[256,2560]{1,0:T(8,128)(2,1)}, u32[]{:S(2)}) %copy-start.1) | copy-done | bytes 1310744
  27.5 26.2 %attend.1 = (bf16[256,2560]{1,0:T(8,128)(2,1)}, bf16[256,2560]{1,0:T(8,128)(2,1)}, f32[256,1024]{1,0:T(8,128)S(1)}, bf16[256,1024]{1,0:T(8,128)(2,1)S(1)}, f32[2...) custom-call(s32[3]{0:T(128)S(1)} %slice.3.seen, bf16[256,2560]{1,0:T(8,128)(2,1)S(1)} %copy-done, ...), custom_call_target="tpu_custom_call" | custom-call | tf_op jit(solution)/shard_map/attend/pallas_call | solution.py:182
  53.8 2.8 %collective-permute-done.9.r3_ref = f32[288,1024]{1,0:T(8,128)S(1)} collective-permute-done((f32[288,1024]{1,0:T(8,128)S(1)}, f32[288,1024]{1,0:T(8,128)S(1)}, u32[]{:S(2)}, u32[]{:S(2)}) %collective-permute-start.9) | collective-permute-done | bytes 1179680 | tf_op jit(solution)/shard_map/ppermute | solution.py:25
  56.7 6.7 %collective-permute-start.10 = (bf16[264,1024]{1,0:T(8,128)(2,1)S(1)}, bf16[264,1024]{1,0:T(8,128)(2,1)S(1)}, u32[]{:S(2)}, u32[]{:S(2)}) collective-permute-start(bf16[264,1024]{1,0:T(8,128)(2,1)S(1)} %get-tuple-element.35), channel_id=1, source_target_pairs={{2,0},{3,1},{4,2},{5,3},{6,4},{7,5},{8,6},{9,7},{10,8},{11,9},{12,... | collective-permute-start | bytes 1622024 | tf_op jit(solution)/shard_map/ppermute | solution.py:25
  63.4 1.3 %collective-permute-start.8 = (bf16[256,1024]{1,0:T(8,128)(2,1)S(1)}, bf16[256,1024]{1,0:T(8,128)(2,1)S(1)}, u32[]{:S(2)}, u32[]{:S(2)}) collective-permute-start(bf16[256,1024]{1,0:T(8,128)(2,1)S(1)} %get-tuple-element.31), channel_id=1, source_target_pairs={{1,0},{3,2},{5,4},{7,6},{9,8},{11,10},{13,12},{15,14},{4,1},{6,3},... | collective-permute-start | bytes 1572872 | tf_op jit(solution)/shard_map/ppermute | solution.py:25
  65.3 4.4 %collective-permute-start.13 = (f32[8,1024]{1,0:T(8,128)S(1)}, f32[8,1024]{1,0:T(8,128)S(1)}, u32[]{:S(2)}, u32[]{:S(2)}) collective-permute-start(f32[8,1024]{1,0:T(8,128)S(1)} %get-tuple-element.39), channel_id=1, source_target_pairs={{8,0},{15,1},{10,2},{1,3},{12,4},{3,5},{14,6},{5,7},{0,8},{7,9},{2... | collective-permute-start | bytes 98312 | tf_op jit(solution)/shard_map/ppermute | solution.py:25
  69.6 11.6 %collective-permute-done.11.refs_0_ = f32[8,1024]{1,0:T(8,128)S(1)} collective-permute-done((f32[8,1024]{1,0:T(8,128)S(1)}, f32[8,1024]{1,0:T(8,128)S(1)}, u32[]{:S(2)}, u32[]{:S(2)}) %collective-permute-start.11) | collective-permute-done | bytes 32800 | tf_op jit(solution)/shard_map/ppermute | solution.py:25
  81.3 1.2 %collective-permute-done.14.got_ref = f32[4,1024]{1,0:T(4,128)S(1)} collective-permute-done((f32[4,1024]{1,0:T(4,128)S(1)}, f32[4,1024]{1,0:T(4,128)S(1)}, u32[]{:S(2)}, u32[]{:S(2)}) %collective-permute-start.14) | collective-permute-done | bytes 16416 | tf_op jit(solution)/shard_map/ppermute | solution.py:25
  82.5 1.2 %finish.1 = (bf16[256,512]{1,0:T(8,128)(2,1)}, bf16[256,512]{1,0:T(8,128)(2,1)}, bf16[4,512]{1,0:T(4,128)(2,1)}, bf16[4,512]{1,0:T(4,128)(2,1)}) custom-call(f32[256,1024]{1,0:T(8,128)S(1)} %get-tuple-element.30.d0_ref, bf16[256,1024]{1,0:T(8,128)(2,1)S(1)} %collective-permute-done.8.r1_ref, bf16[264,1024]{1,0:T(8,128)(2,1)S(1)} %collective-permute-done.10.r2_ref, ...), custom_call_target="tpu_custom_call" | custom-call | tf_op jit(solution)/shard_map/finish/pallas_call | solution.py:275
  (46 shorter events, 2.2 us)
Async XLA Ops:
  0.6 1.0 %copy-start.2 = (bf16[256,512]{1,0:T(8,128)(2,1)S(1)}, bf16[256,512]{1,0:T(8,128)(2,1)}, u32[]{:S(2)}) copy-start(bf16[256,512]{1,0:T(8,128)(2,1)} %k_ref.1) | copy-start | bytes 786436
  1.6 0.9 %copy-start.3 = (bf16[256,512]{1,0:T(8,128)(2,1)S(1)}, bf16[256,512]{1,0:T(8,128)(2,1)}, u32[]{:S(2)}) copy-start(bf16[256,512]{1,0:T(8,128)(2,1)} %v_ref.1) | copy-start | bytes 786436
  2.5 0.7 copy-start.4
  3.2 0.7 copy-start.5
  3.9 22.2 %copy-start = (bf16[256,2560]{1,0:T(8,128)(2,1)S(1)}, bf16[256,2560]{1,0:T(8,128)(2,1)}, u32[]{:S(2)}) copy-start(bf16[256,2560]{1,0:T(8,128)(2,1)} %q_ref.1) | copy-start | bytes 3932164
  4.0 19.6 %collective-permute-start.1 = (bf16[264,1024]{1,0:T(8,128)(2,1)S(1)}, bf16[264,1024]{1,0:T(8,128)(2,1)S(1)}, u32[]{:S(2)}, u32[]{:S(2)}) collective-permute-start(bf16[264,1024]{1,0:T(8,128)(2,1)S(1)} %get-tuple-element.26.own_ref), channel_id=1, source_target_pairs={{0,2},{1,3},{2,4},{3,5},{4,6},{5,7},{6,8},{7,9},{8,10},{9,11},{10,... | collective-permute-start | bytes 1622024 | tf_op jit(solution)/shard_map/ppermute | solution.py:25
  7.0 19.2 %collective-permute-start = (bf16[264,1024]{1,0:T(8,128)(2,1)S(1)}, bf16[264,1024]{1,0:T(8,128)(2,1)S(1)}, u32[]{:S(2)}, u32[]{:S(2)}) collective-permute-start(bf16[264,1024]{1,0:T(8,128)(2,1)S(1)} %get-tuple-element.26.own_ref), channel_id=1, source_target_pairs={{0,1},{2,3},{4,5},{6,7},{8,9},{10,11},{12,13},{14,15},{1,4},{3,6},... | collective-permute-start | bytes 1622024 | tf_op jit(solution)/shard_map/ppermute | solution.py:25
  8.5 4.9 %collective-permute-start.3 = (bf16[4,1024]{1,0:T(4,128)(2,1)S(1)}, bf16[4,1024]{1,0:T(4,128)(2,1)S(1)}, u32[]{:S(2)}, u32[]{:S(2)}) collective-permute-start(bf16[4,1024]{1,0:T(4,128)(2,1)S(1)} %get-tuple-element.27.mine_ref), channel_id=1, source_target_pairs={{0,1},{1,0},{2,3},{3,2},{4,5},{5,4},{6,7},{7,6},{8,9},{9,8},{10,11... | collective-permute-start | bytes 24584 | tf_op jit(solution)/shard_map/ppermute | solution.py:25
  13.4 5.6 %collective-permute-start.4 = (bf16[8,1024]{1,0:T(8,128)(2,1)S(1)}, bf16[8,1024]{1,0:T(8,128)(2,1)S(1)}, u32[]{:S(2)}, u32[]{:S(2)}) collective-permute-start(bf16[8,1024]{1,0:T(8,128)(2,1)S(1)} %pad_maximum_fusion), channel_id=1, source_target_pairs={{0,4},{1,11},{2,6},{3,13},{4,8},{5,15},{6,10},{7,1},{8,12},{9,3},{... | collective-permute-start | bytes 49160 | tf_op jit(solution)/shard_map/ppermute | solution.py:25
  15.0 8.5 %collective-permute-start.6 = (bf16[8,1024]{1,0:T(8,128)(2,1)S(1)}, bf16[8,1024]{1,0:T(8,128)(2,1)S(1)}, u32[]{:S(2)}, u32[]{:S(2)}) collective-permute-start(bf16[8,1024]{1,0:T(8,128)(2,1)S(1)} %pad_maximum_fusion), channel_id=1, source_target_pairs={{0,8},{1,15},{2,10},{3,1},{4,12},{5,3},{6,14},{7,5},{8,0},{9,7},{1... | collective-permute-start | bytes 49160 | tf_op jit(solution)/shard_map/ppermute | solution.py:25
  16.1 7.4 %collective-permute-start.5 = (bf16[8,1024]{1,0:T(8,128)(2,1)S(1)}, bf16[8,1024]{1,0:T(8,128)(2,1)S(1)}, u32[]{:S(2)}, u32[]{:S(2)}) collective-permute-start(bf16[8,1024]{1,0:T(8,128)(2,1)S(1)} %pad_maximum_fusion), channel_id=1, source_target_pairs={{0,6},{1,13},{2,8},{3,15},{4,10},{5,1},{6,12},{7,3},{8,14},{9,5},{... | collective-permute-start | bytes 49160 | tf_op jit(solution)/shard_map/ppermute | solution.py:25
  23.5 2.6 %collective-permute-start.2 = (bf16[264,1024]{1,0:T(8,128)(2,1)S(1)}, bf16[264,1024]{1,0:T(8,128)(2,1)S(1)}, u32[]{:S(2)}, u32[]{:S(2)}) collective-permute-start(bf16[264,1024]{1,0:T(8,128)(2,1)S(1)} %collective-permute-done.1.w2_ref), channel_id=1, source_target_pairs={{0,1},{1,0},{2,3},{3,2},{4,5},{5,4},{6,7},{7,6},{8,9},{9,8},{10,11... | collective-permute-start | bytes 1622024 | tf_op jit(solution)/shard_map/ppermute | solution.py:25
  23.6 2.6 %collective-permute-start.7 = (bf16[24,1024]{1,0:T(8,128)(2,1)S(1)}, bf16[24,1024]{1,0:T(8,128)(2,1)S(1)}, u32[]{:S(2)}, u32[]{:S(2)}) collective-permute-start(bf16[24,1024]{1,0:T(8,128)(2,1)S(1)} %constant_dynamic-update-slice_fusion.near_ref), channel_id=1, source_target_pairs={{0,1},{1,0},{2,3},{3,2},{4,5},{5,4},{6,7},{7,6},{8,9},{9,8},{10,11... | collective-permute-start | bytes 147464 | tf_op jit(solution)/shard_map/ppermute | solution.py:25
  26.2 1.3 %copy-start.1 = (bf16[256,2560]{1,0:T(8,128)(2,1)S(1)}, bf16[256,2560]{1,0:T(8,128)(2,1)}, u32[]{:S(2)}) copy-start(bf16[256,2560]{1,0:T(8,128)(2,1)} %g_ref.1) | copy-start | bytes 3932164
  53.7 2.8 %collective-permute-start.9 = (f32[288,1024]{1,0:T(8,128)S(1)}, f32[288,1024]{1,0:T(8,128)S(1)}, u32[]{:S(2)}, u32[]{:S(2)}) collective-permute-start(f32[288,1024]{1,0:T(8,128)S(1)} %get-tuple-element.33), channel_id=1, source_target_pairs={{0,1},{1,0},{2,3},{3,2},{4,5},{5,4},{6,7},{7,6},{8,9},{9,8},{10,11... | collective-permute-start | bytes 3538952 | tf_op jit(solution)/shard_map/ppermute | solution.py:25
  56.7 25.8 %collective-permute-start.10 = (bf16[264,1024]{1,0:T(8,128)(2,1)S(1)}, bf16[264,1024]{1,0:T(8,128)(2,1)S(1)}, u32[]{:S(2)}, u32[]{:S(2)}) collective-permute-start(bf16[264,1024]{1,0:T(8,128)(2,1)S(1)} %get-tuple-element.35), channel_id=1, source_target_pairs={{2,0},{3,1},{4,2},{5,3},{6,4},{7,5},{8,6},{9,7},{10,8},{11,9},{12,... | collective-permute-start | bytes 1622024 | tf_op jit(solution)/shard_map/ppermute | solution.py:25
  63.4 17.9 %collective-permute-start.8 = (bf16[256,1024]{1,0:T(8,128)(2,1)S(1)}, bf16[256,1024]{1,0:T(8,128)(2,1)S(1)}, u32[]{:S(2)}, u32[]{:S(2)}) collective-permute-start(bf16[256,1024]{1,0:T(8,128)(2,1)S(1)} %get-tuple-element.31), channel_id=1, source_target_pairs={{1,0},{3,2},{5,4},{7,6},{9,8},{11,10},{13,12},{15,14},{4,1},{6,3},... | collective-permute-start | bytes 1572872 | tf_op jit(solution)/shard_map/ppermute | solution.py:25
  64.7 16.6 %collective-permute-start.11 = (f32[8,1024]{1,0:T(8,128)S(1)}, f32[8,1024]{1,0:T(8,128)S(1)}, u32[]{:S(2)}, u32[]{:S(2)}) collective-permute-start(f32[8,1024]{1,0:T(8,128)S(1)} %get-tuple-element.37), channel_id=1, source_target_pairs={{4,0},{11,1},{6,2},{13,3},{8,4},{15,5},{10,6},{1,7},{12,8},{3,9},{... | collective-permute-start | bytes 98312 | tf_op jit(solution)/shard_map/ppermute | solution.py:25
  65.2 16.0 %collective-permute-start.12 = (f32[8,1024]{1,0:T(8,128)S(1)}, f32[8,1024]{1,0:T(8,128)S(1)}, u32[]{:S(2)}, u32[]{:S(2)}) collective-permute-start(f32[8,1024]{1,0:T(8,128)S(1)} %get-tuple-element.38), channel_id=1, source_target_pairs={{6,0},{13,1},{8,2},{15,3},{10,4},{1,5},{12,6},{3,7},{14,8},{5,9},{... | collective-permute-start | bytes 98312 | tf_op jit(solution)/shard_map/ppermute | solution.py:25
  65.3 16.0 %collective-permute-start.13 = (f32[8,1024]{1,0:T(8,128)S(1)}, f32[8,1024]{1,0:T(8,128)S(1)}, u32[]{:S(2)}, u32[]{:S(2)}) collective-permute-start(f32[8,1024]{1,0:T(8,128)S(1)} %get-tuple-element.39), channel_id=1, source_target_pairs={{8,0},{15,1},{10,2},{1,3},{12,4},{3,5},{14,6},{5,7},{0,8},{7,9},{2... | collective-permute-start | bytes 98312 | tf_op jit(solution)/shard_map/ppermute | solution.py:25
  81.2 1.2 %collective-permute-start.14 = (f32[4,1024]{1,0:T(4,128)S(1)}, f32[4,1024]{1,0:T(4,128)S(1)}, u32[]{:S(2)}, u32[]{:S(2)}) collective-permute-start(f32[4,1024]{1,0:T(4,128)S(1)} %get-tuple-element.41), channel_id=1, source_target_pairs={{0,1},{1,0},{2,3},{3,2},{4,5},{5,4},{6,7},{7,6},{8,9},{9,8},{10,11... | collective-permute-start | bytes 49160 | tf_op jit(solution)/shard_map/ppermute | solution.py:25

commit v5 on v4

--- a/solution.py
+++ b/solution.py
@@ -21,6 +21,10 @@
 bf16 = jnp.bfloat16
 
 
+def in_hbm(value):
+    return pltpu.with_memory_space_constraint(value, pltpu.HBM)
+
+
 def permute(value, pairs):
     return lax.ppermute(value, "ctx", pairs)
 
@@ -46,29 +50,46 @@
 
 
 IN_VMEM = pl.BlockSpec(memory_space=pltpu.VMEM)
-
-
-def pack_kernel(k_ref, v_ref, pk_ref, pv_ref, own_ref, mine_ref):
-    rows, few = k_ref.shape[0], pk_ref.shape[0]
-    own_ref[:rows, :WIDTH] = k_ref[...]
-    own_ref[:rows, WIDTH:] = v_ref[...]
-    mine_ref[:, :WIDTH] = pk_ref[...]
-    mine_ref[:, WIDTH:] = pv_ref[...]
+IN_HBM = pl.BlockSpec(memory_space=pltpu.HBM)
+
+
+def pack_kernel(k_ref, v_ref, pk_ref, pv_ref, own_ref, mine_ref, sems):
+    rows = k_ref.shape[0]
+    copies = [
+        pltpu.make_async_copy(src, dst, sems.at[i])
+        for i, (src, dst) in enumerate(
+            (
+                (pk_ref, mine_ref.at[:, :WIDTH]),
+                (pv_ref, mine_ref.at[:, WIDTH:]),
+                (k_ref, own_ref.at[:rows, :WIDTH]),
+                (v_ref, own_ref.at[:rows, WIDTH:]),
+            )
+        )
+    ]
+    for copy in copies:
+        copy.start()
+    copies[0].wait()
+    copies[1].wait()
     twice = jnp.concatenate([mine_ref[...].astype(f32)] * 2, axis=0)
     own_ref[rows:, :] = twice.astype(bf16)
+    copies[2].wait()
+    copies[3].wait()
 
 
 def pack(keys, values, prompt_keys, prompt_values):
+    rows = keys.shape[0] + 2 * prompt_keys.shape[0]
     return pl.pallas_call(
         pack_kernel,
+        in_specs=[IN_HBM] * 4,
         out_shape=[
-            jax.ShapeDtypeStruct((keys.shape[0] + 2 * prompt_keys.shape[0], 2 * WIDTH), bf16),
+            jax.ShapeDtypeStruct((rows, 2 * WIDTH), bf16),
             jax.ShapeDtypeStruct((prompt_keys.shape[0], 2 * WIDTH), bf16),
         ],
         out_specs=[IN_VMEM, IN_VMEM],
-        compiler_params=pltpu.CompilerParams(vmem_limit_bytes=6 * 2**20),
+        scratch_shapes=[pltpu.SemaphoreType.DMA((4,))],
+        compiler_params=pltpu.CompilerParams(vmem_limit_bytes=4 * 2**20),
         name="pack",
-    )(keys, values, prompt_keys, prompt_values)
+    )(*(in_hbm(x) for x in (keys, values, prompt_keys, prompt_values)))
 
 
 def attend_kernel(
@@ -194,16 +215,20 @@
         + [jax.ShapeDtypeStruct((r, wide), t) for r, t in outs],
         compiler_params=pltpu.CompilerParams(vmem_limit_bytes=40 * 2**20),
         name="attend",
-    )(seen, queries, grads, cosine, sine, *blocks, *prompts)
-
-
-def merge_kernel(d2_ref, r3_ref, dp_ref, x2_ref, keep_ref, *outs):
+    )(seen, in_hbm(queries), in_hbm(grads), cosine, sine, *blocks, *prompts)
+
+
+def merge_kernel(d2_ref, r3_ref, dp_ref, xk_ref, xv_ref, keep_ref, *outs):
     rows, few = d2_ref.shape[0], keep_ref.shape[0]
-    x2_ref[:rows, :] = (d2_ref[...] + r3_ref[:rows, :]).astype(bf16)
+    x2 = (d2_ref[...] + r3_ref[:rows, :]).astype(bf16)
+    xk_ref[:rows, :] = x2[:, :WIDTH]
+    xv_ref[:rows, :] = x2[:, WIDTH:]
     keep_ref[...] = dp_ref[:few, :] + r3_ref[rows : rows + few, :]
     near = dp_ref[few : 2 * few, :] + r3_ref[rows + few : rows + 2 * few, :]
     high = near.astype(bf16).astype(f32)
-    x2_ref[rows:, :] = jnp.concatenate([high, near - high], axis=0).astype(bf16)
+    pair = jnp.concatenate([high, near - high], axis=0).astype(bf16)
+    xk_ref[rows:, :] = pair[:, :WIDTH]
+    xv_ref[rows:, :] = pair[:, WIDTH:]
     for j, out in enumerate(outs):
         step = out.shape[0]
         at = 2 * few + j * step
@@ -215,9 +240,10 @@
     return pl.pallas_call(
         merge_kernel,
         in_specs=[IN_VMEM] * 3,
-        out_specs=[IN_VMEM] * (2 + pieces),
+        out_specs=[IN_VMEM] * (3 + pieces),
         out_shape=[
-            jax.ShapeDtypeStruct((rows + 2 * few, wide), bf16),
+            jax.ShapeDtypeStruct((rows + 2 * few, WIDTH), bf16),
+            jax.ShapeDtypeStruct((rows + 2 * few, WIDTH), bf16),
             jax.ShapeDtypeStruct((few, wide), f32),
         ]
         + [jax.ShapeDtypeStruct((2 * few, wide), f32)] * pieces,
@@ -226,7 +252,7 @@
     )(d2, r3, dp)
 
 
-def tally_kernel(*refs):
+def tally_kernel(after_ref, *refs):
     terms, keep_ref, send_ref = refs[:-2], refs[-2], refs[-1]
     few = keep_ref.shape[0]
     total = terms[0][...]
@@ -236,20 +262,20 @@
     send_ref[...] = total[few:]
 
 
-def tally(terms):
+def tally(after, terms):
     few, wide = terms[0].shape
     return pl.pallas_call(
         tally_kernel,
-        in_specs=[IN_VMEM] * len(terms),
+        in_specs=[IN_VMEM] * (1 + len(terms)),
         out_specs=[IN_VMEM] * 2,
         out_shape=[jax.ShapeDtypeStruct((few // 2, wide), f32)] * 2,
         compiler_params=pltpu.CompilerParams(vmem_limit_bytes=2 * 2**20),
         name="tally",
-    )(*terms)
+    )(after, *terms)
 
 
 def finish_kernel(
-    d0_ref, r1_ref, r2_ref, cos_ref, sin_ref, keep_ref, sum_ref, got_ref,
+    d0_ref, r1_ref, rk_ref, rv_ref, cos_ref, sin_ref, keep_ref, sum_ref, got_ref,
     gk_ref, gv_ref, gpk_ref, gpv_ref,
 ):
     rows = d0_ref.shape[0]
@@ -260,25 +286,25 @@
     for h in range(KVH):
         at = slice(h * HD, (h + 1) * HD)
         vat = slice(WIDTH + h * HD, WIDTH + (h + 1) * HD)
-        for cols, out in ((at, gk_ref), (vat, gv_ref)):
-            total = d0_ref[:, cols] + (r1_ref[:, cols].astype(f32) + r2_ref[:rows, cols].astype(f32))
+        for cols, r2_ref, out in ((at, rk_ref, gk_ref), (vat, rv_ref, gv_ref)):
+            total = d0_ref[:, cols] + (r1_ref[:, cols].astype(f32) + r2_ref[:rows, at].astype(f32))
             out[:, at] = (turn(total, cosine, sine) if out is gk_ref else total).astype(bf16)
-        for cols, out in ((at, gpk_ref), (vat, gpv_ref)):
-            pair = r2_ref[rows:, cols].astype(f32)
+        for cols, r2_ref, out in ((at, rk_ref, gpk_ref), (vat, rv_ref, gpv_ref)):
+            pair = r2_ref[rows:, at].astype(f32)
             total = keep_ref[:, cols] + (pair[:few] + pair[few:])
             total = total + (sum_ref[:, cols] + got_ref[:, cols])
             out[:, at] = (turn(total, pcos, psin) if out is gpk_ref else total).astype(bf16)
 
 
-def finish(d0, r1, r2, cosine, sine, keep, tallied, got):
+def finish(d0, r1, rk, rv, cosine, sine, keep, tallied, got):
     rows, few = d0.shape[0], keep.shape[0]
     return pl.pallas_call(
         finish_kernel,
-        in_specs=[IN_VMEM] * 8,
+        in_specs=[IN_VMEM] * 9,
         out_shape=[jax.ShapeDtypeStruct((r, WIDTH), bf16) for r in (rows, rows, few, few)],
         compiler_params=pltpu.CompilerParams(vmem_limit_bytes=6 * 2**20),
         name="finish",
-    )(d0, r1, r2, cosine, sine, keep, tallied, got)
+    )(d0, r1, rk, rv, cosine, sine, keep, tallied, got)
 
 
 def local(
@@ -332,12 +358,14 @@
     )
     r3 = permute(d3, swap)
     r1 = permute(d1, back(across))
-    x2, keep, *terms = merge(d2, r3, dp, few, turns)
-    r2 = permute(x2, back(ahead))
-    tallied, send = tally([permute(t, back(p)) for t, p in zip(terms, rounds)])
+    xk, xv, keep, *terms = merge(d2, r3, dp, few, turns)
+    rk = permute(xk, back(ahead))
+    sums = [permute(t, back(p)) for t, p in zip(terms, rounds)]
+    rv = permute(lax.optimization_barrier((xv, *sums))[0], back(ahead))
+    tallied, send = tally(r1, sums)
     got = permute(send, swap)
     grad_keys, grad_values, grad_prompt_keys, grad_prompt_values = finish(
-        d0, r1, r2, cosine, sine, keep, tallied, got
+        d0, r1, rk, rv, cosine, sine, keep, tallied, got
     )
     return (attended, grad_queries, grad_keys, grad_values, grad_prompt_keys, grad_prompt_values)
 

time: 84.5 us -> 78.7 us (0.931)
  waiting for transfers between devices: 20.2 us -> 14.9 us
  local copies, waits for them, and re-layouts: 4.85 us -> 0.27 us
  starting transfers between devices: 25.7 us -> 27.9 us
  Pallas kernels: 27.6 us -> 29.5 us
    ppermute x15 -> x16, waiting for transfers between devices: 20.2 us -> 14.9 us  [permute(): return lax.ppermute(value, 'ctx', pairs)]
    unnamed x15 -> x3, local copies, waits for them, and re-layouts: 4.59 us -> 0.01 us
    ppermute x15 -> x16, starting transfers between devices: 25.7 us -> 27.9 us  [permute(): return lax.ppermute(value, 'ctx', pairs)]
    pallas_call x3, Pallas kernels: 1.21 us -> 2.23 us  [the longest x1 1.12 us: finish(): pl.pallas_call(finish_kernel, in_specs=[IN_VMEM] * 9, out_shape=[jax.Shap...]
    pallas_call x1, Pallas kernels: 26.2 us -> 27.2 us  [attend(): pl.pallas_call(attend_kernel, grid_spec=pltpu.PrefetchScalarGridSpec(num_...]
  transfers between devices with their start and end apart: 15 -> 16, of which waited for: 5 -> 7; matrix products, arithmetic and copies ran while one was open for 6% -> 6% of each run, Pallas kernels for 0% -> 0%
where the time goes in v5:
time: 78.7 us; the launch traced here: 77.9 us
  Pallas kernels  29.5 us (37%)
  starting transfers between devices  27.9 us (35%)
  waiting for transfers between devices  14.9 us (19%)
  other arithmetic  4.53 us (6%)
    ppermute x16, starting transfers between devices, permute(): return lax.ppermute(value, 'ctx', pairs)  27.9 us
    pallas_call x1, Pallas kernels, attend(): pl.pallas_call(attend_kernel, grid_spec=pltpu.PrefetchScalarGridSpec(num_...  27.2 us
    ppermute x16, waiting for transfers between devices, permute(): return lax.ppermute(value, 'ctx', pairs)  14.9 us
    mul x1, other arithmetic, angle_tables(): return (jnp.cos(angles), jnp.sin(angles) * sign[None, :])  2.01 us
  transfers between devices with their start and end apart: 16, of which 7 were waited for; matrix products, arithmetic and copies ran while one was open for 6% of the time, Pallas kernels for 0%

profile of v5, /device:TPU:0, one launch (start us, length us, event | category | flops | bytes accessed | tf_op | source)
XLA Modules:
  0.0 77.9 jit_solution(4470552142501612547)
XLA Ops:
  0.6 1.1 %pack.1 = (bf16[264,1024]{1,0:T(8,128)(2,1)S(1)}, bf16[4,1024]{1,0:T(4,128)(2,1)S(1)}) custom-call(bf16[256,512]{1,0:T(8,128)(2,1)} %k_ref.1, bf16[256,512]{1,0:T(8,128)(2,1)} %v_ref.1, bf16[4,512]{1,0:T(4,128)(2,1)} %pk_ref.1, bf16[4,512]{1,0:T(4,128)(2,1)} %pv_ref.1), custom_call_target="tpu_custom_call" | custom-call | tf_op jit(solution)/shard_map/pack/pallas_call | solution.py:81
  1.7 3.0 %collective-permute-start.1 = (bf16[264,1024]{1,0:T(8,128)(2,1)S(1)}, bf16[264,1024]{1,0:T(8,128)(2,1)S(1)}, u32[]{:S(2)}, u32[]{:S(2)}) collective-permute-start(bf16[264,1024]{1,0:T(8,128)(2,1)S(1)} %get-tuple-element.28.own_ref), channel_id=1, source_target_pairs={{0,2},{1,3},{2,4},{3,5},{4,6},{5,7},{6,8},{7,9},{8,10},{9,11},{10,... | collective-permute-start | bytes 1622024 | tf_op jit(solution)/shard_map/ppermute | solution.py:29
  4.8 1.5 %collective-permute-start = (bf16[264,1024]{1,0:T(8,128)(2,1)S(1)}, bf16[264,1024]{1,0:T(8,128)(2,1)S(1)}, u32[]{:S(2)}, u32[]{:S(2)}) collective-permute-start(bf16[264,1024]{1,0:T(8,128)(2,1)S(1)} %get-tuple-element.28.own_ref), channel_id=1, source_target_pairs={{0,1},{2,3},{4,5},{6,7},{8,9},{10,11},{12,13},{14,15},{1,4},{3,6},... | collective-permute-start | bytes 1622024 | tf_op jit(solution)/shard_map/ppermute | solution.py:29
  6.2 2.2 %collective-permute-start.3 = (bf16[4,1024]{1,0:T(4,128)(2,1)S(1)}, bf16[4,1024]{1,0:T(4,128)(2,1)S(1)}, u32[]{:S(2)}, u32[]{:S(2)}) collective-permute-start(bf16[4,1024]{1,0:T(4,128)(2,1)S(1)} %get-tuple-element.29.mine_ref), channel_id=1, source_target_pairs={{0,1},{1,0},{2,3},{3,2},{4,5},{5,4},{6,7},{7,6},{8,9},{9,8},{10,11... | collective-permute-start | bytes 24584 | tf_op jit(solution)/shard_map/ppermute | solution.py:29
  8.4 0.9 %select_reduce_fusion = (s32[4]{0:T(128)S(1)}, s32[4]{0:T(128)S(1)}) fusion(s32[16]{0:T(128)} %bitcast.9, s32[4]{0:T(128)S(1)} %fusion.10, pred[16]{0:T(512)(128)(4,1)S(1)} %iota_compare_fusion.2), kind=kLoop, calls=%fused_computation.12 | loop fusion | flops 440 | bytes 128 | tf_op jit(solution)/shard_map/reduce_sum | solution.py:341
  9.3 0.7 broadcast_select_fusion.1
  10.2 0.7 subtract_bitcast_fusion
  11.2 1.6 %collective-permute-start.4 = (bf16[8,1024]{1,0:T(8,128)(2,1)S(1)}, bf16[8,1024]{1,0:T(8,128)(2,1)S(1)}, u32[]{:S(2)}, u32[]{:S(2)}) collective-permute-start(bf16[8,1024]{1,0:T(8,128)(2,1)S(1)} %pad_maximum_fusion), channel_id=1, source_target_pairs={{0,4},{1,11},{2,6},{3,13},{4,8},{5,15},{6,10},{7,1},{8,12},{9,3},{... | collective-permute-start | bytes 49160 | tf_op jit(solution)/shard_map/ppermute | solution.py:29
  12.8 1.1 %collective-permute-start.6 = (bf16[8,1024]{1,0:T(8,128)(2,1)S(1)}, bf16[8,1024]{1,0:T(8,128)(2,1)S(1)}, u32[]{:S(2)}, u32[]{:S(2)}) collective-permute-start(bf16[8,1024]{1,0:T(8,128)(2,1)S(1)} %pad_maximum_fusion), channel_id=1, source_target_pairs={{0,8},{1,15},{2,10},{3,1},{4,12},{5,3},{6,14},{7,5},{8,0},{9,7},{1... | collective-permute-start | bytes 49160 | tf_op jit(solution)/shard_map/ppermute | solution.py:29
  13.9 2.7 %collective-permute-start.5 = (bf16[8,1024]{1,0:T(8,128)(2,1)S(1)}, bf16[8,1024]{1,0:T(8,128)(2,1)S(1)}, u32[]{:S(2)}, u32[]{:S(2)}) collective-permute-start(bf16[8,1024]{1,0:T(8,128)(2,1)S(1)} %pad_maximum_fusion), channel_id=1, source_target_pairs={{0,6},{1,13},{2,8},{3,15},{4,10},{5,1},{6,12},{7,3},{8,14},{9,5},{... | collective-permute-start | bytes 49160 | tf_op jit(solution)/shard_map/ppermute | solution.py:29
  16.8 4.5 %collective-permute-done.5 = bf16[8,1024]{1,0:T(8,128)(2,1)S(1)} collective-permute-done((bf16[8,1024]{1,0:T(8,128)(2,1)S(1)}, bf16[8,1024]{1,0:T(8,128)(2,1)S(1)}, u32[]{:S(2)}, u32[]{:S(2)}) %collective-permute-start.5) | collective-permute-done | bytes 16416 | tf_op jit(solution)/shard_map/ppermute | solution.py:29
  21.8 2.0 %fusion = (f32[1088,128]{1,0:T(8,128)S(1)}, f32[1088,128]{1,0:T(8,128)S(1)}) fusion(f32[128]{0:T(128)S(1)} %get-tuple-element.58, f32[128]{0:T(128)S(1)} %get-tuple-element.59, f32[1088]{0:T(1024)S(1)} %add_convert_fusion), kind=kLoop, calls=%fused_computation.2 | loop fusion | flops 278528 | bytes 1119488 | tf_op jit(solution)/shard_map/mul | solution.py:41
  23.9 27.2 %attend.1 = (bf16[256,2560]{1,0:T(8,128)(2,1)}, bf16[256,2560]{1,0:T(8,128)(2,1)}, f32[256,1024]{1,0:T(8,128)S(1)}, bf16[256,1024]{1,0:T(8,128)(2,1)S(1)}, f32[2...) custom-call(s32[3]{0:T(128)S(1)} %slice.3.seen, bf16[256,2560]{1,0:T(8,128)(2,1)} %q_ref.1, ...), custom_call_target="tpu_custom_call" | custom-call | tf_op jit(solution)/shard_map/attend/pallas_call | solution.py:203
  51.2 1.3 %collective-permute-start.8 = (bf16[256,1024]{1,0:T(8,128)(2,1)S(1)}, bf16[256,1024]{1,0:T(8,128)(2,1)S(1)}, u32[]{:S(2)}, u32[]{:S(2)}) collective-permute-start(bf16[256,1024]{1,0:T(8,128)(2,1)S(1)} %get-tuple-element.33), channel_id=1, source_target_pairs={{1,0},{3,2},{5,4},{7,6},{9,8},{11,10},{13,12},{15,14},{4,1},{6,3},... | collective-permute-start | bytes 1572872 | tf_op jit(solution)/shard_map/ppermute | solution.py:29
  52.5 1.5 %collective-permute-done.9.r3_ref = f32[288,1024]{1,0:T(8,128)S(1)} collective-permute-done((f32[288,1024]{1,0:T(8,128)S(1)}, f32[288,1024]{1,0:T(8,128)S(1)}, u32[]{:S(2)}, u32[]{:S(2)}) %collective-permute-start.9) | collective-permute-done | bytes 1179680 | tf_op jit(solution)/shard_map/ppermute | solution.py:29
  54.1 6.6 %collective-permute-start.11 = (f32[8,1024]{1,0:T(8,128)S(1)}, f32[8,1024]{1,0:T(8,128)S(1)}, u32[]{:S(2)}, u32[]{:S(2)}) collective-permute-start(f32[8,1024]{1,0:T(8,128)S(1)} %get-tuple-element.39), channel_id=1, source_target_pairs={{4,0},{11,1},{6,2},{13,3},{8,4},{15,5},{10,6},{1,7},{12,8},{3,9},{... | collective-permute-start | bytes 98312 | tf_op jit(solution)/shard_map/ppermute | solution.py:29
  60.7 3.0 %collective-permute-start.13 = (f32[8,1024]{1,0:T(8,128)S(1)}, f32[8,1024]{1,0:T(8,128)S(1)}, u32[]{:S(2)}, u32[]{:S(2)}) collective-permute-start(f32[8,1024]{1,0:T(8,128)S(1)} %get-tuple-element.41), channel_id=1, source_target_pairs={{8,0},{15,1},{10,2},{1,3},{12,4},{3,5},{14,6},{5,7},{0,8},{7,9},{2... | collective-permute-start | bytes 98312 | tf_op jit(solution)/shard_map/ppermute | solution.py:29
  63.7 2.3 %collective-permute-start.10 = (bf16[264,512]{1,0:T(8,128)(2,1)S(1)}, bf16[264,512]{1,0:T(8,128)(2,1)S(1)}, u32[]{:S(2)}, u32[]{:S(2)}) collective-permute-start(bf16[264,512]{1,0:T(8,128)(2,1)S(1)} %get-tuple-element.37), channel_id=1, source_target_pairs={{2,0},{3,1},{4,2},{5,3},{6,4},{7,5},{8,6},{9,7},{10,8},{11,9},{12,... | collective-permute-start | bytes 811016 | tf_op jit(solution)/shard_map/ppermute | solution.py:29
  66.0 0.8 %collective-permute-done.12.refs_1_ = f32[8,1024]{1,0:T(8,128)S(1)} collective-permute-done((f32[8,1024]{1,0:T(8,128)S(1)}, f32[8,1024]{1,0:T(8,128)S(1)}, u32[]{:S(2)}, u32[]{:S(2)}) %collective-permute-start.12) | collective-permute-done | bytes 32800 | tf_op jit(solution)/shard_map/ppermute | solution.py:29
  66.8 2.0 %collective-permute-start.14 = (bf16[264,512]{1,0:T(8,128)(2,1)S(1)}, bf16[264,512]{1,0:T(8,128)(2,1)S(1)}, u32[]{:S(2)}, u32[]{:S(2)}) collective-permute-start(bf16[264,512]{1,0:T(8,128)(2,1)S(1)} %get-tuple-element.42), channel_id=1, source_target_pairs={{2,0},{3,1},{4,2},{5,3},{6,4},{7,5},{8,6},{9,7},{10,8},{11,9},{12,... | collective-permute-start | bytes 811016 | tf_op jit(solution)/shard_map/ppermute | solution.py:29
  68.9 1.2 %collective-permute-done.15.got_ref = f32[4,1024]{1,0:T(4,128)S(1)} collective-permute-done((f32[4,1024]{1,0:T(4,128)S(1)}, f32[4,1024]{1,0:T(4,128)S(1)}, u32[]{:S(2)}, u32[]{:S(2)}) %collective-permute-start.15) | collective-permute-done | bytes 16416 | tf_op jit(solution)/shard_map/ppermute | solution.py:29
  70.1 3.0 %collective-permute-done.10.rk_ref = bf16[264,512]{1,0:T(8,128)(2,1)S(1)} collective-permute-done((bf16[264,512]{1,0:T(8,128)(2,1)S(1)}, bf16[264,512]{1,0:T(8,128)(2,1)S(1)}, u32[]{:S(2)}, u32[]{:S(2)}) %collective-permute-start.10) | collective-permute-done | bytes 270368 | tf_op jit(solution)/shard_map/ppermute | solution.py:29
  73.1 3.7 %collective-permute-done.14.rv_ref = bf16[264,512]{1,0:T(8,128)(2,1)S(1)} collective-permute-done((bf16[264,512]{1,0:T(8,128)(2,1)S(1)}, bf16[264,512]{1,0:T(8,128)(2,1)S(1)}, u32[]{:S(2)}, u32[]{:S(2)}) %collective-permute-start.14) | collective-permute-done | bytes 270368 | tf_op jit(solution)/shard_map/ppermute | solution.py:29
  76.8 1.1 %finish.1 = (bf16[256,512]{1,0:T(8,128)(2,1)}, bf16[256,512]{1,0:T(8,128)(2,1)}, bf16[4,512]{1,0:T(4,128)(2,1)}, bf16[4,512]{1,0:T(4,128)(2,1)}) custom-call(f32[256,1024]{1,0:T(8,128)S(1)} %get-tuple-element.32.d0_ref, bf16[256,1024]{1,0:T(8,128)(2,1)S(1)} %collective-permute-done.8.after_ref.r1_ref, bf16[264,512]{1,0:T(8,128)(2,1)S(1)} %collective-permute-done.10.rk_ref, ...), custom_call_target="tpu_custom_call" | custom-call | tf_op jit(solution)/shard_map/finish/pallas_call | solution.py:301
  (36 shorter events, 1.5 us)
Async XLA Ops:
  1.7 19.6 %collective-permute-start.1 = (bf16[264,1024]{1,0:T(8,128)(2,1)S(1)}, bf16[264,1024]{1,0:T(8,128)(2,1)S(1)}, u32[]{:S(2)}, u32[]{:S(2)}) collective-permute-start(bf16[264,1024]{1,0:T(8,128)(2,1)S(1)} %get-tuple-element.28.own_ref), channel_id=1, source_target_pairs={{0,2},{1,3},{2,4},{3,5},{4,6},{5,7},{6,8},{7,9},{8,10},{9,11},{10,... | collective-permute-start | bytes 1622024 | tf_op jit(solution)/shard_map/ppermute | solution.py:29
  4.8 19.2 %collective-permute-start = (bf16[264,1024]{1,0:T(8,128)(2,1)S(1)}, bf16[264,1024]{1,0:T(8,128)(2,1)S(1)}, u32[]{:S(2)}, u32[]{:S(2)}) collective-permute-start(bf16[264,1024]{1,0:T(8,128)(2,1)S(1)} %get-tuple-element.28.own_ref), channel_id=1, source_target_pairs={{0,1},{2,3},{4,5},{6,7},{8,9},{10,11},{12,13},{14,15},{1,4},{3,6},... | collective-permute-start | bytes 1622024 | tf_op jit(solution)/shard_map/ppermute | solution.py:29
  6.2 4.9 %collective-permute-start.3 = (bf16[4,1024]{1,0:T(4,128)(2,1)S(1)}, bf16[4,1024]{1,0:T(4,128)(2,1)S(1)}, u32[]{:S(2)}, u32[]{:S(2)}) collective-permute-start(bf16[4,1024]{1,0:T(4,128)(2,1)S(1)} %get-tuple-element.29.mine_ref), channel_id=1, source_target_pairs={{0,1},{1,0},{2,3},{3,2},{4,5},{5,4},{6,7},{7,6},{8,9},{9,8},{10,11... | collective-permute-start | bytes 24584 | tf_op jit(solution)/shard_map/ppermute | solution.py:29
  11.2 5.6 %collective-permute-start.4 = (bf16[8,1024]{1,0:T(8,128)(2,1)S(1)}, bf16[8,1024]{1,0:T(8,128)(2,1)S(1)}, u32[]{:S(2)}, u32[]{:S(2)}) collective-permute-start(bf16[8,1024]{1,0:T(8,128)(2,1)S(1)} %pad_maximum_fusion), channel_id=1, source_target_pairs={{0,4},{1,11},{2,6},{3,13},{4,8},{5,15},{6,10},{7,1},{8,12},{9,3},{... | collective-permute-start | bytes 49160 | tf_op jit(solution)/shard_map/ppermute | solution.py:29
  12.8 8.5 %collective-permute-start.6 = (bf16[8,1024]{1,0:T(8,128)(2,1)S(1)}, bf16[8,1024]{1,0:T(8,128)(2,1)S(1)}, u32[]{:S(2)}, u32[]{:S(2)}) collective-permute-start(bf16[8,1024]{1,0:T(8,128)(2,1)S(1)} %pad_maximum_fusion), channel_id=1, source_target_pairs={{0,8},{1,15},{2,10},{3,1},{4,12},{5,3},{6,14},{7,5},{8,0},{9,7},{1... | collective-permute-start | bytes 49160 | tf_op jit(solution)/shard_map/ppermute | solution.py:29
  13.9 7.4 %collective-permute-start.5 = (bf16[8,1024]{1,0:T(8,128)(2,1)S(1)}, bf16[8,1024]{1,0:T(8,128)(2,1)S(1)}, u32[]{:S(2)}, u32[]{:S(2)}) collective-permute-start(bf16[8,1024]{1,0:T(8,128)(2,1)S(1)} %pad_maximum_fusion), channel_id=1, source_target_pairs={{0,6},{1,13},{2,8},{3,15},{4,10},{5,1},{6,12},{7,3},{8,14},{9,5},{... | collective-permute-start | bytes 49160 | tf_op jit(solution)/shard_map/ppermute | solution.py:29
  21.3 2.6 %collective-permute-start.2 = (bf16[264,1024]{1,0:T(8,128)(2,1)S(1)}, bf16[264,1024]{1,0:T(8,128)(2,1)S(1)}, u32[]{:S(2)}, u32[]{:S(2)}) collective-permute-start(bf16[264,1024]{1,0:T(8,128)(2,1)S(1)} %collective-permute-done.1.w2_ref), channel_id=1, source_target_pairs={{0,1},{1,0},{2,3},{3,2},{4,5},{5,4},{6,7},{7,6},{8,9},{9,8},{10,11... | collective-permute-start | bytes 1622024 | tf_op jit(solution)/shard_map/ppermute | solution.py:29
  21.3 2.6 %collective-permute-start.7 = (bf16[24,1024]{1,0:T(8,128)(2,1)S(1)}, bf16[24,1024]{1,0:T(8,128)(2,1)S(1)}, u32[]{:S(2)}, u32[]{:S(2)}) collective-permute-start(bf16[24,1024]{1,0:T(8,128)(2,1)S(1)} %constant_dynamic-update-slice_fusion.near_ref), channel_id=1, source_target_pairs={{0,1},{1,0},{2,3},{3,2},{4,5},{5,4},{6,7},{7,6},{8,9},{9,8},{10,11... | collective-permute-start | bytes 147464 | tf_op jit(solution)/shard_map/ppermute | solution.py:29
  51.1 2.8 %collective-permute-start.9 = (f32[288,1024]{1,0:T(8,128)S(1)}, f32[288,1024]{1,0:T(8,128)S(1)}, u32[]{:S(2)}, u32[]{:S(2)}) collective-permute-start(f32[288,1024]{1,0:T(8,128)S(1)} %get-tuple-element.35), channel_id=1, source_target_pairs={{0,1},{1,0},{2,3},{3,2},{4,5},{5,4},{6,7},{7,6},{8,9},{9,8},{10,11... | collective-permute-start | bytes 3538952 | tf_op jit(solution)/shard_map/ppermute | solution.py:29
  51.2 17.6 %collective-permute-start.8 = (bf16[256,1024]{1,0:T(8,128)(2,1)S(1)}, bf16[256,1024]{1,0:T(8,128)(2,1)S(1)}, u32[]{:S(2)}, u32[]{:S(2)}) collective-permute-start(bf16[256,1024]{1,0:T(8,128)(2,1)S(1)} %get-tuple-element.33), channel_id=1, source_target_pairs={{1,0},{3,2},{5,4},{7,6},{9,8},{11,10},{13,12},{15,14},{4,1},{6,3},... | collective-permute-start | bytes 1572872 | tf_op jit(solution)/shard_map/ppermute | solution.py:29
  54.1 11.9 %collective-permute-start.11 = (f32[8,1024]{1,0:T(8,128)S(1)}, f32[8,1024]{1,0:T(8,128)S(1)}, u32[]{:S(2)}, u32[]{:S(2)}) collective-permute-start(f32[8,1024]{1,0:T(8,128)S(1)} %get-tuple-element.39), channel_id=1, source_target_pairs={{4,0},{11,1},{6,2},{13,3},{8,4},{15,5},{10,6},{1,7},{12,8},{3,9},{... | collective-permute-start | bytes 98312 | tf_op jit(solution)/shard_map/ppermute | solution.py:29
  60.7 6.1 %collective-permute-start.12 = (f32[8,1024]{1,0:T(8,128)S(1)}, f32[8,1024]{1,0:T(8,128)S(1)}, u32[]{:S(2)}, u32[]{:S(2)}) collective-permute-start(f32[8,1024]{1,0:T(8,128)S(1)} %get-tuple-element.40), channel_id=1, source_target_pairs={{6,0},{13,1},{8,2},{15,3},{10,4},{1,5},{12,6},{3,7},{14,8},{5,9},{... | collective-permute-start | bytes 98312 | tf_op jit(solution)/shard_map/ppermute | solution.py:29
  60.7 6.1 %collective-permute-start.13 = (f32[8,1024]{1,0:T(8,128)S(1)}, f32[8,1024]{1,0:T(8,128)S(1)}, u32[]{:S(2)}, u32[]{:S(2)}) collective-permute-start(f32[8,1024]{1,0:T(8,128)S(1)} %get-tuple-element.41), channel_id=1, source_target_pairs={{8,0},{15,1},{10,2},{1,3},{12,4},{3,5},{14,6},{5,7},{0,8},{7,9},{2... | collective-permute-start | bytes 98312 | tf_op jit(solution)/shard_map/ppermute | solution.py:29
  63.7 9.4 %collective-permute-start.10 = (bf16[264,512]{1,0:T(8,128)(2,1)S(1)}, bf16[264,512]{1,0:T(8,128)(2,1)S(1)}, u32[]{:S(2)}, u32[]{:S(2)}) collective-permute-start(bf16[264,512]{1,0:T(8,128)(2,1)S(1)} %get-tuple-element.37), channel_id=1, source_target_pairs={{2,0},{3,1},{4,2},{5,3},{6,4},{7,5},{8,6},{9,7},{10,8},{11,9},{12,... | collective-permute-start | bytes 811016 | tf_op jit(solution)/shard_map/ppermute | solution.py:29
  66.8 10.0 %collective-permute-start.14 = (bf16[264,512]{1,0:T(8,128)(2,1)S(1)}, bf16[264,512]{1,0:T(8,128)(2,1)S(1)}, u32[]{:S(2)}, u32[]{:S(2)}) collective-permute-start(bf16[264,512]{1,0:T(8,128)(2,1)S(1)} %get-tuple-element.42), channel_id=1, source_target_pairs={{2,0},{3,1},{4,2},{5,3},{6,4},{7,5},{8,6},{9,7},{10,8},{11,9},{12,... | collective-permute-start | bytes 811016 | tf_op jit(solution)/shard_map/ppermute | solution.py:29
  68.8 1.2 %collective-permute-start.15 = (f32[4,1024]{1,0:T(4,128)S(1)}, f32[4,1024]{1,0:T(4,128)S(1)}, u32[]{:S(2)}, u32[]{:S(2)}) collective-permute-start(f32[4,1024]{1,0:T(4,128)S(1)} %get-tuple-element.45), channel_id=1, source_target_pairs={{0,1},{1,0},{2,3},{3,2},{4,5},{5,4},{6,7},{7,6},{8,9},{9,8},{10,11... | collective-permute-start | bytes 49160 | tf_op jit(solution)/shard_map/ppermute | solution.py:29

commit v6 on v5

--- a/solution.py
+++ b/solution.py
@@ -92,14 +92,31 @@
     )(*(in_hbm(x) for x in (keys, values, prompt_keys, prompt_values)))
 
 
+def gather_kernel(near_ref, far_ref, out_ref):
+    both = jnp.concatenate([near_ref[...].astype(f32), far_ref[...].astype(f32)], axis=0)
+    out_ref[...] = both.astype(bf16)
+
+
+def gather(near, far):
+    half, wide = near.shape
+    return pl.pallas_call(
+        gather_kernel,
+        in_specs=[IN_VMEM] * 2,
+        out_specs=IN_VMEM,
+        out_shape=jax.ShapeDtypeStruct((2 * half, wide), bf16),
+        compiler_params=pltpu.CompilerParams(vmem_limit_bytes=2 * 2**20),
+        name="gather",
+    )(near, far)
+
+
 def attend_kernel(
     seen, q_ref, g_ref, cos_ref, sin_ref, own_ref, w1_ref, w2_ref, w3_ref,
-    mine_ref, theirs_ref, near_ref, far_ref,
+    mine_ref, theirs_ref, others_ref,
     o_ref, dq_ref, d0_ref, d1_ref, d2_ref, d3_ref, dp_ref,
     k_buf, v_buf, dk_buf, dv_buf, p_buf,
 ):
     rows = q_ref.shape[0]
-    few, half = mine_ref.shape[0], near_ref.shape[0]
+    few, half = mine_ref.shape[0], others_ref.shape[0] // 2
     col = pl.program_id(0) * HD
     k_at = pl.ds(pl.multiple_of(col, HD), HD)
     v_at = pl.ds(pl.multiple_of(col + WIDTH, HD), HD)
@@ -110,17 +127,16 @@
         v_buf[span, :] = part[:rows, v_at]
     span = slice(SPAN * rows, SPAN * rows + 4 * few + 2 * half)
 
-    def gather(at):
+    def prompt(at):
         p_buf[:few, :] = mine_ref[:, at].astype(f32)
         p_buf[few : 2 * few, :] = theirs_ref[:, at].astype(f32)
         p_buf[2 * few : 3 * few, :] = w2_ref[rows:, at].astype(f32)[:few]
         p_buf[3 * few : 4 * few, :] = w3_ref[rows:, at].astype(f32)[:few]
-        p_buf[4 * few : 4 * few + half, :] = near_ref[:, at].astype(f32)
-        p_buf[4 * few + half :, :] = far_ref[:, at].astype(f32)
+        p_buf[4 * few :, :] = others_ref[:, at].astype(f32)
         return p_buf[...]
 
-    k_buf[span, :] = turn(gather(k_at), cos_ref[span, :], sin_ref[span, :]).astype(bf16)
-    v_buf[span, :] = gather(v_at).astype(bf16)
+    k_buf[span, :] = turn(prompt(k_at), cos_ref[span, :], sin_ref[span, :]).astype(bf16)
+    v_buf[span, :] = prompt(v_at).astype(bf16)
     k, v = k_buf[...], v_buf[...]
     cosine, sine = cos_ref[:rows, :], sin_ref[:rows, :]
     lower = lax.broadcasted_iota(jnp.int32, (rows, rows), 1) <= lax.broadcasted_iota(
@@ -195,7 +211,7 @@
 def attend(seen, queries, grads, cosine, sine, blocks, prompts):
     rows = queries.shape[0]
     wide = blocks[0].shape[1]
-    few, half = prompts[0].shape[0], prompts[2].shape[0]
+    few, half = prompts[0].shape[0], prompts[2].shape[0] // 2
     keys = SPAN * rows + 4 * few + 2 * half
     part = half + 2 * few
     head = pl.BlockSpec((rows, GROUP * HD), lambda i, s: (0, i))
@@ -205,7 +221,7 @@
         grid_spec=pltpu.PrefetchScalarGridSpec(
             num_scalar_prefetch=1,
             grid=(KVH,),
-            in_specs=[head, head] + [IN_VMEM] * 10,
+            in_specs=[head, head] + [IN_VMEM] * 9,
             out_specs=[head, head] + [IN_VMEM] * 5,
             scratch_shapes=[pltpu.VMEM((keys, HD), bf16)] * 2
             + [pltpu.VMEM((keys, HD), f32)] * 2
@@ -252,7 +268,7 @@
     )(d2, r3, dp)
 
 
-def tally_kernel(after_ref, *refs):
+def tally_kernel(after_ref, later_ref, *refs):
     terms, keep_ref, send_ref = refs[:-2], refs[-2], refs[-1]
     few = keep_ref.shape[0]
     total = terms[0][...]
@@ -262,16 +278,16 @@
     send_ref[...] = total[few:]
 
 
-def tally(after, terms):
+def tally(after, later, terms):
     few, wide = terms[0].shape
     return pl.pallas_call(
         tally_kernel,
-        in_specs=[IN_VMEM] * (1 + len(terms)),
+        in_specs=[IN_VMEM] * (2 + len(terms)),
         out_specs=[IN_VMEM] * 2,
         out_shape=[jax.ShapeDtypeStruct((few // 2, wide), f32)] * 2,
         compiler_params=pltpu.CompilerParams(vmem_limit_bytes=2 * 2**20),
         name="tally",
-    )(after, *terms)
+    )(after, later, *terms)
 
 
 def finish_kernel(
@@ -325,12 +341,12 @@
 
     own, mine = pack(answer_keys, answer_values, prompt_keys, prompt_values)
     w2 = permute(own, ahead)
-    w1 = permute(own, across)
     theirs = permute(mine, swap)
     chip = jnp.concatenate([mine, theirs], axis=0)
+    w1 = permute(lax.optimization_barrier((own, chip))[0], across)
     near = jnp.concatenate([permute(chip, pairs) for pairs in rounds], axis=0)
     w3 = permute(w2, swap)
-    far = permute(near, swap)
+    others = gather(near, permute(near, swap))
 
     table = ancestry[0]
     column = jnp.arange(table.shape[0], dtype=jnp.int32)[None, :]
@@ -354,15 +370,15 @@
     cosine, sine = angle_tables(jnp.concatenate([places, prompt_places.reshape(-1)]))
 
     attended, grad_queries, d0, d1, d2, d3, dp = attend(
-        seen[1:], queries, out_grad, cosine, sine, [own, w1, w2, w3], [mine, theirs, near, far]
+        seen[1:], queries, out_grad, cosine, sine, [own, w1, w2, w3], [mine, theirs, others]
     )
     r3 = permute(d3, swap)
     r1 = permute(d1, back(across))
     xk, xv, keep, *terms = merge(d2, r3, dp, few, turns)
     rk = permute(xk, back(ahead))
     sums = [permute(t, back(p)) for t, p in zip(terms, rounds)]
-    rv = permute(lax.optimization_barrier((xv, *sums))[0], back(ahead))
-    tallied, send = tally(r1, sums)
+    rv = permute(lax.optimization_barrier((xv, r1, rk, *sums))[0], back(ahead))
+    tallied, send = tally(r1, rk, sums)
     got = permute(send, swap)
     grad_keys, grad_values, grad_prompt_keys, grad_prompt_values = finish(
         d0, r1, rk, rv, cosine, sine, keep, tallied, got

time: 78.7 us -> 78.5 us (level)
  waiting for transfers between devices: 14.9 us -> 23 us
  starting transfers between devices: 27.9 us -> 20 us
    ppermute x16, waiting for transfers between devices: 14.9 us -> 23 us  [permute(): return lax.ppermute(value, 'ctx', pairs)]
    ppermute x16, starting transfers between devices: 27.9 us -> 20 us  [permute(): return lax.ppermute(value, 'ctx', pairs)]
  transfers between devices with their start and end apart: 16 -> 16, of which waited for: 7 -> 5; matrix products, arithmetic and copies ran while one was open for 6% -> 6% of each run, Pallas kernels for 0% -> 0%
where the time goes in v6:
time: 78.5 us; the launch traced here: 78.2 us
  Pallas kernels  29.5 us (38%)
  waiting for transfers between devices  23 us (29%)
  starting transfers between devices  20 us (25%)
  other arithmetic  4.53 us (6%)
  between operations  0.8 us (1%)
    pallas_call x1, Pallas kernels, attend(): pl.pallas_call(attend_kernel, grid_spec=pltpu.PrefetchScalarGridSpec(num_...  27.2 us
    ppermute x16, waiting for transfers between devices, permute(): return lax.ppermute(value, 'ctx', pairs)  23 us
    ppermute x16, starting transfers between devices, permute(): return lax.ppermute(value, 'ctx', pairs)  20 us
    mul x1, other arithmetic, angle_tables(): return (jnp.cos(angles), jnp.sin(angles) * sign[None, :])  2.01 us
  transfers between devices with their start and end apart: 16, of which 5 were waited for; matrix products, arithmetic and copies ran while one was open for 6% of the time, Pallas kernels for 0%

profile of v6, /device:TPU:0, one launch (start us, length us, event | category | flops | bytes accessed | tf_op | source)
XLA Modules:
  0.0 78.2 jit_solution(8871151465691002631)
XLA Ops:
  0.6 1.1 %pack.1 = (bf16[264,1024]{1,0:T(8,128)(2,1)S(1)}, bf16[4,1024]{1,0:T(4,128)(2,1)S(1)}) custom-call(bf16[256,512]{1,0:T(8,128)(2,1)} %k_ref.1, bf16[256,512]{1,0:T(8,128)(2,1)} %v_ref.1, bf16[4,512]{1,0:T(4,128)(2,1)} %pk_ref.1, bf16[4,512]{1,0:T(4,128)(2,1)} %pv_ref.1), custom_call_target="tpu_custom_call" | custom-call | tf_op jit(solution)/shard_map/pack/pallas_call | solution.py:81
  1.7 0.5 collective-permute-start
  2.3 2.6 %collective-permute-start.2 = (bf16[264,1024]{1,0:T(8,128)(2,1)S(1)}, bf16[264,1024]{1,0:T(8,128)(2,1)S(1)}, u32[]{:S(2)}, u32[]{:S(2)}) collective-permute-start(bf16[264,1024]{1,0:T(8,128)(2,1)S(1)} %get-tuple-element.31.own_ref), channel_id=1, source_target_pairs={{0,2},{1,3},{2,4},{3,5},{4,6},{5,7},{6,8},{7,9},{8,10},{9,11},{10,... | collective-permute-start | bytes 1622024 | tf_op jit(solution)/shard_map/ppermute | solution.py:29
  4.8 0.9 %select_reduce_fusion = (s32[4]{0:T(128)S(1)}, s32[4]{0:T(128)S(1)}) fusion(s32[16]{0:T(128)} %bitcast.9, s32[4]{0:T(128)S(1)} %fusion.10, pred[16]{0:T(512)(128)(4,1)S(1)} %iota_compare_fusion.2), kind=kLoop, calls=%fused_computation.12 | loop fusion | flops 440 | bytes 128 | tf_op jit(solution)/shard_map/reduce_sum | solution.py:357
  5.7 0.7 broadcast_select_fusion.1
  6.6 0.7 subtract_bitcast_fusion
  7.6 1.6 %collective-permute-start.4 = (bf16[8,1024]{1,0:T(8,128)(2,1)S(1)}, bf16[8,1024]{1,0:T(8,128)(2,1)S(1)}, u32[]{:S(2)}, u32[]{:S(2)}) collective-permute-start(bf16[8,1024]{1,0:T(8,128)(2,1)S(1)} %pad_maximum_fusion), channel_id=1, source_target_pairs={{0,4},{1,11},{2,6},{3,13},{4,8},{5,15},{6,10},{7,1},{8,12},{9,3},{... | collective-permute-start | bytes 49160 | tf_op jit(solution)/shard_map/ppermute | solution.py:29
  9.2 2.6 %collective-permute-start.6 = (bf16[8,1024]{1,0:T(8,128)(2,1)S(1)}, bf16[8,1024]{1,0:T(8,128)(2,1)S(1)}, u32[]{:S(2)}, u32[]{:S(2)}) collective-permute-start(bf16[8,1024]{1,0:T(8,128)(2,1)S(1)} %pad_maximum_fusion), channel_id=1, source_target_pairs={{0,8},{1,15},{2,10},{3,1},{4,12},{5,3},{6,14},{7,5},{8,0},{9,7},{1... | collective-permute-start | bytes 49160 | tf_op jit(solution)/shard_map/ppermute | solution.py:29
  11.8 1.2 %collective-permute-start.5 = (bf16[8,1024]{1,0:T(8,128)(2,1)S(1)}, bf16[8,1024]{1,0:T(8,128)(2,1)S(1)}, u32[]{:S(2)}, u32[]{:S(2)}) collective-permute-start(bf16[8,1024]{1,0:T(8,128)(2,1)S(1)} %pad_maximum_fusion), channel_id=1, source_target_pairs={{0,6},{1,13},{2,8},{3,15},{4,10},{5,1},{6,12},{7,3},{8,14},{9,5},{... | collective-permute-start | bytes 49160 | tf_op jit(solution)/shard_map/ppermute | solution.py:29
  13.0 1.3 %collective-permute-start.1 = (bf16[264,1024]{1,0:T(8,128)(2,1)S(1)}, bf16[264,1024]{1,0:T(8,128)(2,1)S(1)}, u32[]{:S(2)}, u32[]{:S(2)}) collective-permute-start(bf16[264,1024]{1,0:T(8,128)(2,1)S(1)} %get-tuple-element.31.own_ref), channel_id=1, source_target_pairs={{0,1},{2,3},{4,5},{6,7},{8,9},{10,11},{12,13},{14,15},{1,4},{3,6},... | collective-permute-start | bytes 1622024 | tf_op jit(solution)/shard_map/ppermute | solution.py:29
  14.3 7.6 %collective-permute-done.5 = bf16[8,1024]{1,0:T(8,128)(2,1)S(1)} collective-permute-done((bf16[8,1024]{1,0:T(8,128)(2,1)S(1)}, bf16[8,1024]{1,0:T(8,128)(2,1)S(1)}, u32[]{:S(2)}, u32[]{:S(2)}) %collective-permute-start.5) | collective-permute-done | bytes 16416 | tf_op jit(solution)/shard_map/ppermute | solution.py:29
  22.0 0.5 collective-permute-start.7
  22.5 2.0 %fusion = (f32[1088,128]{1,0:T(8,128)S(1)}, f32[1088,128]{1,0:T(8,128)S(1)}) fusion(f32[128]{0:T(128)S(1)} %get-tuple-element.60, f32[128]{0:T(128)S(1)} %get-tuple-element.61, f32[1088]{0:T(1024)S(1)} %add_convert_fusion), kind=kLoop, calls=%fused_computation.2 | loop fusion | flops 278528 | bytes 1119488 | tf_op jit(solution)/shard_map/mul | solution.py:41
  24.6 27.2 %attend.1 = (bf16[256,2560]{1,0:T(8,128)(2,1)}, bf16[256,2560]{1,0:T(8,128)(2,1)}, f32[256,1024]{1,0:T(8,128)S(1)}, bf16[256,1024]{1,0:T(8,128)(2,1)S(1)}, f32[2...) custom-call(s32[3]{0:T(128)S(1)} %slice.3.seen, bf16[256,2560]{1,0:T(8,128)(2,1)} %q_ref.1, ...), custom_call_target="tpu_custom_call" | custom-call | tf_op jit(solution)/shard_map/attend/pallas_call | solution.py:219
  51.9 1.3 %collective-permute-start.8 = (bf16[256,1024]{1,0:T(8,128)(2,1)S(1)}, bf16[256,1024]{1,0:T(8,128)(2,1)S(1)}, u32[]{:S(2)}, u32[]{:S(2)}) collective-permute-start(bf16[256,1024]{1,0:T(8,128)(2,1)S(1)} %get-tuple-element.35), channel_id=1, source_target_pairs={{1,0},{3,2},{5,4},{7,6},{9,8},{11,10},{13,12},{15,14},{4,1},{6,3},... | collective-permute-start | bytes 1572872 | tf_op jit(solution)/shard_map/ppermute | solution.py:29
  53.2 1.5 %collective-permute-done.9.r3_ref = f32[288,1024]{1,0:T(8,128)S(1)} collective-permute-done((f32[288,1024]{1,0:T(8,128)S(1)}, f32[288,1024]{1,0:T(8,128)S(1)}, u32[]{:S(2)}, u32[]{:S(2)}) %collective-permute-start.9) | collective-permute-done | bytes 1179680 | tf_op jit(solution)/shard_map/ppermute | solution.py:29
  54.8 4.6 %collective-permute-start.10 = (bf16[264,512]{1,0:T(8,128)(2,1)S(1)}, bf16[264,512]{1,0:T(8,128)(2,1)S(1)}, u32[]{:S(2)}, u32[]{:S(2)}) collective-permute-start(bf16[264,512]{1,0:T(8,128)(2,1)S(1)} %get-tuple-element.39), channel_id=1, source_target_pairs={{2,0},{3,1},{4,2},{5,3},{6,4},{7,5},{8,6},{9,7},{10,8},{11,9},{12,... | collective-permute-start | bytes 811016 | tf_op jit(solution)/shard_map/ppermute | solution.py:29
  59.4 0.8 %collective-permute-start.11 = (f32[8,1024]{1,0:T(8,128)S(1)}, f32[8,1024]{1,0:T(8,128)S(1)}, u32[]{:S(2)}, u32[]{:S(2)}) collective-permute-start(f32[8,1024]{1,0:T(8,128)S(1)} %get-tuple-element.41), channel_id=1, source_target_pairs={{4,0},{11,1},{6,2},{13,3},{8,4},{15,5},{10,6},{1,7},{12,8},{3,9},{... | collective-permute-start | bytes 98312 | tf_op jit(solution)/shard_map/ppermute | solution.py:29
  60.2 2.2 %collective-permute-start.13 = (f32[8,1024]{1,0:T(8,128)S(1)}, f32[8,1024]{1,0:T(8,128)S(1)}, u32[]{:S(2)}, u32[]{:S(2)}) collective-permute-start(f32[8,1024]{1,0:T(8,128)S(1)} %get-tuple-element.43), channel_id=1, source_target_pairs={{8,0},{15,1},{10,2},{1,3},{12,4},{3,5},{14,6},{5,7},{0,8},{7,9},{2... | collective-permute-start | bytes 98312 | tf_op jit(solution)/shard_map/ppermute | solution.py:29
  62.3 8.2 %collective-permute-done.11.refs_0_ = f32[8,1024]{1,0:T(8,128)S(1)} collective-permute-done((f32[8,1024]{1,0:T(8,128)S(1)}, f32[8,1024]{1,0:T(8,128)S(1)}, u32[]{:S(2)}, u32[]{:S(2)}) %collective-permute-start.11) | collective-permute-done | bytes 32800 | tf_op jit(solution)/shard_map/ppermute | solution.py:29
  70.6 0.8 collective-permute-start.14
  71.4 1.2 %collective-permute-done.15.got_ref = f32[4,1024]{1,0:T(4,128)S(1)} collective-permute-done((f32[4,1024]{1,0:T(4,128)S(1)}, f32[4,1024]{1,0:T(4,128)S(1)}, u32[]{:S(2)}, u32[]{:S(2)}) %collective-permute-start.15) | collective-permute-done | bytes 16416 | tf_op jit(solution)/shard_map/ppermute | solution.py:29
  72.6 4.5 %collective-permute-done.14.rv_ref = bf16[264,512]{1,0:T(8,128)(2,1)S(1)} collective-permute-done((bf16[264,512]{1,0:T(8,128)(2,1)S(1)}, bf16[264,512]{1,0:T(8,128)(2,1)S(1)}, u32[]{:S(2)}, u32[]{:S(2)}) %collective-permute-start.14) | collective-permute-done | bytes 270368 | tf_op jit(solution)/shard_map/ppermute | solution.py:29
  77.1 1.1 %finish.1 = (bf16[256,512]{1,0:T(8,128)(2,1)}, bf16[256,512]{1,0:T(8,128)(2,1)}, bf16[4,512]{1,0:T(4,128)(2,1)}, bf16[4,512]{1,0:T(4,128)(2,1)}) custom-call(f32[256,1024]{1,0:T(8,128)S(1)} %get-tuple-element.34.d0_ref, bf16[256,1024]{1,0:T(8,128)(2,1)S(1)} %collective-permute-done.8.after_ref.r1_ref, ...), custom_call_target="tpu_custom_call" | custom-call | tf_op jit(solution)/shard_map/finish/pallas_call | solution.py:317
  (37 shorter events, 0.8 us)
Async XLA Ops:
  1.7 5.8 %collective-permute-start = (bf16[4,1024]{1,0:T(4,128)(2,1)S(1)}, bf16[4,1024]{1,0:T(4,128)(2,1)S(1)}, u32[]{:S(2)}, u32[]{:S(2)}) collective-permute-start(bf16[4,1024]{1,0:T(4,128)(2,1)S(1)} %get-tuple-element.30.mine_ref), channel_id=1, source_target_pairs={{0,1},{1,0},{2,3},{3,2},{4,5},{5,4},{6,7},{7,6},{8,9},{9,8},{10,11... | collective-permute-start | bytes 24584 | tf_op jit(solution)/shard_map/ppermute | solution.py:29
  2.3 19.7 %collective-permute-start.2 = (bf16[264,1024]{1,0:T(8,128)(2,1)S(1)}, bf16[264,1024]{1,0:T(8,128)(2,1)S(1)}, u32[]{:S(2)}, u32[]{:S(2)}) collective-permute-start(bf16[264,1024]{1,0:T(8,128)(2,1)S(1)} %get-tuple-element.31.own_ref), channel_id=1, source_target_pairs={{0,2},{1,3},{2,4},{3,5},{4,6},{5,7},{6,8},{7,9},{8,10},{9,11},{10,... | collective-permute-start | bytes 1622024 | tf_op jit(solution)/shard_map/ppermute | solution.py:29
  7.6 6.7 %collective-permute-start.4 = (bf16[8,1024]{1,0:T(8,128)(2,1)S(1)}, bf16[8,1024]{1,0:T(8,128)(2,1)S(1)}, u32[]{:S(2)}, u32[]{:S(2)}) collective-permute-start(bf16[8,1024]{1,0:T(8,128)(2,1)S(1)} %pad_maximum_fusion), channel_id=1, source_target_pairs={{0,4},{1,11},{2,6},{3,13},{4,8},{5,15},{6,10},{7,1},{8,12},{9,3},{... | collective-permute-start | bytes 49160 | tf_op jit(solution)/shard_map/ppermute | solution.py:29
  9.2 12.8 %collective-permute-start.6 = (bf16[8,1024]{1,0:T(8,128)(2,1)S(1)}, bf16[8,1024]{1,0:T(8,128)(2,1)S(1)}, u32[]{:S(2)}, u32[]{:S(2)}) collective-permute-start(bf16[8,1024]{1,0:T(8,128)(2,1)S(1)} %pad_maximum_fusion), channel_id=1, source_target_pairs={{0,8},{1,15},{2,10},{3,1},{4,12},{5,3},{6,14},{7,5},{8,0},{9,7},{1... | collective-permute-start | bytes 49160 | tf_op jit(solution)/shard_map/ppermute | solution.py:29
  11.8 10.2 %collective-permute-start.5 = (bf16[8,1024]{1,0:T(8,128)(2,1)S(1)}, bf16[8,1024]{1,0:T(8,128)(2,1)S(1)}, u32[]{:S(2)}, u32[]{:S(2)}) collective-permute-start(bf16[8,1024]{1,0:T(8,128)(2,1)S(1)} %pad_maximum_fusion), channel_id=1, source_target_pairs={{0,6},{1,13},{2,8},{3,15},{4,10},{5,1},{6,12},{7,3},{8,14},{9,5},{... | collective-permute-start | bytes 49160 | tf_op jit(solution)/shard_map/ppermute | solution.py:29
  13.0 11.6 %collective-permute-start.1 = (bf16[264,1024]{1,0:T(8,128)(2,1)S(1)}, bf16[264,1024]{1,0:T(8,128)(2,1)S(1)}, u32[]{:S(2)}, u32[]{:S(2)}) collective-permute-start(bf16[264,1024]{1,0:T(8,128)(2,1)S(1)} %get-tuple-element.31.own_ref), channel_id=1, source_target_pairs={{0,1},{2,3},{4,5},{6,7},{8,9},{10,11},{12,13},{14,15},{1,4},{3,6},... | collective-permute-start | bytes 1622024 | tf_op jit(solution)/shard_map/ppermute | solution.py:29
  22.0 2.6 %collective-permute-start.3 = (bf16[264,1024]{1,0:T(8,128)(2,1)S(1)}, bf16[264,1024]{1,0:T(8,128)(2,1)S(1)}, u32[]{:S(2)}, u32[]{:S(2)}) collective-permute-start(bf16[264,1024]{1,0:T(8,128)(2,1)S(1)} %collective-permute-done.2.w2_ref), channel_id=1, source_target_pairs={{0,1},{1,0},{2,3},{3,2},{4,5},{5,4},{6,7},{7,6},{8,9},{9,8},{10,11... | collective-permute-start | bytes 1622024 | tf_op jit(solution)/shard_map/ppermute | solution.py:29
  22.0 2.6 %collective-permute-start.7 = (bf16[24,1024]{1,0:T(8,128)(2,1)S(1)}, bf16[24,1024]{1,0:T(8,128)(2,1)S(1)}, u32[]{:S(2)}, u32[]{:S(2)}) collective-permute-start(bf16[24,1024]{1,0:T(8,128)(2,1)S(1)} %constant_dynamic-update-slice_fusion.near_ref), channel_id=1, source_target_pairs={{0,1},{1,0},{2,3},{3,2},{4,5},{5,4},{6,7},{7,6},{8,9},{9,8},{10,11... | collective-permute-start | bytes 147464 | tf_op jit(solution)/shard_map/ppermute | solution.py:29
  51.8 2.8 %collective-permute-start.9 = (f32[288,1024]{1,0:T(8,128)S(1)}, f32[288,1024]{1,0:T(8,128)S(1)}, u32[]{:S(2)}, u32[]{:S(2)}) collective-permute-start(f32[288,1024]{1,0:T(8,128)S(1)} %get-tuple-element.37), channel_id=1, source_target_pairs={{0,1},{1,0},{2,3},{3,2},{4,5},{5,4},{6,7},{7,6},{8,9},{9,8},{10,11... | collective-permute-start | bytes 3538952 | tf_op jit(solution)/shard_map/ppermute | solution.py:29
  51.9 10.4 %collective-permute-start.8 = (bf16[256,1024]{1,0:T(8,128)(2,1)S(1)}, bf16[256,1024]{1,0:T(8,128)(2,1)S(1)}, u32[]{:S(2)}, u32[]{:S(2)}) collective-permute-start(bf16[256,1024]{1,0:T(8,128)(2,1)S(1)} %get-tuple-element.35), channel_id=1, source_target_pairs={{1,0},{3,2},{5,4},{7,6},{9,8},{11,10},{13,12},{15,14},{4,1},{6,3},... | collective-permute-start | bytes 1572872 | tf_op jit(solution)/shard_map/ppermute | solution.py:29
  54.8 15.8 %collective-permute-start.10 = (bf16[264,512]{1,0:T(8,128)(2,1)S(1)}, bf16[264,512]{1,0:T(8,128)(2,1)S(1)}, u32[]{:S(2)}, u32[]{:S(2)}) collective-permute-start(bf16[264,512]{1,0:T(8,128)(2,1)S(1)} %get-tuple-element.39), channel_id=1, source_target_pairs={{2,0},{3,1},{4,2},{5,3},{6,4},{7,5},{8,6},{9,7},{10,8},{11,9},{12,... | collective-permute-start | bytes 811016 | tf_op jit(solution)/shard_map/ppermute | solution.py:29
  59.4 11.2 %collective-permute-start.11 = (f32[8,1024]{1,0:T(8,128)S(1)}, f32[8,1024]{1,0:T(8,128)S(1)}, u32[]{:S(2)}, u32[]{:S(2)}) collective-permute-start(f32[8,1024]{1,0:T(8,128)S(1)} %get-tuple-element.41), channel_id=1, source_target_pairs={{4,0},{11,1},{6,2},{13,3},{8,4},{15,5},{10,6},{1,7},{12,8},{3,9},{... | collective-permute-start | bytes 98312 | tf_op jit(solution)/shard_map/ppermute | solution.py:29
  60.2 10.4 %collective-permute-start.12 = (f32[8,1024]{1,0:T(8,128)S(1)}, f32[8,1024]{1,0:T(8,128)S(1)}, u32[]{:S(2)}, u32[]{:S(2)}) collective-permute-start(f32[8,1024]{1,0:T(8,128)S(1)} %get-tuple-element.42), channel_id=1, source_target_pairs={{6,0},{13,1},{8,2},{15,3},{10,4},{1,5},{12,6},{3,7},{14,8},{5,9},{... | collective-permute-start | bytes 98312 | tf_op jit(solution)/shard_map/ppermute | solution.py:29
  60.2 10.4 %collective-permute-start.13 = (f32[8,1024]{1,0:T(8,128)S(1)}, f32[8,1024]{1,0:T(8,128)S(1)}, u32[]{:S(2)}, u32[]{:S(2)}) collective-permute-start(f32[8,1024]{1,0:T(8,128)S(1)} %get-tuple-element.43), channel_id=1, source_target_pairs={{8,0},{15,1},{10,2},{1,3},{12,4},{3,5},{14,6},{5,7},{0,8},{7,9},{2... | collective-permute-start | bytes 98312 | tf_op jit(solution)/shard_map/ppermute | solution.py:29
  70.6 6.5 %collective-permute-start.14 = (bf16[264,512]{1,0:T(8,128)(2,1)S(1)}, bf16[264,512]{1,0:T(8,128)(2,1)S(1)}, u32[]{:S(2)}, u32[]{:S(2)}) collective-permute-start(bf16[264,512]{1,0:T(8,128)(2,1)S(1)} %get-tuple-element.44), channel_id=1, source_target_pairs={{2,0},{3,1},{4,2},{5,3},{6,4},{7,5},{8,6},{9,7},{10,8},{11,9},{12,... | collective-permute-start | bytes 811016 | tf_op jit(solution)/shard_map/ppermute | solution.py:29
  71.3 1.2 %collective-permute-start.15 = (f32[4,1024]{1,0:T(4,128)S(1)}, f32[4,1024]{1,0:T(4,128)S(1)}, u32[]{:S(2)}, u32[]{:S(2)}) collective-permute-start(f32[4,1024]{1,0:T(4,128)S(1)} %get-tuple-element.47), channel_id=1, source_target_pairs={{0,1},{1,0},{2,3},{3,2},{4,5},{5,4},{6,7},{7,6},{8,9},{9,8},{10,11... | collective-permute-start | bytes 49160 | tf_op jit(solution)/shard_map/ppermute | solution.py:29

commit v7 on v6

--- a/solution.py
+++ b/solution.py
@@ -8,6 +8,7 @@
 QH = 20
 KVH = 4
 GROUP = QH // KVH
+PAIR = 2
 HD = 128
 WIDTH = KVH * HD
 SPAN = 4
@@ -117,14 +118,15 @@
 ):
     rows = q_ref.shape[0]
     few, half = mine_ref.shape[0], others_ref.shape[0] // 2
-    col = pl.program_id(0) * HD
-    k_at = pl.ds(pl.multiple_of(col, HD), HD)
-    v_at = pl.ds(pl.multiple_of(col + WIDTH, HD), HD)
-    for j, part in enumerate((own_ref, w1_ref, w2_ref, w3_ref)):
-        span = slice(j * rows, (j + 1) * rows)
-        raw = part[:rows, k_at].astype(f32)
-        k_buf[span, :] = turn(raw, cos_ref[span, :], sin_ref[span, :]).astype(bf16)
-        v_buf[span, :] = part[:rows, v_at]
+    col = pl.program_id(0) * (PAIR * HD)
+    k_at = [pl.ds(pl.multiple_of(col + p * HD, HD), HD) for p in range(PAIR)]
+    v_at = [pl.ds(pl.multiple_of(col + p * HD + WIDTH, HD), HD) for p in range(PAIR)]
+    for p in range(PAIR):
+        for j, part in enumerate((own_ref, w1_ref, w2_ref, w3_ref)):
+            span = slice(j * rows, (j + 1) * rows)
+            raw = part[:rows, k_at[p]].astype(f32)
+            k_buf[p, span, :] = turn(raw, cos_ref[span, :], sin_ref[span, :]).astype(bf16)
+            v_buf[p, span, :] = part[:rows, v_at[p]]
     span = slice(SPAN * rows, SPAN * rows + 4 * few + 2 * half)
 
     def prompt(at):
@@ -135,9 +137,10 @@
         p_buf[4 * few :, :] = others_ref[:, at].astype(f32)
         return p_buf[...]
 
-    k_buf[span, :] = turn(prompt(k_at), cos_ref[span, :], sin_ref[span, :]).astype(bf16)
-    v_buf[span, :] = prompt(v_at).astype(bf16)
-    k, v = k_buf[...], v_buf[...]
+    for p in range(PAIR):
+        k_buf[p, span, :] = turn(prompt(k_at[p]), cos_ref[span, :], sin_ref[span, :]).astype(bf16)
+        v_buf[p, span, :] = prompt(v_at[p]).astype(bf16)
+    keys, vals = [k_buf[p] for p in range(PAIR)], [v_buf[p] for p in range(PAIR)]
     cosine, sine = cos_ref[:rows, :], sin_ref[:rows, :]
     lower = lax.broadcasted_iota(jnp.int32, (rows, rows), 1) <= lax.broadcasted_iota(
         jnp.int32, (rows, rows), 0
@@ -150,7 +153,7 @@
     def open_head(h):
         q = turn(q_ref[:, cols(h)].astype(f32), cosine, sine).astype(bf16)
         g = g_ref[:, cols(h)]
-        return q, g, dot(q, k, 1, 1), dot(g, v, 1, 1)
+        return q, g, dot(q, keys[h // GROUP], 1, 1), dot(g, vals[h // GROUP], 1, 1)
 
     def weigh(s):
         s_own = jnp.where(lower, s[:, :rows], HIDDEN)
@@ -171,32 +174,35 @@
         return jnp.concatenate(e, axis=1) * (1.0 / total)
 
     def close_head(h, ds, wb, q, g):
-        dq_ref[:, cols(h)] = turn(dot(ds, k, 1, 0), cosine, -sine).astype(bf16)
+        dq_ref[:, cols(h)] = turn(dot(ds, keys[h // GROUP], 1, 0), cosine, -sine).astype(bf16)
         dk, dv = dot(ds, q, 0, 0), dot(wb, g, 0, 0)
-        if h == 0:
-            dk_buf[...] = dk
-            dv_buf[...] = dv
+        p = h // GROUP
+        if h % GROUP == 0:
+            dk_buf[p] = dk
+            dv_buf[p] = dv
         else:
-            dk_buf[...] += dk
-            dv_buf[...] += dv
+            dk_buf[p] += dk
+            dv_buf[p] += dv
 
     ahead, behind = open_head(0), None
-    for h in range(GROUP):
+    for h in range(PAIR * GROUP):
         q, g, s, dw = ahead
-        if h + 1 < GROUP:
+        if h + 1 < PAIR * GROUP:
             ahead = open_head(h + 1)
         if behind is not None:
             close_head(*behind)
         w = weigh(s)
         wb = w.astype(bf16)
-        o = dot(wb, v, 1, 0).astype(bf16)
+        o = dot(wb, vals[h // GROUP], 1, 0).astype(bf16)
         o_ref[:, cols(h)] = o
         delta = jnp.sum(o.astype(f32) * g.astype(f32), axis=1, keepdims=True)
         behind = (h, (w * (dw - delta) * SCALE).astype(bf16), wb, q, g)
     close_head(*behind)
 
     start = SPAN * rows
-    for at, buf in ((k_at, dk_buf), (v_at, dv_buf)):
+    pairs = [(k_at[p], dk_buf.at[p]) for p in range(PAIR)]
+    pairs += [(v_at[p], dv_buf.at[p]) for p in range(PAIR)]
+    for at, buf in pairs:
         for j, out in enumerate((d0_ref, d1_ref, d2_ref, d3_ref)):
             out[:rows, at] = buf[j * rows : (j + 1) * rows, :].astype(out.dtype)
         for j in range(2):
@@ -214,17 +220,17 @@
     few, half = prompts[0].shape[0], prompts[2].shape[0] // 2
     keys = SPAN * rows + 4 * few + 2 * half
     part = half + 2 * few
-    head = pl.BlockSpec((rows, GROUP * HD), lambda i, s: (0, i))
+    head = pl.BlockSpec((rows, PAIR * GROUP * HD), lambda i, s: (0, i))
     outs = [(rows, f32), (rows, bf16), (rows, f32), (rows + part, f32), (part, f32)]
     return pl.pallas_call(
         attend_kernel,
         grid_spec=pltpu.PrefetchScalarGridSpec(
             num_scalar_prefetch=1,
-            grid=(KVH,),
+            grid=(KVH // PAIR,),
             in_specs=[head, head] + [IN_VMEM] * 9,
             out_specs=[head, head] + [IN_VMEM] * 5,
-            scratch_shapes=[pltpu.VMEM((keys, HD), bf16)] * 2
-            + [pltpu.VMEM((keys, HD), f32)] * 2
+            scratch_shapes=[pltpu.VMEM((PAIR, keys, HD), bf16)] * 2
+            + [pltpu.VMEM((PAIR, keys, HD), f32)] * 2
             + [pltpu.VMEM((2 * part, HD), f32)],
         ),
         out_shape=[jax.ShapeDtypeStruct(queries.shape, bf16)] * 2

time: 78.5 us -> 77.5 us (0.987)
  Pallas kernels: 29.5 us -> 28.5 us
    pallas_call x1, Pallas kernels: 27.2 us -> 26.2 us  [attend(): pl.pallas_call(attend_kernel, grid_spec=pltpu.PrefetchScalarGridSpec(num_...]
where the time goes in v7:
time: 77.5 us; the launch traced here: 77.2 us
  Pallas kernels  28.5 us (37%)
  waiting for transfers between devices  23 us (30%)
  starting transfers between devices  20 us (26%)
  other arithmetic  4.53 us (6%)
  between operations  0.81 us (1%)
    pallas_call x1, Pallas kernels, attend(): pl.pallas_call(attend_kernel, grid_spec=pltpu.PrefetchScalarGridSpec(num_...  26.2 us
    ppermute x16, waiting for transfers between devices, permute(): return lax.ppermute(value, 'ctx', pairs)  23 us
    ppermute x16, starting transfers between devices, permute(): return lax.ppermute(value, 'ctx', pairs)  20 us
    mul x1, other arithmetic, angle_tables(): return (jnp.cos(angles), jnp.sin(angles) * sign[None, :])  2.01 us
  transfers between devices with their start and end apart: 16, of which 5 were waited for; matrix products, arithmetic and copies ran while one was open for 6% of the time, Pallas kernels for 0%

profile of v7, /device:TPU:0, one launch (start us, length us, event | category | flops | bytes accessed | tf_op | source)
XLA Modules:
  0.0 77.2 jit_solution(6188549097681728965)
XLA Ops:
  0.6 1.1 %pack.1 = (bf16[264,1024]{1,0:T(8,128)(2,1)S(1)}, bf16[4,1024]{1,0:T(4,128)(2,1)S(1)}) custom-call(bf16[256,512]{1,0:T(8,128)(2,1)} %k_ref.1, bf16[256,512]{1,0:T(8,128)(2,1)} %v_ref.1, bf16[4,512]{1,0:T(4,128)(2,1)} %pk_ref.1, bf16[4,512]{1,0:T(4,128)(2,1)} %pv_ref.1), custom_call_target="tpu_custom_call" | custom-call | tf_op jit(solution)/shard_map/pack/pallas_call | solution.py:82
  1.7 0.5 collective-permute-start
  2.3 2.6 %collective-permute-start.2 = (bf16[264,1024]{1,0:T(8,128)(2,1)S(1)}, bf16[264,1024]{1,0:T(8,128)(2,1)S(1)}, u32[]{:S(2)}, u32[]{:S(2)}) collective-permute-start(bf16[264,1024]{1,0:T(8,128)(2,1)S(1)} %get-tuple-element.31.own_ref), channel_id=1, source_target_pairs={{0,2},{1,3},{2,4},{3,5},{4,6},{5,7},{6,8},{7,9},{8,10},{9,11},{10,... | collective-permute-start | bytes 1622024 | tf_op jit(solution)/shard_map/ppermute | solution.py:30
  4.8 0.9 %select_reduce_fusion = (s32[4]{0:T(128)S(1)}, s32[4]{0:T(128)S(1)}) fusion(s32[16]{0:T(128)} %bitcast.9, s32[4]{0:T(128)S(1)} %fusion.10, pred[16]{0:T(512)(128)(4,1)S(1)} %iota_compare_fusion.2), kind=kLoop, calls=%fused_computation.12 | loop fusion | flops 440 | bytes 128 | tf_op jit(solution)/shard_map/reduce_sum | solution.py:363
  5.7 0.7 broadcast_select_fusion.1
  6.6 0.7 subtract_bitcast_fusion
  7.6 1.6 %collective-permute-start.4 = (bf16[8,1024]{1,0:T(8,128)(2,1)S(1)}, bf16[8,1024]{1,0:T(8,128)(2,1)S(1)}, u32[]{:S(2)}, u32[]{:S(2)}) collective-permute-start(bf16[8,1024]{1,0:T(8,128)(2,1)S(1)} %pad_maximum_fusion), channel_id=1, source_target_pairs={{0,4},{1,11},{2,6},{3,13},{4,8},{5,15},{6,10},{7,1},{8,12},{9,3},{... | collective-permute-start | bytes 49160 | tf_op jit(solution)/shard_map/ppermute | solution.py:30
  9.2 2.6 %collective-permute-start.6 = (bf16[8,1024]{1,0:T(8,128)(2,1)S(1)}, bf16[8,1024]{1,0:T(8,128)(2,1)S(1)}, u32[]{:S(2)}, u32[]{:S(2)}) collective-permute-start(bf16[8,1024]{1,0:T(8,128)(2,1)S(1)} %pad_maximum_fusion), channel_id=1, source_target_pairs={{0,8},{1,15},{2,10},{3,1},{4,12},{5,3},{6,14},{7,5},{8,0},{9,7},{1... | collective-permute-start | bytes 49160 | tf_op jit(solution)/shard_map/ppermute | solution.py:30
  11.8 1.2 %collective-permute-start.5 = (bf16[8,1024]{1,0:T(8,128)(2,1)S(1)}, bf16[8,1024]{1,0:T(8,128)(2,1)S(1)}, u32[]{:S(2)}, u32[]{:S(2)}) collective-permute-start(bf16[8,1024]{1,0:T(8,128)(2,1)S(1)} %pad_maximum_fusion), channel_id=1, source_target_pairs={{0,6},{1,13},{2,8},{3,15},{4,10},{5,1},{6,12},{7,3},{8,14},{9,5},{... | collective-permute-start | bytes 49160 | tf_op jit(solution)/shard_map/ppermute | solution.py:30
  13.0 1.3 %collective-permute-start.1 = (bf16[264,1024]{1,0:T(8,128)(2,1)S(1)}, bf16[264,1024]{1,0:T(8,128)(2,1)S(1)}, u32[]{:S(2)}, u32[]{:S(2)}) collective-permute-start(bf16[264,1024]{1,0:T(8,128)(2,1)S(1)} %get-tuple-element.31.own_ref), channel_id=1, source_target_pairs={{0,1},{2,3},{4,5},{6,7},{8,9},{10,11},{12,13},{14,15},{1,4},{3,6},... | collective-permute-start | bytes 1622024 | tf_op jit(solution)/shard_map/ppermute | solution.py:30
  14.3 7.6 %collective-permute-done.5 = bf16[8,1024]{1,0:T(8,128)(2,1)S(1)} collective-permute-done((bf16[8,1024]{1,0:T(8,128)(2,1)S(1)}, bf16[8,1024]{1,0:T(8,128)(2,1)S(1)}, u32[]{:S(2)}, u32[]{:S(2)}) %collective-permute-start.5) | collective-permute-done | bytes 16416 | tf_op jit(solution)/shard_map/ppermute | solution.py:30
  22.0 0.5 collective-permute-start.7
  22.5 2.0 %fusion = (f32[1088,128]{1,0:T(8,128)S(1)}, f32[1088,128]{1,0:T(8,128)S(1)}) fusion(f32[128]{0:T(128)S(1)} %get-tuple-element.60, f32[128]{0:T(128)S(1)} %get-tuple-element.61, f32[1088]{0:T(1024)S(1)} %add_convert_fusion), kind=kLoop, calls=%fused_computation.2 | loop fusion | flops 278528 | bytes 1119488 | tf_op jit(solution)/shard_map/mul | solution.py:42
  24.6 26.2 %attend.1 = (bf16[256,2560]{1,0:T(8,128)(2,1)}, bf16[256,2560]{1,0:T(8,128)(2,1)}, f32[256,1024]{1,0:T(8,128)S(1)}, bf16[256,1024]{1,0:T(8,128)(2,1)S(1)}, f32[2...) custom-call(s32[3]{0:T(128)S(1)} %slice.3.seen, bf16[256,2560]{1,0:T(8,128)(2,1)} %q_ref.1, ...), custom_call_target="tpu_custom_call" | custom-call | tf_op jit(solution)/shard_map/attend/pallas_call | solution.py:225
  50.9 1.3 %collective-permute-start.8 = (bf16[256,1024]{1,0:T(8,128)(2,1)S(1)}, bf16[256,1024]{1,0:T(8,128)(2,1)S(1)}, u32[]{:S(2)}, u32[]{:S(2)}) collective-permute-start(bf16[256,1024]{1,0:T(8,128)(2,1)S(1)} %get-tuple-element.35), channel_id=1, source_target_pairs={{1,0},{3,2},{5,4},{7,6},{9,8},{11,10},{13,12},{15,14},{4,1},{6,3},... | collective-permute-start | bytes 1572872 | tf_op jit(solution)/shard_map/ppermute | solution.py:30
  52.2 1.5 %collective-permute-done.9.r3_ref = f32[288,1024]{1,0:T(8,128)S(1)} collective-permute-done((f32[288,1024]{1,0:T(8,128)S(1)}, f32[288,1024]{1,0:T(8,128)S(1)}, u32[]{:S(2)}, u32[]{:S(2)}) %collective-permute-start.9) | collective-permute-done | bytes 1179680 | tf_op jit(solution)/shard_map/ppermute | solution.py:30
  53.8 4.6 %collective-permute-start.10 = (bf16[264,512]{1,0:T(8,128)(2,1)S(1)}, bf16[264,512]{1,0:T(8,128)(2,1)S(1)}, u32[]{:S(2)}, u32[]{:S(2)}) collective-permute-start(bf16[264,512]{1,0:T(8,128)(2,1)S(1)} %get-tuple-element.39), channel_id=1, source_target_pairs={{2,0},{3,1},{4,2},{5,3},{6,4},{7,5},{8,6},{9,7},{10,8},{11,9},{12,... | collective-permute-start | bytes 811016 | tf_op jit(solution)/shard_map/ppermute | solution.py:30
  58.3 0.8 %collective-permute-start.11 = (f32[8,1024]{1,0:T(8,128)S(1)}, f32[8,1024]{1,0:T(8,128)S(1)}, u32[]{:S(2)}, u32[]{:S(2)}) collective-permute-start(f32[8,1024]{1,0:T(8,128)S(1)} %get-tuple-element.41), channel_id=1, source_target_pairs={{4,0},{11,1},{6,2},{13,3},{8,4},{15,5},{10,6},{1,7},{12,8},{3,9},{... | collective-permute-start | bytes 98312 | tf_op jit(solution)/shard_map/ppermute | solution.py:30
  59.1 2.2 %collective-permute-start.13 = (f32[8,1024]{1,0:T(8,128)S(1)}, f32[8,1024]{1,0:T(8,128)S(1)}, u32[]{:S(2)}, u32[]{:S(2)}) collective-permute-start(f32[8,1024]{1,0:T(8,128)S(1)} %get-tuple-element.43), channel_id=1, source_target_pairs={{8,0},{15,1},{10,2},{1,3},{12,4},{3,5},{14,6},{5,7},{0,8},{7,9},{2... | collective-permute-start | bytes 98312 | tf_op jit(solution)/shard_map/ppermute | solution.py:30
  61.3 8.2 %collective-permute-done.11.refs_0_ = f32[8,1024]{1,0:T(8,128)S(1)} collective-permute-done((f32[8,1024]{1,0:T(8,128)S(1)}, f32[8,1024]{1,0:T(8,128)S(1)}, u32[]{:S(2)}, u32[]{:S(2)}) %collective-permute-start.11) | collective-permute-done | bytes 32800 | tf_op jit(solution)/shard_map/ppermute | solution.py:30
  69.5 0.8 collective-permute-start.14
  70.4 1.2 %collective-permute-done.15.got_ref = f32[4,1024]{1,0:T(4,128)S(1)} collective-permute-done((f32[4,1024]{1,0:T(4,128)S(1)}, f32[4,1024]{1,0:T(4,128)S(1)}, u32[]{:S(2)}, u32[]{:S(2)}) %collective-permute-start.15) | collective-permute-done | bytes 16416 | tf_op jit(solution)/shard_map/ppermute | solution.py:30
  71.6 4.5 %collective-permute-done.14.rv_ref = bf16[264,512]{1,0:T(8,128)(2,1)S(1)} collective-permute-done((bf16[264,512]{1,0:T(8,128)(2,1)S(1)}, bf16[264,512]{1,0:T(8,128)(2,1)S(1)}, u32[]{:S(2)}, u32[]{:S(2)}) %collective-permute-start.14) | collective-permute-done | bytes 270368 | tf_op jit(solution)/shard_map/ppermute | solution.py:30
  76.1 1.1 %finish.1 = (bf16[256,512]{1,0:T(8,128)(2,1)}, bf16[256,512]{1,0:T(8,128)(2,1)}, bf16[4,512]{1,0:T(4,128)(2,1)}, bf16[4,512]{1,0:T(4,128)(2,1)}) custom-call(f32[256,1024]{1,0:T(8,128)S(1)} %get-tuple-element.34.d0_ref, bf16[256,1024]{1,0:T(8,128)(2,1)S(1)} %collective-permute-done.8.after_ref.r1_ref, ...), custom_call_target="tpu_custom_call" | custom-call | tf_op jit(solution)/shard_map/finish/pallas_call | solution.py:323
  (37 shorter events, 0.8 us)
Async XLA Ops:
  1.7 5.8 %collective-permute-start = (bf16[4,1024]{1,0:T(4,128)(2,1)S(1)}, bf16[4,1024]{1,0:T(4,128)(2,1)S(1)}, u32[]{:S(2)}, u32[]{:S(2)}) collective-permute-start(bf16[4,1024]{1,0:T(4,128)(2,1)S(1)} %get-tuple-element.30.mine_ref), channel_id=1, source_target_pairs={{0,1},{1,0},{2,3},{3,2},{4,5},{5,4},{6,7},{7,6},{8,9},{9,8},{10,11... | collective-permute-start | bytes 24584 | tf_op jit(solution)/shard_map/ppermute | solution.py:30
  2.3 19.7 %collective-permute-start.2 = (bf16[264,1024]{1,0:T(8,128)(2,1)S(1)}, bf16[264,1024]{1,0:T(8,128)(2,1)S(1)}, u32[]{:S(2)}, u32[]{:S(2)}) collective-permute-start(bf16[264,1024]{1,0:T(8,128)(2,1)S(1)} %get-tuple-element.31.own_ref), channel_id=1, source_target_pairs={{0,2},{1,3},{2,4},{3,5},{4,6},{5,7},{6,8},{7,9},{8,10},{9,11},{10,... | collective-permute-start | bytes 1622024 | tf_op jit(solution)/shard_map/ppermute | solution.py:30
  7.6 6.7 %collective-permute-start.4 = (bf16[8,1024]{1,0:T(8,128)(2,1)S(1)}, bf16[8,1024]{1,0:T(8,128)(2,1)S(1)}, u32[]{:S(2)}, u32[]{:S(2)}) collective-permute-start(bf16[8,1024]{1,0:T(8,128)(2,1)S(1)} %pad_maximum_fusion), channel_id=1, source_target_pairs={{0,4},{1,11},{2,6},{3,13},{4,8},{5,15},{6,10},{7,1},{8,12},{9,3},{... | collective-permute-start | bytes 49160 | tf_op jit(solution)/shard_map/ppermute | solution.py:30
  9.2 12.8 %collective-permute-start.6 = (bf16[8,1024]{1,0:T(8,128)(2,1)S(1)}, bf16[8,1024]{1,0:T(8,128)(2,1)S(1)}, u32[]{:S(2)}, u32[]{:S(2)}) collective-permute-start(bf16[8,1024]{1,0:T(8,128)(2,1)S(1)} %pad_maximum_fusion), channel_id=1, source_target_pairs={{0,8},{1,15},{2,10},{3,1},{4,12},{5,3},{6,14},{7,5},{8,0},{9,7},{1... | collective-permute-start | bytes 49160 | tf_op jit(solution)/shard_map/ppermute | solution.py:30
  11.8 10.2 %collective-permute-start.5 = (bf16[8,1024]{1,0:T(8,128)(2,1)S(1)}, bf16[8,1024]{1,0:T(8,128)(2,1)S(1)}, u32[]{:S(2)}, u32[]{:S(2)}) collective-permute-start(bf16[8,1024]{1,0:T(8,128)(2,1)S(1)} %pad_maximum_fusion), channel_id=1, source_target_pairs={{0,6},{1,13},{2,8},{3,15},{4,10},{5,1},{6,12},{7,3},{8,14},{9,5},{... | collective-permute-start | bytes 49160 | tf_op jit(solution)/shard_map/ppermute | solution.py:30
  13.0 11.6 %collective-permute-start.1 = (bf16[264,1024]{1,0:T(8,128)(2,1)S(1)}, bf16[264,1024]{1,0:T(8,128)(2,1)S(1)}, u32[]{:S(2)}, u32[]{:S(2)}) collective-permute-start(bf16[264,1024]{1,0:T(8,128)(2,1)S(1)} %get-tuple-element.31.own_ref), channel_id=1, source_target_pairs={{0,1},{2,3},{4,5},{6,7},{8,9},{10,11},{12,13},{14,15},{1,4},{3,6},... | collective-permute-start | bytes 1622024 | tf_op jit(solution)/shard_map/ppermute | solution.py:30
  22.0 2.6 %collective-permute-start.3 = (bf16[264,1024]{1,0:T(8,128)(2,1)S(1)}, bf16[264,1024]{1,0:T(8,128)(2,1)S(1)}, u32[]{:S(2)}, u32[]{:S(2)}) collective-permute-start(bf16[264,1024]{1,0:T(8,128)(2,1)S(1)} %collective-permute-done.2.w2_ref), channel_id=1, source_target_pairs={{0,1},{1,0},{2,3},{3,2},{4,5},{5,4},{6,7},{7,6},{8,9},{9,8},{10,11... | collective-permute-start | bytes 1622024 | tf_op jit(solution)/shard_map/ppermute | solution.py:30
  22.0 2.6 %collective-permute-start.7 = (bf16[24,1024]{1,0:T(8,128)(2,1)S(1)}, bf16[24,1024]{1,0:T(8,128)(2,1)S(1)}, u32[]{:S(2)}, u32[]{:S(2)}) collective-permute-start(bf16[24,1024]{1,0:T(8,128)(2,1)S(1)} %constant_dynamic-update-slice_fusion.near_ref), channel_id=1, source_target_pairs={{0,1},{1,0},{2,3},{3,2},{4,5},{5,4},{6,7},{7,6},{8,9},{9,8},{10,11... | collective-permute-start | bytes 147464 | tf_op jit(solution)/shard_map/ppermute | solution.py:30
  50.8 2.8 %collective-permute-start.9 = (f32[288,1024]{1,0:T(8,128)S(1)}, f32[288,1024]{1,0:T(8,128)S(1)}, u32[]{:S(2)}, u32[]{:S(2)}) collective-permute-start(f32[288,1024]{1,0:T(8,128)S(1)} %get-tuple-element.37), channel_id=1, source_target_pairs={{0,1},{1,0},{2,3},{3,2},{4,5},{5,4},{6,7},{7,6},{8,9},{9,8},{10,11... | collective-permute-start | bytes 3538952 | tf_op jit(solution)/shard_map/ppermute | solution.py:30
  50.9 10.4 %collective-permute-start.8 = (bf16[256,1024]{1,0:T(8,128)(2,1)S(1)}, bf16[256,1024]{1,0:T(8,128)(2,1)S(1)}, u32[]{:S(2)}, u32[]{:S(2)}) collective-permute-start(bf16[256,1024]{1,0:T(8,128)(2,1)S(1)} %get-tuple-element.35), channel_id=1, source_target_pairs={{1,0},{3,2},{5,4},{7,6},{9,8},{11,10},{13,12},{15,14},{4,1},{6,3},... | collective-permute-start | bytes 1572872 | tf_op jit(solution)/shard_map/ppermute | solution.py:30
  53.8 15.8 %collective-permute-start.10 = (bf16[264,512]{1,0:T(8,128)(2,1)S(1)}, bf16[264,512]{1,0:T(8,128)(2,1)S(1)}, u32[]{:S(2)}, u32[]{:S(2)}) collective-permute-start(bf16[264,512]{1,0:T(8,128)(2,1)S(1)} %get-tuple-element.39), channel_id=1, source_target_pairs={{2,0},{3,1},{4,2},{5,3},{6,4},{7,5},{8,6},{9,7},{10,8},{11,9},{12,... | collective-permute-start | bytes 811016 | tf_op jit(solution)/shard_map/ppermute | solution.py:30
  58.3 11.2 %collective-permute-start.11 = (f32[8,1024]{1,0:T(8,128)S(1)}, f32[8,1024]{1,0:T(8,128)S(1)}, u32[]{:S(2)}, u32[]{:S(2)}) collective-permute-start(f32[8,1024]{1,0:T(8,128)S(1)} %get-tuple-element.41), channel_id=1, source_target_pairs={{4,0},{11,1},{6,2},{13,3},{8,4},{15,5},{10,6},{1,7},{12,8},{3,9},{... | collective-permute-start | bytes 98312 | tf_op jit(solution)/shard_map/ppermute | solution.py:30
  59.1 10.4 %collective-permute-start.12 = (f32[8,1024]{1,0:T(8,128)S(1)}, f32[8,1024]{1,0:T(8,128)S(1)}, u32[]{:S(2)}, u32[]{:S(2)}) collective-permute-start(f32[8,1024]{1,0:T(8,128)S(1)} %get-tuple-element.42), channel_id=1, source_target_pairs={{6,0},{13,1},{8,2},{15,3},{10,4},{1,5},{12,6},{3,7},{14,8},{5,9},{... | collective-permute-start | bytes 98312 | tf_op jit(solution)/shard_map/ppermute | solution.py:30
  59.1 10.4 %collective-permute-start.13 = (f32[8,1024]{1,0:T(8,128)S(1)}, f32[8,1024]{1,0:T(8,128)S(1)}, u32[]{:S(2)}, u32[]{:S(2)}) collective-permute-start(f32[8,1024]{1,0:T(8,128)S(1)} %get-tuple-element.43), channel_id=1, source_target_pairs={{8,0},{15,1},{10,2},{1,3},{12,4},{3,5},{14,6},{5,7},{0,8},{7,9},{2... | collective-permute-start | bytes 98312 | tf_op jit(solution)/shard_map/ppermute | solution.py:30
  69.5 6.5 %collective-permute-start.14 = (bf16[264,512]{1,0:T(8,128)(2,1)S(1)}, bf16[264,512]{1,0:T(8,128)(2,1)S(1)}, u32[]{:S(2)}, u32[]{:S(2)}) collective-permute-start(bf16[264,512]{1,0:T(8,128)(2,1)S(1)} %get-tuple-element.44), channel_id=1, source_target_pairs={{2,0},{3,1},{4,2},{5,3},{6,4},{7,5},{8,6},{9,7},{10,8},{11,9},{12,... | collective-permute-start | bytes 811016 | tf_op jit(solution)/shard_map/ppermute | solution.py:30
  70.3 1.2 %collective-permute-start.15 = (f32[4,1024]{1,0:T(4,128)S(1)}, f32[4,1024]{1,0:T(4,128)S(1)}, u32[]{:S(2)}, u32[]{:S(2)}) collective-permute-start(f32[4,1024]{1,0:T(4,128)S(1)} %get-tuple-element.47), channel_id=1, source_target_pairs={{0,1},{1,0},{2,3},{3,2},{4,5},{5,4},{6,7},{7,6},{8,9},{9,8},{10,11... | collective-permute-start | bytes 49160 | tf_op jit(solution)/shard_map/ppermute | solution.py:30

commit v8 on v7

--- a/solution.py
+++ b/solution.py
@@ -13,7 +13,6 @@
 WIDTH = KVH * HD
 SPAN = 4
 SCALE = HD**-0.5
-LOG2E = 1.4426950408889634
 HIDDEN = -1e30
 
 rope_base = 1000000.0
@@ -164,11 +163,11 @@
         )
         for i in range(3):
             peak = jnp.maximum(peak, jnp.max(s_win[i], axis=1, keepdims=True) + bias[i])
-        base = peak * (SCALE * LOG2E)
+        base = peak * SCALE
         e = (
-            [jnp.exp2(s_own * (SCALE * LOG2E) - base)]
-            + [jnp.exp2(s_win[i] * (SCALE * LOG2E) - (base - bias[i])) for i in range(3)]
-            + [jnp.exp2(s_pr * (SCALE * LOG2E) - base)]
+            [jnp.exp(s_own * SCALE - base)]
+            + [jnp.exp(s_win[i] * SCALE - (base - bias[i])) for i in range(3)]
+            + [jnp.exp(s_pr * SCALE - base)]
         )
         total = sum(jnp.sum(x, axis=1, keepdims=True) for x in e)
         return jnp.concatenate(e, axis=1) * (1.0 / total)

time: 77.5 us -> 77.8 us (level)
  no operation moved by 1% of the time
where the time goes in v8:
time: 77.8 us; the launch traced here: 77.6 us
  Pallas kernels  28.9 us (37%)
  waiting for transfers between devices  23 us (30%)
  starting transfers between devices  20 us (26%)
  other arithmetic  4.53 us (6%)
  between operations  0.81 us (1%)
    pallas_call x1, Pallas kernels, attend(): pl.pallas_call(attend_kernel, grid_spec=pltpu.PrefetchScalarGridSpec(num_...  26.5 us
    ppermute x16, waiting for transfers between devices, permute(): return lax.ppermute(value, 'ctx', pairs)  23 us
    ppermute x16, starting transfers between devices, permute(): return lax.ppermute(value, 'ctx', pairs)  20 us
    mul x1, other arithmetic, angle_tables(): return (jnp.cos(angles), jnp.sin(angles) * sign[None, :])  2.01 us
  transfers between devices with their start and end apart: 16, of which 5 were waited for; matrix products, arithmetic and copies ran while one was open for 6% of the time, Pallas kernels for 0%

profile of v8, /device:TPU:0, one launch (start us, length us, event | category | flops | bytes accessed | tf_op | source)
XLA Modules:
  0.0 77.6 jit_solution(16567126333248643837)
XLA Ops:
  0.6 1.1 %pack.1 = (bf16[264,1024]{1,0:T(8,128)(2,1)S(1)}, bf16[4,1024]{1,0:T(4,128)(2,1)S(1)}) custom-call(bf16[256,512]{1,0:T(8,128)(2,1)} %k_ref.1, bf16[256,512]{1,0:T(8,128)(2,1)} %v_ref.1, bf16[4,512]{1,0:T(4,128)(2,1)} %pk_ref.1, bf16[4,512]{1,0:T(4,128)(2,1)} %pv_ref.1), custom_call_target="tpu_custom_call" | custom-call | tf_op jit(solution)/shard_map/pack/pallas_call | solution.py:81
  1.7 0.5 collective-permute-start
  2.3 2.6 %collective-permute-start.2 = (bf16[264,1024]{1,0:T(8,128)(2,1)S(1)}, bf16[264,1024]{1,0:T(8,128)(2,1)S(1)}, u32[]{:S(2)}, u32[]{:S(2)}) collective-permute-start(bf16[264,1024]{1,0:T(8,128)(2,1)S(1)} %get-tuple-element.31.own_ref), channel_id=1, source_target_pairs={{0,2},{1,3},{2,4},{3,5},{4,6},{5,7},{6,8},{7,9},{8,10},{9,11},{10,... | collective-permute-start | bytes 1622024 | tf_op jit(solution)/shard_map/ppermute | solution.py:29
  4.8 0.9 %select_reduce_fusion = (s32[4]{0:T(128)S(1)}, s32[4]{0:T(128)S(1)}) fusion(s32[16]{0:T(128)} %bitcast.9, s32[4]{0:T(128)S(1)} %fusion.10, pred[16]{0:T(512)(128)(4,1)S(1)} %iota_compare_fusion.2), kind=kLoop, calls=%fused_computation.12 | loop fusion | flops 440 | bytes 128 | tf_op jit(solution)/shard_map/reduce_sum | solution.py:362
  5.7 0.7 broadcast_select_fusion.1
  6.6 0.7 subtract_bitcast_fusion
  7.6 1.6 %collective-permute-start.4 = (bf16[8,1024]{1,0:T(8,128)(2,1)S(1)}, bf16[8,1024]{1,0:T(8,128)(2,1)S(1)}, u32[]{:S(2)}, u32[]{:S(2)}) collective-permute-start(bf16[8,1024]{1,0:T(8,128)(2,1)S(1)} %pad_maximum_fusion), channel_id=1, source_target_pairs={{0,4},{1,11},{2,6},{3,13},{4,8},{5,15},{6,10},{7,1},{8,12},{9,3},{... | collective-permute-start | bytes 49160 | tf_op jit(solution)/shard_map/ppermute | solution.py:29
  9.2 2.6 %collective-permute-start.6 = (bf16[8,1024]{1,0:T(8,128)(2,1)S(1)}, bf16[8,1024]{1,0:T(8,128)(2,1)S(1)}, u32[]{:S(2)}, u32[]{:S(2)}) collective-permute-start(bf16[8,1024]{1,0:T(8,128)(2,1)S(1)} %pad_maximum_fusion), channel_id=1, source_target_pairs={{0,8},{1,15},{2,10},{3,1},{4,12},{5,3},{6,14},{7,5},{8,0},{9,7},{1... | collective-permute-start | bytes 49160 | tf_op jit(solution)/shard_map/ppermute | solution.py:29
  11.8 1.2 %collective-permute-start.5 = (bf16[8,1024]{1,0:T(8,128)(2,1)S(1)}, bf16[8,1024]{1,0:T(8,128)(2,1)S(1)}, u32[]{:S(2)}, u32[]{:S(2)}) collective-permute-start(bf16[8,1024]{1,0:T(8,128)(2,1)S(1)} %pad_maximum_fusion), channel_id=1, source_target_pairs={{0,6},{1,13},{2,8},{3,15},{4,10},{5,1},{6,12},{7,3},{8,14},{9,5},{... | collective-permute-start | bytes 49160 | tf_op jit(solution)/shard_map/ppermute | solution.py:29
  13.0 1.3 %collective-permute-start.1 = (bf16[264,1024]{1,0:T(8,128)(2,1)S(1)}, bf16[264,1024]{1,0:T(8,128)(2,1)S(1)}, u32[]{:S(2)}, u32[]{:S(2)}) collective-permute-start(bf16[264,1024]{1,0:T(8,128)(2,1)S(1)} %get-tuple-element.31.own_ref), channel_id=1, source_target_pairs={{0,1},{2,3},{4,5},{6,7},{8,9},{10,11},{12,13},{14,15},{1,4},{3,6},... | collective-permute-start | bytes 1622024 | tf_op jit(solution)/shard_map/ppermute | solution.py:29
  14.3 7.6 %collective-permute-done.5 = bf16[8,1024]{1,0:T(8,128)(2,1)S(1)} collective-permute-done((bf16[8,1024]{1,0:T(8,128)(2,1)S(1)}, bf16[8,1024]{1,0:T(8,128)(2,1)S(1)}, u32[]{:S(2)}, u32[]{:S(2)}) %collective-permute-start.5) | collective-permute-done | bytes 16416 | tf_op jit(solution)/shard_map/ppermute | solution.py:29
  22.0 0.5 collective-permute-start.7
  22.5 2.0 %fusion = (f32[1088,128]{1,0:T(8,128)S(1)}, f32[1088,128]{1,0:T(8,128)S(1)}) fusion(f32[128]{0:T(128)S(1)} %get-tuple-element.60, f32[128]{0:T(128)S(1)} %get-tuple-element.61, f32[1088]{0:T(1024)S(1)} %add_convert_fusion), kind=kLoop, calls=%fused_computation.2 | loop fusion | flops 278528 | bytes 1119488 | tf_op jit(solution)/shard_map/mul | solution.py:41
  24.6 26.5 %attend.1 = (bf16[256,2560]{1,0:T(8,128)(2,1)}, bf16[256,2560]{1,0:T(8,128)(2,1)}, f32[256,1024]{1,0:T(8,128)S(1)}, bf16[256,1024]{1,0:T(8,128)(2,1)S(1)}, f32[2...) custom-call(s32[3]{0:T(128)S(1)} %slice.3.seen, bf16[256,2560]{1,0:T(8,128)(2,1)} %q_ref.1, ...), custom_call_target="tpu_custom_call" | custom-call | tf_op jit(solution)/shard_map/attend/pallas_call | solution.py:224
  51.3 1.3 %collective-permute-start.8 = (bf16[256,1024]{1,0:T(8,128)(2,1)S(1)}, bf16[256,1024]{1,0:T(8,128)(2,1)S(1)}, u32[]{:S(2)}, u32[]{:S(2)}) collective-permute-start(bf16[256,1024]{1,0:T(8,128)(2,1)S(1)} %get-tuple-element.35), channel_id=1, source_target_pairs={{1,0},{3,2},{5,4},{7,6},{9,8},{11,10},{13,12},{15,14},{4,1},{6,3},... | collective-permute-start | bytes 1572872 | tf_op jit(solution)/shard_map/ppermute | solution.py:29
  52.5 1.5 %collective-permute-done.9.r3_ref = f32[288,1024]{1,0:T(8,128)S(1)} collective-permute-done((f32[288,1024]{1,0:T(8,128)S(1)}, f32[288,1024]{1,0:T(8,128)S(1)}, u32[]{:S(2)}, u32[]{:S(2)}) %collective-permute-start.9) | collective-permute-done | bytes 1179680 | tf_op jit(solution)/shard_map/ppermute | solution.py:29
  54.1 4.6 %collective-permute-start.10 = (bf16[264,512]{1,0:T(8,128)(2,1)S(1)}, bf16[264,512]{1,0:T(8,128)(2,1)S(1)}, u32[]{:S(2)}, u32[]{:S(2)}) collective-permute-start(bf16[264,512]{1,0:T(8,128)(2,1)S(1)} %get-tuple-element.39), channel_id=1, source_target_pairs={{2,0},{3,1},{4,2},{5,3},{6,4},{7,5},{8,6},{9,7},{10,8},{11,9},{12,... | collective-permute-start | bytes 811016 | tf_op jit(solution)/shard_map/ppermute | solution.py:29
  58.7 0.8 %collective-permute-start.11 = (f32[8,1024]{1,0:T(8,128)S(1)}, f32[8,1024]{1,0:T(8,128)S(1)}, u32[]{:S(2)}, u32[]{:S(2)}) collective-permute-start(f32[8,1024]{1,0:T(8,128)S(1)} %get-tuple-element.41), channel_id=1, source_target_pairs={{4,0},{11,1},{6,2},{13,3},{8,4},{15,5},{10,6},{1,7},{12,8},{3,9},{... | collective-permute-start | bytes 98312 | tf_op jit(solution)/shard_map/ppermute | solution.py:29
  59.5 2.2 %collective-permute-start.13 = (f32[8,1024]{1,0:T(8,128)S(1)}, f32[8,1024]{1,0:T(8,128)S(1)}, u32[]{:S(2)}, u32[]{:S(2)}) collective-permute-start(f32[8,1024]{1,0:T(8,128)S(1)} %get-tuple-element.43), channel_id=1, source_target_pairs={{8,0},{15,1},{10,2},{1,3},{12,4},{3,5},{14,6},{5,7},{0,8},{7,9},{2... | collective-permute-start | bytes 98312 | tf_op jit(solution)/shard_map/ppermute | solution.py:29
  61.7 8.2 %collective-permute-done.11.refs_0_ = f32[8,1024]{1,0:T(8,128)S(1)} collective-permute-done((f32[8,1024]{1,0:T(8,128)S(1)}, f32[8,1024]{1,0:T(8,128)S(1)}, u32[]{:S(2)}, u32[]{:S(2)}) %collective-permute-start.11) | collective-permute-done | bytes 32800 | tf_op jit(solution)/shard_map/ppermute | solution.py:29
  69.9 0.8 collective-permute-start.14
  70.8 1.2 %collective-permute-done.15.got_ref = f32[4,1024]{1,0:T(4,128)S(1)} collective-permute-done((f32[4,1024]{1,0:T(4,128)S(1)}, f32[4,1024]{1,0:T(4,128)S(1)}, u32[]{:S(2)}, u32[]{:S(2)}) %collective-permute-start.15) | collective-permute-done | bytes 16416 | tf_op jit(solution)/shard_map/ppermute | solution.py:29
  71.9 4.5 %collective-permute-done.14.rv_ref = bf16[264,512]{1,0:T(8,128)(2,1)S(1)} collective-permute-done((bf16[264,512]{1,0:T(8,128)(2,1)S(1)}, bf16[264,512]{1,0:T(8,128)(2,1)S(1)}, u32[]{:S(2)}, u32[]{:S(2)}) %collective-permute-start.14) | collective-permute-done | bytes 270368 | tf_op jit(solution)/shard_map/ppermute | solution.py:29
  76.5 1.1 %finish.1 = (bf16[256,512]{1,0:T(8,128)(2,1)}, bf16[256,512]{1,0:T(8,128)(2,1)}, bf16[4,512]{1,0:T(4,128)(2,1)}, bf16[4,512]{1,0:T(4,128)(2,1)}) custom-call(f32[256,1024]{1,0:T(8,128)S(1)} %get-tuple-element.34.d0_ref, bf16[256,1024]{1,0:T(8,128)(2,1)S(1)} %collective-permute-done.8.after_ref.r1_ref, ...), custom_call_target="tpu_custom_call" | custom-call | tf_op jit(solution)/shard_map/finish/pallas_call | solution.py:322
  (37 shorter events, 0.8 us)
Async XLA Ops:
  1.7 5.8 %collective-permute-start = (bf16[4,1024]{1,0:T(4,128)(2,1)S(1)}, bf16[4,1024]{1,0:T(4,128)(2,1)S(1)}, u32[]{:S(2)}, u32[]{:S(2)}) collective-permute-start(bf16[4,1024]{1,0:T(4,128)(2,1)S(1)} %get-tuple-element.30.mine_ref), channel_id=1, source_target_pairs={{0,1},{1,0},{2,3},{3,2},{4,5},{5,4},{6,7},{7,6},{8,9},{9,8},{10,11... | collective-permute-start | bytes 24584 | tf_op jit(solution)/shard_map/ppermute | solution.py:29
  2.3 19.7 %collective-permute-start.2 = (bf16[264,1024]{1,0:T(8,128)(2,1)S(1)}, bf16[264,1024]{1,0:T(8,128)(2,1)S(1)}, u32[]{:S(2)}, u32[]{:S(2)}) collective-permute-start(bf16[264,1024]{1,0:T(8,128)(2,1)S(1)} %get-tuple-element.31.own_ref), channel_id=1, source_target_pairs={{0,2},{1,3},{2,4},{3,5},{4,6},{5,7},{6,8},{7,9},{8,10},{9,11},{10,... | collective-permute-start | bytes 1622024 | tf_op jit(solution)/shard_map/ppermute | solution.py:29
  7.6 6.7 %collective-permute-start.4 = (bf16[8,1024]{1,0:T(8,128)(2,1)S(1)}, bf16[8,1024]{1,0:T(8,128)(2,1)S(1)}, u32[]{:S(2)}, u32[]{:S(2)}) collective-permute-start(bf16[8,1024]{1,0:T(8,128)(2,1)S(1)} %pad_maximum_fusion), channel_id=1, source_target_pairs={{0,4},{1,11},{2,6},{3,13},{4,8},{5,15},{6,10},{7,1},{8,12},{9,3},{... | collective-permute-start | bytes 49160 | tf_op jit(solution)/shard_map/ppermute | solution.py:29
  9.2 12.8 %collective-permute-start.6 = (bf16[8,1024]{1,0:T(8,128)(2,1)S(1)}, bf16[8,1024]{1,0:T(8,128)(2,1)S(1)}, u32[]{:S(2)}, u32[]{:S(2)}) collective-permute-start(bf16[8,1024]{1,0:T(8,128)(2,1)S(1)} %pad_maximum_fusion), channel_id=1, source_target_pairs={{0,8},{1,15},{2,10},{3,1},{4,12},{5,3},{6,14},{7,5},{8,0},{9,7},{1... | collective-permute-start | bytes 49160 | tf_op jit(solution)/shard_map/ppermute | solution.py:29
  11.8 10.2 %collective-permute-start.5 = (bf16[8,1024]{1,0:T(8,128)(2,1)S(1)}, bf16[8,1024]{1,0:T(8,128)(2,1)S(1)}, u32[]{:S(2)}, u32[]{:S(2)}) collective-permute-start(bf16[8,1024]{1,0:T(8,128)(2,1)S(1)} %pad_maximum_fusion), channel_id=1, source_target_pairs={{0,6},{1,13},{2,8},{3,15},{4,10},{5,1},{6,12},{7,3},{8,14},{9,5},{... | collective-permute-start | bytes 49160 | tf_op jit(solution)/shard_map/ppermute | solution.py:29
  13.0 11.6 %collective-permute-start.1 = (bf16[264,1024]{1,0:T(8,128)(2,1)S(1)}, bf16[264,1024]{1,0:T(8,128)(2,1)S(1)}, u32[]{:S(2)}, u32[]{:S(2)}) collective-permute-start(bf16[264,1024]{1,0:T(8,128)(2,1)S(1)} %get-tuple-element.31.own_ref), channel_id=1, source_target_pairs={{0,1},{2,3},{4,5},{6,7},{8,9},{10,11},{12,13},{14,15},{1,4},{3,6},... | collective-permute-start | bytes 1622024 | tf_op jit(solution)/shard_map/ppermute | solution.py:29
  22.0 2.6 %collective-permute-start.3 = (bf16[264,1024]{1,0:T(8,128)(2,1)S(1)}, bf16[264,1024]{1,0:T(8,128)(2,1)S(1)}, u32[]{:S(2)}, u32[]{:S(2)}) collective-permute-start(bf16[264,1024]{1,0:T(8,128)(2,1)S(1)} %collective-permute-done.2.w2_ref), channel_id=1, source_target_pairs={{0,1},{1,0},{2,3},{3,2},{4,5},{5,4},{6,7},{7,6},{8,9},{9,8},{10,11... | collective-permute-start | bytes 1622024 | tf_op jit(solution)/shard_map/ppermute | solution.py:29
  22.0 2.6 %collective-permute-start.7 = (bf16[24,1024]{1,0:T(8,128)(2,1)S(1)}, bf16[24,1024]{1,0:T(8,128)(2,1)S(1)}, u32[]{:S(2)}, u32[]{:S(2)}) collective-permute-start(bf16[24,1024]{1,0:T(8,128)(2,1)S(1)} %constant_dynamic-update-slice_fusion.near_ref), channel_id=1, source_target_pairs={{0,1},{1,0},{2,3},{3,2},{4,5},{5,4},{6,7},{7,6},{8,9},{9,8},{10,11... | collective-permute-start | bytes 147464 | tf_op jit(solution)/shard_map/ppermute | solution.py:29
  51.2 2.8 %collective-permute-start.9 = (f32[288,1024]{1,0:T(8,128)S(1)}, f32[288,1024]{1,0:T(8,128)S(1)}, u32[]{:S(2)}, u32[]{:S(2)}) collective-permute-start(f32[288,1024]{1,0:T(8,128)S(1)} %get-tuple-element.37), channel_id=1, source_target_pairs={{0,1},{1,0},{2,3},{3,2},{4,5},{5,4},{6,7},{7,6},{8,9},{9,8},{10,11... | collective-permute-start | bytes 3538952 | tf_op jit(solution)/shard_map/ppermute | solution.py:29
  51.3 10.4 %collective-permute-start.8 = (bf16[256,1024]{1,0:T(8,128)(2,1)S(1)}, bf16[256,1024]{1,0:T(8,128)(2,1)S(1)}, u32[]{:S(2)}, u32[]{:S(2)}) collective-permute-start(bf16[256,1024]{1,0:T(8,128)(2,1)S(1)} %get-tuple-element.35), channel_id=1, source_target_pairs={{1,0},{3,2},{5,4},{7,6},{9,8},{11,10},{13,12},{15,14},{4,1},{6,3},... | collective-permute-start | bytes 1572872 | tf_op jit(solution)/shard_map/ppermute | solution.py:29
  54.1 15.8 %collective-permute-start.10 = (bf16[264,512]{1,0:T(8,128)(2,1)S(1)}, bf16[264,512]{1,0:T(8,128)(2,1)S(1)}, u32[]{:S(2)}, u32[]{:S(2)}) collective-permute-start(bf16[264,512]{1,0:T(8,128)(2,1)S(1)} %get-tuple-element.39), channel_id=1, source_target_pairs={{2,0},{3,1},{4,2},{5,3},{6,4},{7,5},{8,6},{9,7},{10,8},{11,9},{12,... | collective-permute-start | bytes 811016 | tf_op jit(solution)/shard_map/ppermute | solution.py:29
  58.7 11.2 %collective-permute-start.11 = (f32[8,1024]{1,0:T(8,128)S(1)}, f32[8,1024]{1,0:T(8,128)S(1)}, u32[]{:S(2)}, u32[]{:S(2)}) collective-permute-start(f32[8,1024]{1,0:T(8,128)S(1)} %get-tuple-element.41), channel_id=1, source_target_pairs={{4,0},{11,1},{6,2},{13,3},{8,4},{15,5},{10,6},{1,7},{12,8},{3,9},{... | collective-permute-start | bytes 98312 | tf_op jit(solution)/shard_map/ppermute | solution.py:29
  59.5 10.4 %collective-permute-start.12 = (f32[8,1024]{1,0:T(8,128)S(1)}, f32[8,1024]{1,0:T(8,128)S(1)}, u32[]{:S(2)}, u32[]{:S(2)}) collective-permute-start(f32[8,1024]{1,0:T(8,128)S(1)} %get-tuple-element.42), channel_id=1, source_target_pairs={{6,0},{13,1},{8,2},{15,3},{10,4},{1,5},{12,6},{3,7},{14,8},{5,9},{... | collective-permute-start | bytes 98312 | tf_op jit(solution)/shard_map/ppermute | solution.py:29
  59.5 10.4 %collective-permute-start.13 = (f32[8,1024]{1,0:T(8,128)S(1)}, f32[8,1024]{1,0:T(8,128)S(1)}, u32[]{:S(2)}, u32[]{:S(2)}) collective-permute-start(f32[8,1024]{1,0:T(8,128)S(1)} %get-tuple-element.43), channel_id=1, source_target_pairs={{8,0},{15,1},{10,2},{1,3},{12,4},{3,5},{14,6},{5,7},{0,8},{7,9},{2... | collective-permute-start | bytes 98312 | tf_op jit(solution)/shard_map/ppermute | solution.py:29
  69.9 6.5 %collective-permute-start.14 = (bf16[264,512]{1,0:T(8,128)(2,1)S(1)}, bf16[264,512]{1,0:T(8,128)(2,1)S(1)}, u32[]{:S(2)}, u32[]{:S(2)}) collective-permute-start(bf16[264,512]{1,0:T(8,128)(2,1)S(1)} %get-tuple-element.44), channel_id=1, source_target_pairs={{2,0},{3,1},{4,2},{5,3},{6,4},{7,5},{8,6},{9,7},{10,8},{11,9},{12,... | collective-permute-start | bytes 811016 | tf_op jit(solution)/shard_map/ppermute | solution.py:29
  70.7 1.2 %collective-permute-start.15 = (f32[4,1024]{1,0:T(4,128)S(1)}, f32[4,1024]{1,0:T(4,128)S(1)}, u32[]{:S(2)}, u32[]{:S(2)}) collective-permute-start(f32[4,1024]{1,0:T(4,128)S(1)} %get-tuple-element.47), channel_id=1, source_target_pairs={{0,1},{1,0},{2,3},{3,2},{4,5},{5,4},{6,7},{7,6},{8,9},{9,8},{10,11... | collective-permute-start | bytes 49160 | tf_op jit(solution)/shard_map/ppermute | solution.py:29
